TPU v7x, 32 devices: a whole 2x2x4 slice. The times are simulated.
32 devices in a mesh: ctx: 4 (over y, core), fsdp: 8 (over z, x).
Axes of the slice: x: 2, y: 2, z: 4, core: 2. Of those that a mesh axis runs over, the one named last changes fastest.
Arguments:
- layer_in: bfloat16 [8, 512, 1600], P('fsdp', 'ctx'), may hold values from -6 to 6
- out_grad: bfloat16 [8, 512, 1600], P('fsdp', 'ctx'), may hold values from -6 to 6
- doc_lengths: int32 [8, 8], P('fsdp'), may hold values from 1 to 256, 512 in all within a row
- block_deal: int32 [4, 2], replicated, may hold values from 0 to 7, as said below
- norm_gains: bfloat16 [4, 1600], P(None, 'fsdp'), may hold values from 0.5 to 1.5
- query_weight: bfloat16 [1600, 1600], P('fsdp'), may hold values from -0.15625 to 0.15625
- keyval_weight: bfloat16 [1600, 640], P('fsdp'), may hold values from -0.15625 to 0.15625
- attn_proj: bfloat16 [1600, 1600], P('fsdp'), may hold values from -0.15625 to 0.15625
- mamba_in: bfloat16 [1600, 6400], P('fsdp'), may hold values from -0.15625 to 0.15625
- conv_taps: bfloat16 [4, 3200], P(None, 'fsdp'), may hold values from -3 to 3
- conv_bias: bfloat16 [3200], P('fsdp'), may hold values from -1.5 to 1.5
- step_bias: bfloat16 [3200], P('fsdp'), may hold values from -5 to -2
- skip_gain: bfloat16 [3200], P('fsdp'), may hold values from 0.5 to 1.5
- decay_log: bfloat16 [16, 3200], P(None, 'fsdp'), may hold values from -7 to 1
- select_proj: bfloat16 [3200, 132], P('fsdp'), may hold values from -0.109375 to 0.109375
- step_proj: bfloat16 [100, 3200], P(None, 'fsdp'), may hold values from -0.625 to 0.625
- mamba_proj: bfloat16 [3200, 1600], P('fsdp'), may hold values from -0.109375 to 0.109375
- gate_weight: bfloat16 [1600, 5504], P('fsdp'), may hold values from -0.15625 to 0.15625
- up_weight: bfloat16 [1600, 5504], P('fsdp'), may hold values from -0.15625 to 0.15625
- down_weight: bfloat16 [5504, 1600], P('fsdp'), may hold values from -0.078125 to 0.078125
Outputs:
- result: bfloat16 [8, 512, 1600], P('fsdp', 'ctx')
- stream_grad: float32 [8, 512, 1600], P('fsdp', 'ctx')
- gains_grad: float32 [4, 1600], P(None, 'fsdp')
- query_grad: float32 [1600, 1600], P('fsdp')
- keyval_grad: float32 [1600, 640], P('fsdp')
- attn_proj_grad: float32 [1600, 1600], P('fsdp')
- mamba_in_grad: float32 [1600, 6400], P('fsdp')
- conv_taps_grad: float32 [4, 3200], P(None, 'fsdp')
- conv_bias_grad: float32 [3200], P('fsdp')
- step_bias_grad: float32 [3200], P('fsdp')
- skip_gain_grad: float32 [3200], P('fsdp')
- decay_log_grad: float32 [16, 3200], P(None, 'fsdp')
- select_proj_grad: float32 [3200, 132], P('fsdp')
- step_proj_grad: float32 [100, 3200], P(None, 'fsdp')
- mamba_proj_grad: float32 [3200, 1600], P('fsdp')
- gate_grad: float32 [1600, 5504], P('fsdp')
- up_grad: float32 [1600, 5504], P('fsdp')
- down_grad: float32 [5504, 1600], P('fsdp')
Inputs may be any that keep to these rules, and one draw needn't show every extreme that they name: `block_deal`: row c names a block b and its mirror 8 - 1 - b; every block of 0 to 7 stands in exactly one row. `doc_lengths`: each stream's 8 lengths sum to 512, and the longest has exactly 256 tokens.
All inputs are finite; a program needn't handle non-finite values.
Results may differ from a plain program's by a relative error of at most 0.022.
Values may be sent and summed in bfloat16 or wider, within the bound.
A program may use at most 384 MiB of HBM per device.

v0:
```python
import math

import jax
import jax.numpy as jnp
from jax import lax
from jax.sharding import PartitionSpec as P

H = 25
KV = 5
HD = 64
INNER = 3200
NS = 16
RANK = 100
CONV = 4


EPS = 1e-06
score_scale = 0.125


def norm_forward(values, gain):
    inverse = lax.rsqrt(jnp.mean(values * values, axis=-1, keepdims=True) + EPS)
    return (values * inverse * gain, inverse)


def norm_backward(grad, values, inverse, gain):
    normed = values * inverse
    gain_grad = jnp.sum(grad * normed, axis=0)
    scaled = grad * gain
    return (
        inverse * (scaled - normed * jnp.mean(scaled * normed, axis=-1, keepdims=True)),
        gain_grad,
    )


def silu_slope(values):
    sigma = jax.nn.sigmoid(values)
    return sigma * (1.0 + values * (1.0 - sigma))


def block_scan(start, rate, steps, inputs, writes, reads):
    batch_count, length, channels = steps.shape
    piece_len = math.gcd(length, 8)
    pieces = length // piece_len

    def split(values):
        return values.reshape(batch_count, pieces, piece_len, values.shape[-1]).transpose(
            1, 0, 2, 3
        )

    def one_piece(carried, columns):
        step_c, input_c, write_c, read_c = columns
        climbing = jnp.cumsum(step_c[:, :, None, :] * rate, axis=1)
        pushed = write_c[:, :, :, None] * (step_c * input_c)[:, :, None, :]
        inner = jnp.exp(climbing) * (
            carried[:, None] + jnp.cumsum(jnp.exp(-climbing) * pushed, axis=1)
        )
        return (inner[:, -1], jnp.sum(inner * read_c[:, :, :, None], axis=2))

    final, outputs = lax.scan(
        jax.checkpoint(one_piece), start, (split(steps), split(inputs), split(writes), split(reads))
    )
    return (outputs.transpose(1, 0, 2, 3).reshape(batch_count, length, channels), final)


def on_device(
    layer_in,
    out_grad,
    doc_lengths,
    block_deal,
    norm_gains,
    query_weight,
    keyval_weight,
    attn_proj,
    mamba_in,
    conv_taps,
    conv_bias,
    step_bias,
    skip_gain,
    decay_log,
    select_proj,
    step_proj,
    mamba_proj,
    gate_weight,
    up_weight,
    down_weight,
):
    f32 = jnp.float32
    bf16 = jnp.bfloat16
    row_count = layer_in.shape[1]
    half_rows = row_count // 2
    blocks_all = 2 * lax.axis_size("ctx")
    group = H // KV
    ctx_place = lax.axis_index("ctx")
    deal_flat = block_deal.reshape(-1)
    my_blocks = lax.dynamic_slice_in_dim(block_deal, ctx_place, 1, 0)[0]
    offsets = jnp.arange(half_rows, dtype=jnp.int32)
    my_places = (my_blocks[:, None] * half_rows + offsets[None, :]).reshape(-1)
    key_places = (deal_flat[:, None] * half_rows + offsets[None, :]).reshape(-1)
    lengths = doc_lengths[0]
    starts = jnp.cumsum(lengths) - lengths

    def segment(places):
        return jnp.sum((places[:, None] >= starts[None, :]).astype(jnp.int32), axis=1)

    allowed = (key_places[None, :] <= my_places[:, None]) & (
        segment(key_places)[None, :] == segment(my_places)[:, None]
    )
    inverse = jnp.argsort(deal_flat)
    (
        gain_rows,
        query_mat,
        keyval_mat,
        attn_mat,
        entry_mat,
        taps_mat,
        conv_shift,
        step_shift,
        skip_rows,
        decay_mat,
        select_mat,
        step_mat,
        mamba_mat,
    ) = (
        lax.all_gather(norm_gains, "fsdp", axis=1, tiled=True),
        lax.all_gather(query_weight, "fsdp", axis=0, tiled=True),
        lax.all_gather(keyval_weight, "fsdp", axis=0, tiled=True),
        lax.all_gather(attn_proj, "fsdp", axis=0, tiled=True),
        lax.all_gather(mamba_in, "fsdp", axis=0, tiled=True),
        lax.all_gather(conv_taps, "fsdp", axis=1, tiled=True),
        lax.all_gather(conv_bias, "fsdp", axis=0, tiled=True),
        lax.all_gather(step_bias, "fsdp", axis=0, tiled=True),
        lax.all_gather(skip_gain, "fsdp", axis=0, tiled=True),
        lax.all_gather(decay_log, "fsdp", axis=1, tiled=True),
        lax.all_gather(select_proj, "fsdp", axis=0, tiled=True),
        lax.all_gather(step_proj, "fsdp", axis=1, tiled=True),
        lax.all_gather(mamba_proj, "fsdp", axis=0, tiled=True),
    )
    gain_float = gain_rows.astype(f32)
    stream = layer_in[0].astype(f32)
    normed_in, inv_in = norm_forward(stream, gain_float[0])
    normed_low = normed_in.astype(bf16)
    queries = jnp.dot(normed_low, query_mat, preferred_element_type=f32).astype(bf16)
    keyvals = jnp.dot(normed_low, keyval_mat, preferred_element_type=f32).astype(bf16)
    keyvals_all = lax.all_gather(keyvals, "ctx", axis=0, tiled=True)
    query_groups = queries.reshape(row_count, KV, group, HD).transpose(1, 0, 2, 3)
    key_groups = keyvals_all[:, : KV * HD].reshape(-1, KV, HD).transpose(1, 0, 2)
    value_groups = keyvals_all[:, KV * HD :].reshape(-1, KV, HD).transpose(1, 0, 2)

    def attend(parts):
        query_part, key_part, value_part = parts
        scores = (
            jnp.einsum("lgd,sd->gls", query_part, key_part, preferred_element_type=f32)
            * score_scale
        )
        scores = jnp.where(allowed[None], scores, -1e30)
        largest = jnp.max(scores, axis=-1, keepdims=True)
        expo = jnp.exp(scores - largest)
        total = jnp.sum(expo, axis=-1, keepdims=True)
        probs = (expo / total).astype(bf16)
        output = jnp.einsum("gls,sd->lgd", probs, value_part, preferred_element_type=f32)
        return (output, largest + jnp.log(total))

    attn_groups, log_totals = lax.map(attend, (query_groups, key_groups, value_groups))
    attn_rows = attn_groups.transpose(1, 0, 2, 3).reshape(row_count, H * HD).astype(bf16)
    attn_out = jnp.dot(attn_rows, attn_mat, preferred_element_type=f32)
    attn_normed, inv_attn = norm_forward(attn_out, gain_float[1])
    entry = jnp.dot(normed_low, entry_mat, preferred_element_type=f32)
    mixer_in = entry[:, :INNER].astype(bf16)
    gate_side = entry[:, INNER:]
    mixer_blocks = mixer_in.reshape(2, half_rows, INNER)
    tails = mixer_blocks[:, half_rows - (CONV - 1) :]
    tails_all = lax.all_gather(tails, "ctx", axis=0, tiled=True)
    before_index = inverse[jnp.maximum(my_blocks - 1, 0)]
    has_before = my_blocks > 0
    prior_tail = jnp.where(
        has_before[:, None, None], jnp.take(tails_all, before_index, axis=0), jnp.zeros_like(tails)
    )
    padded = jnp.concatenate([prior_tail, mixer_blocks], axis=1).astype(f32)
    taps_float = taps_mat.astype(f32)
    conv_blocks_out = conv_shift.astype(f32) + sum(
        (taps_float[offset] * padded[:, offset : offset + half_rows] for offset in range(CONV))
    )
    conv_out = conv_blocks_out.reshape(row_count, INNER)
    signal = jax.nn.silu(conv_out).astype(bf16)
    signal_float = signal.astype(f32)
    selected = jnp.dot(signal, select_mat, preferred_element_type=f32)
    step_low = selected[:, :RANK].astype(bf16)
    writes = selected[:, RANK : RANK + NS]
    reads = selected[:, RANK + NS :]
    step_pre = jnp.dot(step_low, step_mat, preferred_element_type=f32) + step_shift.astype(f32)
    step_sizes = jax.nn.softplus(step_pre)
    rate = -jnp.exp(decay_mat.astype(f32))
    block_steps = step_sizes.reshape(2, half_rows, INNER)
    block_inputs = signal_float.reshape(2, half_rows, INNER)
    block_writes = writes.reshape(2, half_rows, NS)
    block_reads = reads.reshape(2, half_rows, NS)
    zero_state = jnp.zeros((2, NS, INNER), f32)
    _, local_end = block_scan(
        zero_state, rate, block_steps, block_inputs, block_writes, block_reads
    )
    step_totals = jnp.sum(block_steps, axis=1)
    ends_all, totals_all = (
        lax.all_gather(local_end.astype(jnp.bfloat16), "ctx", axis=0, tiled=True).astype(
            local_end.dtype
        ),
        lax.all_gather(step_totals.astype(jnp.bfloat16), "ctx", axis=0, tiled=True).astype(
            step_totals.dtype
        ),
    )
    decays_true = jnp.exp(rate[None] * jnp.take(totals_all, inverse, axis=0)[:, None, :])
    ends_true = jnp.take(ends_all, inverse, axis=0)

    def link(carried, pair):
        decay_part, end_part = pair
        return (decay_part * carried + end_part, carried)

    _, starts_true = lax.scan(link, zero_state[0], (decays_true, ends_true))
    start_state = jnp.take(starts_true, my_blocks, axis=0)
    (scan_blocks, _), scan_pull = jax.vjp(
        block_scan, start_state, rate, block_steps, block_inputs, block_writes, block_reads
    )
    skip_float = skip_rows.astype(f32)
    scanned = scan_blocks.reshape(row_count, INNER) + skip_float * signal_float
    gate_act = jax.nn.silu(gate_side)
    mamba_rows = (scanned * gate_act).astype(bf16)
    mamba_out = jnp.dot(mamba_rows, mamba_mat, preferred_element_type=f32)
    mamba_normed, inv_mamba = norm_forward(mamba_out, gain_float[2])
    middle = stream + 0.5 * (attn_normed + mamba_normed)
    gate_mat, up_mat, down_mat = (
        lax.all_gather(gate_weight, "fsdp", axis=0, tiled=True),
        lax.all_gather(up_weight, "fsdp", axis=0, tiled=True),
        lax.all_gather(down_weight, "fsdp", axis=0, tiled=True),
    )
    ffn_normed, inv_ffn = norm_forward(middle, gain_float[3])
    ffn_low = ffn_normed.astype(bf16)
    gate_pre = jnp.dot(ffn_low, gate_mat, preferred_element_type=f32)
    up_pre = jnp.dot(ffn_low, up_mat, preferred_element_type=f32)
    hidden = (jax.nn.silu(gate_pre) * up_pre).astype(bf16)
    result = middle + jnp.dot(hidden, down_mat, preferred_element_type=f32)
    grad_rows = out_grad[0]
    down_wgrad = jnp.einsum("lf,ld->fd", hidden, grad_rows, preferred_element_type=f32)
    hidden_back = jnp.einsum("ld,fd->lf", grad_rows, down_mat, preferred_element_type=f32)
    gate_back = (hidden_back * up_pre * silu_slope(gate_pre)).astype(bf16)
    up_back = (hidden_back * jax.nn.silu(gate_pre)).astype(bf16)
    gate_wgrad = jnp.einsum("ld,lf->df", ffn_low, gate_back, preferred_element_type=f32)
    up_wgrad = jnp.einsum("ld,lf->df", ffn_low, up_back, preferred_element_type=f32)
    ffn_back = jnp.einsum(
        "lf,df->ld", gate_back, gate_mat, preferred_element_type=f32
    ) + jnp.einsum("lf,df->ld", up_back, up_mat, preferred_element_type=f32)
    middle_part, ffn_gain_grad = norm_backward(ffn_back, middle, inv_ffn, gain_float[3])
    middle_back = grad_rows.astype(f32) + middle_part
    gate_share, up_share, down_share = (
        lax.psum_scatter(
            gate_wgrad.astype(jnp.bfloat16), "fsdp", scatter_dimension=0, tiled=True
        ).astype(jnp.float32),
        lax.psum_scatter(
            up_wgrad.astype(jnp.bfloat16), "fsdp", scatter_dimension=0, tiled=True
        ).astype(jnp.float32),
        lax.psum_scatter(
            down_wgrad.astype(jnp.bfloat16), "fsdp", scatter_dimension=0, tiled=True
        ).astype(jnp.float32),
    )
    branch_back = 0.5 * middle_back
    attn_part, attn_gain_grad = norm_backward(branch_back, attn_out, inv_attn, gain_float[1])
    mamba_part, mamba_gain_grad = norm_backward(branch_back, mamba_out, inv_mamba, gain_float[2])
    attn_back = attn_part.astype(bf16)
    mamba_back = mamba_part.astype(bf16)
    attn_wgrad = jnp.einsum("lh,ld->hd", attn_rows, attn_back, preferred_element_type=f32)
    rows_back = jnp.einsum("ld,hd->lh", attn_back, attn_mat, preferred_element_type=f32).astype(
        bf16
    )
    mamba_wgrad = jnp.einsum("li,ld->id", mamba_rows, mamba_back, preferred_element_type=f32)
    mrows_back = jnp.einsum("ld,id->li", mamba_back, mamba_mat, preferred_element_type=f32)
    scan_back = mrows_back * gate_act
    side_back = mrows_back * scanned * silu_slope(gate_side)
    skip_grad = jnp.sum(scan_back * signal_float, axis=0)
    block_dout = scan_back.reshape(2, half_rows, INNER)
    local_back = scan_pull((block_dout, zero_state))[0]
    backs_all = lax.all_gather(local_back.astype(jnp.bfloat16), "ctx", axis=0, tiled=True).astype(
        local_back.dtype
    )
    backs_true = jnp.take(backs_all, inverse, axis=0)

    def link_back(grad_next, pair):
        decay_part, back_part = pair
        return (back_part + decay_part * grad_next, grad_next)

    _, ends_back_true = lax.scan(link_back, zero_state[0], (decays_true, backs_true), reverse=True)
    end_back = jnp.take(ends_back_true, my_blocks, axis=0)
    _, rate_back, steps_back, inputs_back, writes_back, reads_back = scan_pull(
        (block_dout, end_back)
    )
    decay_grad = rate_back * rate
    step_back = steps_back.reshape(row_count, INNER)
    signal_back = scan_back * skip_float + inputs_back.reshape(row_count, INNER)
    write_back = writes_back.reshape(row_count, NS)
    read_back = reads_back.reshape(row_count, NS)
    pre_back = (step_back * jax.nn.sigmoid(step_pre)).astype(bf16)
    step_wgrad = jnp.einsum("lr,li->ri", step_low, pre_back, preferred_element_type=f32)
    bias_grad = jnp.sum(pre_back.astype(f32), axis=0)
    rank_back = jnp.einsum("li,ri->lr", pre_back, step_mat, preferred_element_type=f32)
    select_back = jnp.concatenate([rank_back, write_back, read_back], axis=1).astype(bf16)
    select_wgrad = jnp.einsum("li,lk->ik", signal, select_back, preferred_element_type=f32)
    signal_back = signal_back + jnp.einsum(
        "lk,ik->li", select_back, select_mat, preferred_element_type=f32
    )
    conv_back = signal_back * silu_slope(conv_out)
    conv_blocks = conv_back.reshape(2, half_rows, INNER)
    taps_grad = jnp.stack(
        [
            jnp.sum(conv_blocks * padded[:, offset : offset + half_rows], axis=(0, 1))
            for offset in range(CONV)
        ]
    )
    shift_grad = jnp.sum(conv_back, axis=0)
    padded_back = sum(
        (
            jnp.pad(taps_float[offset] * conv_blocks, ((0, 0), (offset, CONV - 1 - offset), (0, 0)))
            for offset in range(CONV)
        )
    )
    tail_back = jnp.where(has_before[:, None, None], padded_back[:, : CONV - 1], 0.0)
    tails_back_all = lax.all_gather(
        tail_back.astype(jnp.bfloat16), "ctx", axis=0, tiled=True
    ).astype(tail_back.dtype)
    after_index = inverse[jnp.minimum(my_blocks + 1, blocks_all - 1)]
    has_after = my_blocks < blocks_all - 1
    incoming = jnp.where(
        has_after[:, None, None], jnp.take(tails_back_all, after_index, axis=0), 0.0
    )
    mixer_back = padded_back[:, CONV - 1 :] + jnp.pad(
        incoming, ((0, 0), (half_rows - (CONV - 1), 0), (0, 0))
    )
    entry_back = jnp.concatenate([mixer_back.reshape(row_count, INNER), side_back], axis=1).astype(
        bf16
    )
    entry_wgrad = jnp.einsum("ld,lk->dk", normed_low, entry_back, preferred_element_type=f32)
    input_back = jnp.einsum("lk,dk->ld", entry_back, entry_mat, preferred_element_type=f32)
    dout_groups = rows_back.reshape(row_count, KV, group, HD).transpose(1, 0, 2, 3)

    def attend_back(parts):
        query_part, key_part, value_part, dout_part, log_part = parts
        scores = (
            jnp.einsum("lgd,sd->gls", query_part, key_part, preferred_element_type=f32)
            * score_scale
        )
        scores = jnp.where(allowed[None], scores, -1e30)
        probs = jnp.exp(scores - log_part)
        value_grad = jnp.einsum(
            "gls,lgd->sd", probs.astype(bf16), dout_part, preferred_element_type=f32
        )
        prob_grad = jnp.einsum("lgd,sd->gls", dout_part, value_part, preferred_element_type=f32)
        centre = jnp.sum(probs * prob_grad, axis=-1, keepdims=True)
        score_grad = (probs * (prob_grad - centre)).astype(bf16)
        query_grad = (
            jnp.einsum("gls,sd->lgd", score_grad, key_part, preferred_element_type=f32)
            * score_scale
        )
        key_grad = (
            jnp.einsum("gls,lgd->sd", score_grad, query_part, preferred_element_type=f32)
            * score_scale
        )
        return (query_grad, key_grad, value_grad)

    query_grads, key_grads, value_grads = lax.map(
        attend_back, (query_groups, key_groups, value_groups, dout_groups, log_totals)
    )
    keyval_terms = jnp.concatenate(
        [
            key_grads.transpose(1, 0, 2).reshape(-1, KV * HD),
            value_grads.transpose(1, 0, 2).reshape(-1, KV * HD),
        ],
        axis=1,
    )
    keyval_back = (
        lax.psum_scatter(keyval_terms.astype(jnp.bfloat16), "ctx", scatter_dimension=0, tiled=True)
        .astype(jnp.float32)
        .astype(bf16)
    )
    query_back = query_grads.transpose(1, 0, 2, 3).reshape(row_count, H * HD).astype(bf16)
    query_wgrad = jnp.einsum("ld,lk->dk", normed_low, query_back, preferred_element_type=f32)
    keyval_wgrad = jnp.einsum("ld,lk->dk", normed_low, keyval_back, preferred_element_type=f32)
    input_back = input_back + jnp.einsum(
        "lk,dk->ld", query_back, query_mat, preferred_element_type=f32
    )
    input_back = input_back + jnp.einsum(
        "lk,dk->ld", keyval_back, keyval_mat, preferred_element_type=f32
    )
    stream_part, in_gain_grad = norm_backward(input_back, stream, inv_in, gain_float[0])
    stream_back = middle_back + stream_part
    gain_grad = jnp.stack([in_gain_grad, attn_gain_grad, mamba_gain_grad, ffn_gain_grad])
    (
        gain_share,
        query_share,
        keyval_share,
        attn_share,
        entry_share,
        taps_share,
        shift_share,
        bias_share,
        skip_share,
        decay_share,
        select_share,
        step_share,
        mamba_share,
    ) = (
        lax.psum_scatter(
            gain_grad.astype(jnp.bfloat16), "fsdp", scatter_dimension=1, tiled=True
        ).astype(jnp.float32),
        lax.psum_scatter(
            query_wgrad.astype(jnp.bfloat16), "fsdp", scatter_dimension=0, tiled=True
        ).astype(jnp.float32),
        lax.psum_scatter(
            keyval_wgrad.astype(jnp.bfloat16), "fsdp", scatter_dimension=0, tiled=True
        ).astype(jnp.float32),
        lax.psum_scatter(
            attn_wgrad.astype(jnp.bfloat16), "fsdp", scatter_dimension=0, tiled=True
        ).astype(jnp.float32),
        lax.psum_scatter(
            entry_wgrad.astype(jnp.bfloat16), "fsdp", scatter_dimension=0, tiled=True
        ).astype(jnp.float32),
        lax.psum_scatter(
            taps_grad.astype(jnp.bfloat16), "fsdp", scatter_dimension=1, tiled=True
        ).astype(jnp.float32),
        lax.psum_scatter(
            shift_grad.astype(jnp.bfloat16), "fsdp", scatter_dimension=0, tiled=True
        ).astype(jnp.float32),
        lax.psum_scatter(
            bias_grad.astype(jnp.bfloat16), "fsdp", scatter_dimension=0, tiled=True
        ).astype(jnp.float32),
        lax.psum_scatter(
            skip_grad.astype(jnp.bfloat16), "fsdp", scatter_dimension=0, tiled=True
        ).astype(jnp.float32),
        lax.psum_scatter(
            decay_grad.astype(jnp.bfloat16), "fsdp", scatter_dimension=1, tiled=True
        ).astype(jnp.float32),
        lax.psum_scatter(
            select_wgrad.astype(jnp.bfloat16), "fsdp", scatter_dimension=0, tiled=True
        ).astype(jnp.float32),
        lax.psum_scatter(
            step_wgrad.astype(jnp.bfloat16), "fsdp", scatter_dimension=1, tiled=True
        ).astype(jnp.float32),
        lax.psum_scatter(
            mamba_wgrad.astype(jnp.bfloat16), "fsdp", scatter_dimension=0, tiled=True
        ).astype(jnp.float32),
    )
    pieces = (
        lax.psum_scatter(
            gain_share.reshape(-1).astype(jnp.bfloat16), "ctx", scatter_dimension=0, tiled=True
        ).astype(jnp.float32),
        lax.psum_scatter(
            query_share.reshape(-1).astype(jnp.bfloat16), "ctx", scatter_dimension=0, tiled=True
        ).astype(jnp.float32),
        lax.psum_scatter(
            keyval_share.reshape(-1).astype(jnp.bfloat16), "ctx", scatter_dimension=0, tiled=True
        ).astype(jnp.float32),
        lax.psum_scatter(
            attn_share.reshape(-1).astype(jnp.bfloat16), "ctx", scatter_dimension=0, tiled=True
        ).astype(jnp.float32),
        lax.psum_scatter(
            entry_share.reshape(-1).astype(jnp.bfloat16), "ctx", scatter_dimension=0, tiled=True
        ).astype(jnp.float32),
        lax.psum_scatter(
            taps_share.reshape(-1).astype(jnp.bfloat16), "ctx", scatter_dimension=0, tiled=True
        ).astype(jnp.float32),
        lax.psum_scatter(
            shift_share.astype(jnp.bfloat16), "ctx", scatter_dimension=0, tiled=True
        ).astype(jnp.float32),
        lax.psum_scatter(
            bias_share.astype(jnp.bfloat16), "ctx", scatter_dimension=0, tiled=True
        ).astype(jnp.float32),
        lax.psum_scatter(
            skip_share.astype(jnp.bfloat16), "ctx", scatter_dimension=0, tiled=True
        ).astype(jnp.float32),
        lax.psum_scatter(
            decay_share.reshape(-1).astype(jnp.bfloat16), "ctx", scatter_dimension=0, tiled=True
        ).astype(jnp.float32),
        lax.psum_scatter(
            select_share.reshape(-1).astype(jnp.bfloat16), "ctx", scatter_dimension=0, tiled=True
        ).astype(jnp.float32),
        lax.psum_scatter(
            step_share.reshape(-1).astype(jnp.bfloat16), "ctx", scatter_dimension=0, tiled=True
        ).astype(jnp.float32),
        lax.psum_scatter(
            mamba_share.reshape(-1).astype(jnp.bfloat16), "ctx", scatter_dimension=0, tiled=True
        ).astype(jnp.float32),
        lax.psum_scatter(
            gate_share.reshape(-1).astype(jnp.bfloat16), "ctx", scatter_dimension=0, tiled=True
        ).astype(jnp.float32),
        lax.psum_scatter(
            up_share.reshape(-1).astype(jnp.bfloat16), "ctx", scatter_dimension=0, tiled=True
        ).astype(jnp.float32),
        lax.psum_scatter(
            down_share.reshape(-1).astype(jnp.bfloat16), "ctx", scatter_dimension=0, tiled=True
        ).astype(jnp.float32),
    )
    gathered = (
        lax.all_gather(pieces[0].astype(jnp.bfloat16), "ctx", axis=0, tiled=True).astype(
            jnp.float32
        ),
        lax.all_gather(pieces[1].astype(jnp.bfloat16), "ctx", axis=0, tiled=True).astype(
            jnp.float32
        ),
        lax.all_gather(pieces[2].astype(jnp.bfloat16), "ctx", axis=0, tiled=True).astype(
            jnp.float32
        ),
        lax.all_gather(pieces[3].astype(jnp.bfloat16), "ctx", axis=0, tiled=True).astype(
            jnp.float32
        ),
        lax.all_gather(pieces[4].astype(jnp.bfloat16), "ctx", axis=0, tiled=True).astype(
            jnp.float32
        ),
        lax.all_gather(pieces[5].astype(jnp.bfloat16), "ctx", axis=0, tiled=True).astype(
            jnp.float32
        ),
        lax.all_gather(pieces[6].astype(jnp.bfloat16), "ctx", axis=0, tiled=True).astype(
            jnp.float32
        ),
        lax.all_gather(pieces[7].astype(jnp.bfloat16), "ctx", axis=0, tiled=True).astype(
            jnp.float32
        ),
        lax.all_gather(pieces[8].astype(jnp.bfloat16), "ctx", axis=0, tiled=True).astype(
            jnp.float32
        ),
        lax.all_gather(pieces[9].astype(jnp.bfloat16), "ctx", axis=0, tiled=True).astype(
            jnp.float32
        ),
        lax.all_gather(pieces[10].astype(jnp.bfloat16), "ctx", axis=0, tiled=True).astype(
            jnp.float32
        ),
        lax.all_gather(pieces[11].astype(jnp.bfloat16), "ctx", axis=0, tiled=True).astype(
            jnp.float32
        ),
        lax.all_gather(pieces[12].astype(jnp.bfloat16), "ctx", axis=0, tiled=True).astype(
            jnp.float32
        ),
        lax.all_gather(pieces[13].astype(jnp.bfloat16), "ctx", axis=0, tiled=True).astype(
            jnp.float32
        ),
        lax.all_gather(pieces[14].astype(jnp.bfloat16), "ctx", axis=0, tiled=True).astype(
            jnp.float32
        ),
        lax.all_gather(pieces[15].astype(jnp.bfloat16), "ctx", axis=0, tiled=True).astype(
            jnp.float32
        ),
    )
    shapes = (
        norm_gains.shape,
        query_weight.shape,
        keyval_weight.shape,
        attn_proj.shape,
        mamba_in.shape,
        conv_taps.shape,
        conv_bias.shape,
        step_bias.shape,
        skip_gain.shape,
        decay_log.shape,
        select_proj.shape,
        step_proj.shape,
        mamba_proj.shape,
        gate_weight.shape,
        up_weight.shape,
        down_weight.shape,
    )
    summed = tuple((piece.reshape(shape) for piece, shape in zip(gathered, shapes)))
    return (
        result.astype(bf16)[None],
        stream_back[None],
        summed[0],
        summed[1],
        summed[2],
        summed[3],
        summed[4],
        summed[5],
        summed[6],
        summed[7],
        summed[8],
        summed[9],
        summed[10],
        summed[11],
        summed[12],
        summed[13],
        summed[14],
        summed[15],
    )


def solution(mesh):
    in_specs = (
        P("fsdp", "ctx", None),
        P("fsdp", "ctx", None),
        P("fsdp", None),
        P(),
        P(None, "fsdp"),
        P("fsdp", None),
        P("fsdp", None),
        P("fsdp", None),
        P("fsdp", None),
        P(None, "fsdp"),
        P("fsdp"),
        P("fsdp"),
        P("fsdp"),
        P(None, "fsdp"),
        P("fsdp", None),
        P(None, "fsdp"),
        P("fsdp", None),
        P("fsdp", None),
        P("fsdp", None),
        P("fsdp", None),
    )
    out_specs = (
        P("fsdp", "ctx", None),
        P("fsdp", "ctx", None),
        P(None, "fsdp"),
        P("fsdp", None),
        P("fsdp", None),
        P("fsdp", None),
        P("fsdp", None),
        P(None, "fsdp"),
        P("fsdp"),
        P("fsdp"),
        P("fsdp"),
        P(None, "fsdp"),
        P("fsdp", None),
        P(None, "fsdp"),
        P("fsdp", None),
        P("fsdp", None),
        P("fsdp", None),
        P("fsdp", None),
    )
    return jax.shard_map(
        on_device, mesh=mesh, in_specs=in_specs, out_specs=out_specs, check_vma=False
    )
```

profile of v0, /device:TPU:0, one launch (start us, length us, event | category | flops | bytes accessed | tf_op | source)
XLA Modules:
  0.0 4939.1 jit_solution(15685132545454915052)
XLA Ops:
  48.8 36.3 all-reduce.45
  117.2 36.5 all-gather.3
  156.4 35.6 all_gather.125
  272.9 387.5 %all-gather.33.cloned.1.call-done = bf16[1600,6400]{1,0:T(8,128)(2,1)} async-done(((bf16[200,6400]{1,0:T(8,128)(2,1)}), bf16[1600,6400]{1,0:T(8,128)(2,1)}) %all-gather.33.cloned.1.call-update) | async-done | bytes 20480016 | tf_op jit(solution)/shard_map/all_gather | solution.py:129
  766.6 53.5 %while.122 = (s32[]{:T(128)}, f32[2,16,3200]{2,1,0:T(8,128)S(1)}, f32[8,2,8,3200]{3,1,2,0:T(2,128)}, f32[8,2,16,3200]{3,2,1,0:T(8,128)}, f32[8,2,8,3200]{3,2,1,0...) while((s32[]{:T(128)}, f32[2,16,3200]{2,1,0:T(8,128)S(1)}, ...), condition=%wide.region_21.24_spmd, body=%wide.region_17.23_spmd.sunk | while | flops 18022400 | bytes 14961781 | solution.py:60
  835.3 318.3 %all-gather.37.cloned.1.call-done = bf16[1600,5504]{1,0:T(8,128)(2,1)} async-done(((bf16[200,5504]{1,0:T(8,128)(2,1)}), bf16[1600,5504]{1,0:T(8,128)(2,1)}) %all-gather.37.cloned.1.call-update) | async-done | bytes 17612816 | tf_op jit(solution)/shard_map/all_gather | solution.py:231
  1164.2 329.8 %all-gather.39.cloned.1.call-done = bf16[1600,5504]{1,0:T(8,128)(2,1)} async-done(((bf16[200,5504]{1,0:T(8,128)(2,1)}), bf16[1600,5504]{1,0:T(8,128)(2,1)}) %all-gather.39.cloned.1.call-update) | async-done | bytes 17612816 | tf_op jit(solution)/shard_map/all_gather | solution.py:232
  1504.6 343.0 %all-gather.41.cloned.1.call-done = bf16[5504,1600]{1,0:T(8,128)(2,1)} async-done(((bf16[688,1600]{1,0:T(8,128)(2,1)}), bf16[5504,1600]{1,0:T(8,128)(2,1)}) %all-gather.41.cloned.1.call-update) | async-done | bytes 17612816 | tf_op jit(solution)/shard_map/all_gather | solution.py:233
  1942.3 111.3 %while.128 = (s32[]{:T(128)}, f32[16,3200]{1,0:T(8,128)S(1)}, f32[2,16,3200]{2,1,0:T(8,128)S(1)}, f32[8,2,8,3200]{3,1,2,0:T(2,128)}, f32[8,2,8,3200]{3,1,2,0:T(2...) while((s32[]{:T(128)}, f32[16,3200]{1,0:T(8,128)S(1)}, ...), condition=%wide.region_43.46_spmd.clone, body=%wide.region_32.45_spmd.clone.sunk | while | flops 51660288 | bytes 39760080 | solution.py:60
  2065.3 32.4 while.125
  2116.9 66.8 %reduce-scatter.49.cloned.1.call-done = bf16[400,132]{1,0:T(8,128)(2,1)} async-done(((bf16[3200,132]{1,0:T(8,128)(2,1)}), bf16[400,132]{1,0:T(8,128)(2,1)}) %reduce-scatter.49.cloned.1.call-update) | async-done | bytes 105616 | tf_op jit(solution)/shard_map/reduce_scatter | solution.py:438
  2322.2 125.2 %reduce-scatter.51.cloned.1.call-done = bf16[200,1600]{1,0:T(8,128)(2,1)} async-done(((bf16[1600,1600]{1,0:T(8,128)(2,1)}), bf16[200,1600]{1,0:T(8,128)(2,1)}) %reduce-scatter.51.cloned.1.call-update) | async-done | bytes 640016
  2450.1 123.5 %reduce-scatter.55.cloned.1.call-done = bf16[200,1600]{1,0:T(8,128)(2,1)} async-done(((bf16[1600,1600]{1,0:T(8,128)(2,1)}), bf16[200,1600]{1,0:T(8,128)(2,1)}) %reduce-scatter.55.cloned.1.call-update) | async-done | bytes 640016
  2576.4 181.4 %reduce-scatter.39.cloned.1.call-done = bf16[400,1600]{1,0:T(8,128)(2,1)} async-done(((bf16[3200,1600]{1,0:T(8,128)(2,1)}), bf16[400,1600]{1,0:T(8,128)(2,1)}) %reduce-scatter.39.cloned.1.call-update) | async-done | bytes 1280016 | tf_op jit(solution)/shard_map/reduce_scatter | solution.py:444
  2761.6 369.0 %reduce-scatter.59.cloned.1.call-done = bf16[200,5504]{1,0:T(8,128)(2,1)} async-done(((bf16[1600,5504]{1,0:T(8,128)(2,1)}), bf16[200,5504]{1,0:T(8,128)(2,1)}) %reduce-scatter.59.cloned.1.call-update) | async-done | bytes 2201616
  3136.0 365.9 %reduce-scatter.61.cloned.1.call-done = bf16[200,5504]{1,0:T(8,128)(2,1)} async-done(((bf16[1600,5504]{1,0:T(8,128)(2,1)}), bf16[200,5504]{1,0:T(8,128)(2,1)}) %reduce-scatter.61.cloned.1.call-update) | async-done | bytes 2201616
  3507.3 355.2 %reduce-scatter.41.cloned.1.call-done = bf16[688,1600]{1,0:T(8,128)(2,1)} async-done(((bf16[5504,1600]{1,0:T(8,128)(2,1)}), bf16[688,1600]{1,0:T(8,128)(2,1)}) %reduce-scatter.41.cloned.1.call-update) | async-done | bytes 2201616 | tf_op jit(solution)/shard_map/reduce_scatter | solution.py:260
  3868.0 386.6 %reduce-scatter.57.cloned.1.call-done = bf16[200,6400]{1,0:T(8,128)(2,1)} async-done(((bf16[1600,6400]{1,0:T(8,128)(2,1)}), bf16[200,6400]{1,0:T(8,128)(2,1)}) %reduce-scatter.57.cloned.1.call-update) | async-done | bytes 2560016
  4267.6 210.9 %all-reduce.53.cloned.1.call-done = (bf16[52800]{0:T(1024)(128)(2,1)}, bf16[40000]{0:T(1024)(128)(2,1)}, bf16[320000]{0:T(1024)(128)(2,1)}, bf16[128000]{0:T(102...) async-done(((bf16[52800]{0:T(1024)(128)(2,1)}, ...) | async-done | bytes 12166416
  4548.3 51.4 %reduce-scatter.47.cloned.1.call-done = bf16[400,16]{1,0:T(8,128)(2,1)} async-done(((bf16[3200,16]{1,0:T(8,128)(2,1)}), bf16[400,16]{1,0:T(8,128)(2,1)}) %reduce-scatter.47.cloned.1.call-update) | async-done | bytes 12816
  4614.4 35.7 all-reduce.44
  4752.4 44.0 convert_reduce_fusion.1
  4804.6 44.2 convert_reduce_fusion.3
  4855.2 43.9 convert_reduce_fusion.2
  (1043 shorter events, 1100.4 us)
Async XLA Ops:
  7.2 218.5 %all-gather.27.cloned.1.call-start = ((), (), s32[]{:S(2)}) async-start(), calls=%async_computation.13 | async-start | bytes 2304000 | tf_op jit(solution)/shard_map/all_gather | solution.py:127
  7.9 228.3 %all-gather.29.cloned.1.call-start = ((), (), s32[]{:S(2)}) async-start(), calls=%async_computation.14 | async-start | bytes 5990400 | tf_op jit(solution)/shard_map/all_gather | solution.py:126
  8.7 259.4 %all-gather.31.cloned.1.call-start = ((), (), s32[]{:S(2)}) async-start(), calls=%async_computation.15 | async-start | bytes 5990400 | tf_op jit(solution)/shard_map/all_gather | solution.py:128
  9.4 650.9 %all-gather.33.cloned.1.call-start = ((), (), s32[]{:S(2)}) async-start(), calls=%async_computation.16 | async-start | bytes 23040000 | tf_op jit(solution)/shard_map/all_gather | solution.py:129
  10.0 815.1 %all-gather.35.cloned.1.call-start = ((), (), s32[]{:S(2)}) async-start(), calls=%async_computation.17 | async-start | bytes 11980800 | tf_op jit(solution)/shard_map/all_gather | solution.py:137
  10.6 1143.1 %all-gather.37.cloned.1.call-start = ((), (), s32[]{:S(2)}) async-start(), calls=%async_computation.18 | async-start | bytes 19814400 | tf_op jit(solution)/shard_map/all_gather | solution.py:231
  11.2 1482.8 %all-gather.39.cloned.1.call-start = ((), (), s32[]{:S(2)}) async-start(), calls=%async_computation.19 | async-start | bytes 19814400 | tf_op jit(solution)/shard_map/all_gather | solution.py:232
  12.0 1835.5 %all-gather.41.cloned.1.call-start = ((), (), s32[]{:S(2)}) async-start(), calls=%async_computation.20 | async-start | bytes 20606976 | tf_op jit(solution)/shard_map/all_gather | solution.py:233
  12.8 2102.2 %reduce-scatter.37.cloned.1.call-start = ((), (), s32[]{:S(2)}) async-start(), calls=%async_computation.21 | async-start | bytes 921600 | tf_op jit(solution)/shard_map/reduce_scatter | solution.py:441
  2211.2 236.3 %reduce-scatter.51.cloned.1.call-start = ((), (), s32[]{:S(2)}) async-start(), calls=%async_computation.33 | async-start | bytes 5990400
  2215.1 358.5 %reduce-scatter.55.cloned.1.call-start = ((), (), s32[]{:S(2)}) async-start(), calls=%async_computation.35 | async-start | bytes 5990400
  2220.2 537.6 %reduce-scatter.39.cloned.1.call-start = ((), (), s32[]{:S(2)}) async-start(), calls=%async_computation.22 | async-start | bytes 11980800 | tf_op jit(solution)/shard_map/reduce_scatter | solution.py:444
  2228.3 902.3 %reduce-scatter.59.cloned.1.call-start = ((), (), s32[]{:S(2)}) async-start(), calls=%async_computation.37 | async-start | bytes 19814400
  2238.3 1263.6 %reduce-scatter.61.cloned.1.call-start = ((), (), s32[]{:S(2)}) async-start(), calls=%async_computation.38 | async-start | bytes 19814400
  2248.3 1614.3 %reduce-scatter.41.cloned.1.call-start = ((), (), s32[]{:S(2)}) async-start(), calls=%async_computation.23 | async-start | bytes 20606976 | tf_op jit(solution)/shard_map/reduce_scatter | solution.py:260
  2258.6 1995.9 %reduce-scatter.57.cloned.1.call-start = ((), (), s32[]{:S(2)}) async-start(), calls=%async_computation.36 | async-start | bytes 23040000
  2287.6 2190.9 %all-reduce.53.cloned.1.call-start = ((), (), s32[]{:S(2)}) async-start(), calls=%async_computation.39 | async-start | bytes 24342528
  4260.4 286.7 %reduce-scatter.45.cloned.1.call-start = ((), (), s32[]{:S(2)}) async-start(), calls=%async_computation.30 | async-start | bytes 921600
  4265.6 334.1 %reduce-scatter.47.cloned.1.call-start = ((), (), s32[]{:S(2)}) async-start(), calls=%async_computation.31 | async-start | bytes 921600
  4266.9 472.6 %all-gather.45.cloned.1.call-start = ((), (), s32[]{:S(2)}) async-start(), calls=%async_computation.25 | async-start | bytes 3200000 | tf_op jit(solution)/shard_map/all_gather | solution.py:535
  4484.5 267.9 %all-gather.51.cloned.1.call-start = ((), (), s32[]{:S(2)}) async-start(), calls=%async_computation.28 | async-start | bytes 5504000 | tf_op jit(solution)/shard_map/all_gather | solution.py:544
  4493.6 311.0 %all-gather.47.cloned.1.call-start = ((), (), s32[]{:S(2)}) async-start(), calls=%async_computation.26 | async-start | bytes 5504000 | tf_op jit(solution)/shard_map/all_gather | solution.py:538
  4502.1 353.1 %all-gather.49.cloned.1.call-start = ((), (), s32[]{:S(2)}) async-start(), calls=%async_computation.27 | async-start | bytes 5504000 | tf_op jit(solution)/shard_map/all_gather | solution.py:541
  4518.6 387.0 %all-gather.43.cloned.1.call-start = ((), (), s32[]{:S(2)}) async-start(), calls=%async_computation.24 | async-start | bytes 6400000 | tf_op jit(solution)/shard_map/all_gather | solution.py:511
  (126 other events, 7623.4 us)
Sparse Core Ops, SparseCore 0:
  10.2 52.0 all-gather.26
  64.5 113.2 all-gather.28
  180.0 88.0 all-gather.30
  269.5 390.8 all-gather.32
  662.4 152.8 all-gather.34
  816.6 336.9 all-gather.36
  1155.2 338.7 all-gather.38
  1495.5 351.9 all-gather.40
  2057.8 57.0 reduce-scatter.36
  2119.2 64.3 reduce-scatter.48
  2247.2 73.1 reduce-scatter.52
  2324.1 123.3 reduce-scatter.50
  2450.8 122.8 reduce-scatter.54
  2577.5 180.2 reduce-scatter.38
  2760.1 370.4 reduce-scatter.58
  3132.9 368.9 reduce-scatter.60
  3505.9 356.6 reduce-scatter.40
  3866.0 388.5 reduce-scatter.56
  4260.6 217.8 all-reduce.52
  4482.8 57.3 reduce-scatter.44
  4543.4 56.2 reduce-scatter.46
  4666.6 42.4 all-gather.46
  4711.2 41.6 all-gather.48
  4754.6 39.7 all-gather.42
  (4 shorter events, 113.4 us)
where the time goes:
time: 4960 us; the launch traced here: 4940 us
  waiting for transfers between devices  3700 us (75%)
  other arithmetic  378 us (8%)
  blocking collectives  339 us (7%)
  local copies, waits for them, and re-layouts  273 us (6%)
  matrix products  213 us (4%)
    unnamed x39, waiting for transfers between devices  1690 us
    all_gather x1, waiting for transfers between devices, on_device(): lax.all_gather(mamba_in, 'fsdp', axis=0, tiled=True)  387 us
    reduce_scatter x1, waiting for transfers between devices, on_device(): lax.psum_scatter(down_wgrad.astype(jnp.bfloat16), 'fsdp', scatter_dimensi...  355 us
    all_gather x1, waiting for transfers between devices, on_device(): lax.all_gather(down_weight, 'fsdp', axis=0, tiled=True)  343 us
    all_gather x1, waiting for transfers between devices, on_device(): lax.all_gather(up_weight, 'fsdp', axis=0, tiled=True)  330 us
    all_gather x1, waiting for transfers between devices, on_device(): lax.all_gather(gate_weight, 'fsdp', axis=0, tiled=True)  318 us
    reduce_scatter x1, waiting for transfers between devices, on_device(): lax.psum_scatter(mamba_wgrad.astype(jnp.bfloat16), 'fsdp', scatter_dimens...  181 us
    reshape x8, other arithmetic, on_device(): piece.reshape(shape)  170 us
  transfers between devices with their start and end apart: 28, of which 18 were waited for; matrix products, arithmetic and copies ran while one was open for 12% of the time, Pallas kernels for 0%

commit v1 on v0

v1 whole, which is shorter than its diff:
```python
import functools
import math

import jax
import jax.numpy as jnp
from jax import lax
from jax.experimental import pallas as pl
from jax.experimental.pallas import tpu as pltpu
from jax.sharding import PartitionSpec as P

H = 25
KV = 5
HD = 64
INNER = 3200
NS = 16
RANK = 100
CONV = 4

EPS = 1e-06
score_scale = 0.125
MESH = pl.DeviceIdType.MESH
ANY = pl.BlockSpec(memory_space=pl.ANY)
VM = pl.BlockSpec(memory_space=pltpu.VMEM)
DMA = pltpu.SemaphoreType.DMA
f32 = jnp.float32
bf16 = jnp.bfloat16


def params(cid, vmem=None):
    return pltpu.CompilerParams(collective_id=cid, has_side_effects=True, vmem_limit_bytes=vmem)


def rcopy(src, dst, ssem, rsem, dev):
    return pltpu.make_async_remote_copy(
        src_ref=src, dst_ref=dst, send_sem=ssem, recv_sem=rsem, device_id=dev, device_id_type=MESH
    )


def greet_line(a, b, lanes):
    bar = pltpu.get_barrier_semaphore()

    @pl.when(a > 0)
    def _():
        pl.semaphore_signal(bar, inc=1, device_id={"fsdp": 2 * (a - 1) + b}, device_id_type=MESH)

    @pl.when(a < lanes - 1)
    def _():
        pl.semaphore_signal(bar, inc=1, device_id={"fsdp": 2 * (a + 1) + b}, device_id_type=MESH)

    pl.semaphore_signal(bar, inc=1, device_id={"fsdp": 2 * a + 1 - b}, device_id_type=MESH)
    peers = 1 + (a > 0).astype(jnp.int32) + (a < lanes - 1).astype(jnp.int32)
    pl.semaphore_wait(bar, peers)


def greet_all(axis, size):
    me = lax.axis_index(axis)
    bar = pltpu.get_barrier_semaphore()
    for d in range(1, size):
        pl.semaphore_signal(
            bar, inc=1, device_id={axis: lax.rem(me + d, size)}, device_id_type=MESH
        )
    pl.semaphore_wait(bar, size - 1)


def gather_rows(x, size, cid):
    rows, cols = x.shape
    lanes = size // 2
    steps = lanes - 1

    def kernel(x_ref, o_ref, lsem, up_s, up_r, dn_s, dn_r, px_s, px_r):
        f = lax.axis_index("fsdp")
        a, b = f // 2, lax.rem(f, 2)
        greet_line(a, b, lanes)
        mine = o_ref.at[pl.ds(pl.multiple_of(f * rows, rows), rows)]
        local = pltpu.make_async_copy(x_ref, mine, lsem)
        local.start()

        def piece(origin):
            at = pl.multiple_of((2 * origin + b) * rows, rows)
            return o_ref.at[pl.ds(at, rows)]

        def up(s):
            src = x_ref if s == 0 else piece(a - s)
            return rcopy(src, piece(a - s), up_s.at[s], up_r.at[s], {"fsdp": 2 * (a + 1) + b})

        def down(s):
            src = x_ref if s == 0 else piece(a + s)
            return rcopy(src, piece(a + s), dn_s.at[s], dn_r.at[s], {"fsdp": 2 * (a - 1) + b})

        def across(origin, own=False):
            src = x_ref if own else piece(origin)
            return rcopy(
                src, piece(origin), px_s.at[origin], px_r.at[origin], {"fsdp": 2 * a + 1 - b}
            )

        def partner(origin):
            at = pl.multiple_of((2 * origin + 1 - b) * rows, rows)
            ref = o_ref.at[pl.ds(at, rows)]
            return rcopy(ref, ref, px_s.at[origin], px_r.at[origin], {"fsdp": 2 * a + 1 - b})

        @pl.when(a < lanes - 1)
        def _():
            up(0).start()

        @pl.when(a > 0)
        def _():
            down(0).start()

        across(a, True).start()
        for s in range(steps):
            @pl.when(a - 1 - s >= 0)
            def _():
                o = piece(a - 1 - s)
                rcopy(o, o, up_s.at[s], up_r.at[s], {"fsdp": 2 * (a - 1) + b}).wait_recv()

                @pl.when(a < lanes - 1)
                def _():
                    up(s + 1).start()

                across(a - 1 - s).start()

            @pl.when(a + 1 + s <= lanes - 1)
            def _():
                o = piece(a + 1 + s)
                rcopy(o, o, dn_s.at[s], dn_r.at[s], {"fsdp": 2 * (a + 1) + b}).wait_recv()

                @pl.when(a > 0)
                def _():
                    down(s + 1).start()

                across(a + 1 + s).start()

        local.wait()
        for s in range(steps):
            @pl.when((a - s >= 0) & (a < lanes - 1))
            def _():
                up(s).wait_send()

            @pl.when((a + s <= lanes - 1) & (a > 0))
            def _():
                down(s).wait_send()

        for origin in range(lanes):
            across(origin).wait_send()
            partner(origin).wait_recv()

    return pl.pallas_call(
        kernel,
        out_shape=jax.ShapeDtypeStruct((size * rows, cols), x.dtype),
        in_specs=[ANY],
        out_specs=ANY,
        scratch_shapes=[DMA]
        + [DMA((lanes,))] * 6,
        compiler_params=params(cid),
        name="gather_rows",
    )(x)


def scatter_rows(p, size, cid):
    rows, cols = p.shape[0] // size, p.shape[1]
    lanes = size // 2
    part = 32 if rows % 32 == 0 else rows

    def kernel(p_ref, o_ref, xbuf, upb, dnb, up_s, up_r, dn_s, dn_r, px_s, px_r):
        f = lax.axis_index("fsdp")
        a, b = f // 2, lax.rem(f, 2)
        greet_line(a, b, lanes)

        def across(dest):
            src = p_ref.at[pl.ds(pl.multiple_of((2 * dest + 1 - b) * rows, rows), rows)]
            return rcopy(
                src, xbuf.at[dest], px_s.at[dest], px_r.at[dest], {"fsdp": 2 * a + 1 - b}
            )

        def up(dest):
            return rcopy(
                xbuf.at[dest], upb.at[dest], up_s.at[dest], up_r.at[dest], {"fsdp": 2 * (a + 1) + b}
            )

        def down(dest):
            return rcopy(
                xbuf.at[dest], dnb.at[dest], dn_s.at[dest], dn_r.at[dest], {"fsdp": 2 * (a - 1) + b}
            )

        def add_in(dest, extra):
            base = pl.multiple_of((2 * dest + b) * rows, rows)

            def body(i, carry):
                at = pl.multiple_of(i * part, part)
                total = xbuf[dest, pl.ds(at, part), :].astype(f32)
                total += p_ref[pl.ds(base + at, part), :].astype(f32)
                if extra is not None:
                    total += extra[dest, pl.ds(at, part), :].astype(f32)
                xbuf[dest, pl.ds(at, part), :] = total.astype(bf16)
                return carry

            lax.fori_loop(0, rows // part, body, 0)

        for d in range(lanes - 1, -1, -1):
            @pl.when(a + d <= lanes - 1)
            def _():
                across(a + d).start()

            if d > 0:
                @pl.when(a - d >= 0)
                def _():
                    across(a - d).start()

        for d in range(lanes - 1, 0, -1):
            @pl.when(a + d <= lanes - 1)
            def _():
                across(a + d).wait_recv()

                @pl.when(a > 0)
                def _():
                    up(a + d).wait_recv()
                    add_in(a + d, upb)

                @pl.when(a == 0)
                def _():
                    add_in(a + d, None)

                up(a + d).start()

            @pl.when(a - d >= 0)
            def _():
                across(a - d).wait_recv()

                @pl.when(a < lanes - 1)
                def _():
                    down(a - d).wait_recv()
                    add_in(a - d, dnb)

                @pl.when(a == lanes - 1)
                def _():
                    add_in(a - d, None)

                down(a - d).start()

        across(a).wait_recv()

        @pl.when(a > 0)
        def _():
            up(a).wait_recv()

        @pl.when(a < lanes - 1)
        def _():
            down(a).wait_recv()

        base = pl.multiple_of((2 * a + b) * rows, rows)
        below, above = (a > 0).astype(f32), (a < lanes - 1).astype(f32)

        def last(i, carry):
            at = pl.multiple_of(i * part, part)
            total = xbuf[a, pl.ds(at, part), :].astype(f32)
            total += p_ref[pl.ds(base + at, part), :].astype(f32)
            o_ref[pl.ds(at, part), :] = total
            return carry

        lax.fori_loop(0, rows // part, last, 0)

        def more(buf):
            def body(i, carry):
                at = pl.multiple_of(i * part, part)
                o_ref[pl.ds(at, part), :] += buf[a, pl.ds(at, part), :].astype(f32)
                return carry

            lax.fori_loop(0, rows // part, body, 0)

        @pl.when(a > 0)
        def _():
            more(upb)

        @pl.when(a < lanes - 1)
        def _():
            more(dnb)

        for dest in range(lanes):
            across(dest).wait_send()

        for d in range(lanes - 1, 0, -1):
            @pl.when(a + d <= lanes - 1)
            def _():
                up(a + d).wait_send()

            @pl.when(a - d >= 0)
            def _():
                down(a - d).wait_send()

    return pl.pallas_call(
        kernel,
        out_shape=jax.ShapeDtypeStruct((rows, cols), f32),
        in_specs=[VM],
        out_specs=VM,
        scratch_shapes=[pltpu.VMEM((lanes, rows, cols), bf16)] * 3 + [DMA((lanes,))] * 6,
        compiler_params=params(cid, 60 << 20),
        name="scatter_rows",
    )(p)


def exchange(x, size, cid, axis="fsdp"):
    def kernel(x_ref, o_ref, lsem, ssem, rsem):
        me = lax.axis_index(axis)
        greet_all(axis, size)
        local = pltpu.make_async_copy(x_ref.at[me], o_ref.at[me], lsem)
        local.start()
        copies = []
        for d in range(1, size):
            to = lax.rem(me + d, size)
            copies.append(
                rcopy(x_ref.at[to], o_ref.at[me], ssem.at[d], rsem.at[d], {axis: to})
            )
            copies[-1].start()
        local.wait()
        for copy in copies:
            copy.wait()

    return pl.pallas_call(
        kernel,
        out_shape=jax.ShapeDtypeStruct(x.shape, x.dtype),
        in_specs=[ANY],
        out_specs=ANY,
        scratch_shapes=[DMA, DMA((size,)), DMA((size,))],
        compiler_params=params(cid),
        name="exchange",
    )(x)


def sum_rows(p, size, cid):
    rows, cols = p.shape[0] // size, p.shape[1]

    def kernel(p_ref, o_ref, buf, ssem, rsem, gs, gr):
        me = lax.axis_index("fsdp")
        greet_all("fsdp", size)

        def at(i):
            return pl.ds(pl.multiple_of(i * rows, rows), rows)

        first = []
        for d in range(1, size):
            to = lax.rem(me + d, size)
            first.append(
                rcopy(p_ref.at[at(to)], buf.at[d], ssem.at[d], rsem.at[d], {"fsdp": to})
            )
            first[-1].start()
        total = p_ref[at(me), :].astype(f32)
        for d in range(1, size):
            first[d - 1].wait_recv()
            total += buf[d].astype(f32)
        o_ref[at(me), :] = total.astype(bf16)
        second = []
        for d in range(1, size):
            to = lax.rem(me + d, size)
            second.append(
                rcopy(o_ref.at[at(me)], o_ref.at[at(me)], gs.at[d], gr.at[d], {"fsdp": to})
            )
            second[-1].start()
        for d in range(1, size):
            first[d - 1].wait_send()
            second[d - 1].wait()

    return pl.pallas_call(
        kernel,
        out_shape=jax.ShapeDtypeStruct(p.shape, bf16),
        in_specs=[VM],
        out_specs=VM,
        scratch_shapes=[pltpu.VMEM((size, rows, cols), bf16)] + [DMA((size,))] * 4,
        compiler_params=params(cid, 32 << 20),
        name="sum_rows",
    )(p)


def gather_ctx(x, size, cid):
    half = size // 2

    def kernel(x_ref, o_ref, lsem, ssem, rsem):
        c = lax.axis_index("ctx")
        greet_all("ctx", size)
        local = pltpu.make_async_copy(x_ref, o_ref.at[c], lsem)
        local.start()
        copies = []
        for d in range(1, size):
            copies.append(
                rcopy(x_ref, o_ref.at[c], ssem.at[d], rsem.at[d], {"ctx": lax.rem(c + d, size)})
            )
            copies[-1].start()
        local.wait()
        for copy in copies:
            copy.wait()

    return pl.pallas_call(
        kernel,
        out_shape=jax.ShapeDtypeStruct((size,) + x.shape, x.dtype),
        in_specs=[ANY],
        out_specs=ANY,
        scratch_shapes=[DMA, DMA((size,)), DMA((size,))],
        compiler_params=params(cid),
        name="gather_ctx",
    )(x)

def norm_forward(values, gain):
    inverse = lax.rsqrt(jnp.mean(values * values, axis=-1, keepdims=True) + EPS)
    return (values * inverse * gain, inverse)


def norm_backward(grad, values, inverse, gain):
    normed = values * inverse
    gain_grad = jnp.sum(grad * normed, axis=0)
    scaled = grad * gain
    return (
        inverse * (scaled - normed * jnp.mean(scaled * normed, axis=-1, keepdims=True)),
        gain_grad,
    )


def silu_slope(values):
    sigma = jax.nn.sigmoid(values)
    return sigma * (1.0 + values * (1.0 - sigma))


def block_scan(start, rate, steps, inputs, writes, reads):
    batch_count, length, channels = steps.shape
    piece_len = math.gcd(length, 8)
    pieces = length // piece_len

    def split(values):
        return values.reshape(batch_count, pieces, piece_len, values.shape[-1]).transpose(
            1, 0, 2, 3
        )

    def one_piece(carried, columns):
        step_c, input_c, write_c, read_c = columns
        climbing = jnp.cumsum(step_c[:, :, None, :] * rate, axis=1)
        pushed = write_c[:, :, :, None] * (step_c * input_c)[:, :, None, :]
        inner = jnp.exp(climbing) * (
            carried[:, None] + jnp.cumsum(jnp.exp(-climbing) * pushed, axis=1)
        )
        return (inner[:, -1], jnp.sum(inner * read_c[:, :, :, None], axis=2))

    final, outputs = lax.scan(
        jax.checkpoint(one_piece), start, (split(steps), split(inputs), split(writes), split(reads))
    )
    return (outputs.transpose(1, 0, 2, 3).reshape(batch_count, length, channels), final)


def on_device(
    layer_in,
    out_grad,
    doc_lengths,
    block_deal,
    norm_gains,
    query_weight,
    keyval_weight,
    attn_proj,
    mamba_in,
    conv_taps,
    conv_bias,
    step_bias,
    skip_gain,
    decay_log,
    select_proj,
    step_proj,
    mamba_proj,
    gate_weight,
    up_weight,
    down_weight,
):
    size = lax.axis_size("fsdp")
    n_ctx = lax.axis_size("ctx")
    rows = layer_in.shape[1]
    half_rows = rows // 2
    width = layer_in.shape[2]
    blocks_all = 2 * n_ctx
    group = H // KV
    chan = INNER // size
    q_cols, kv_cols = H * HD // size, 2 * KV * HD // size
    ff_cols = gate_weight.shape[1] // size
    rows_all = size * rows
    ctx_place = lax.axis_index("ctx")
    deal_flat = block_deal.reshape(-1)
    my_blocks = lax.dynamic_slice_in_dim(block_deal, ctx_place, 1, 0)[0]
    offsets = jnp.arange(half_rows, dtype=jnp.int32)
    my_places = (my_blocks[:, None] * half_rows + offsets[None, :]).reshape(-1)
    key_places = (deal_flat[:, None] * half_rows + offsets[None, :]).reshape(-1)
    lengths = doc_lengths[0]
    starts = jnp.cumsum(lengths) - lengths

    def segment(places):
        return jnp.sum((places[:, None] >= starts[None, :]).astype(jnp.int32), axis=1)

    allowed = (key_places[None, :] <= my_places[:, None]) & (
        segment(key_places)[None, :] == segment(my_places)[:, None]
    )
    inverse = jnp.argsort(deal_flat)

    def to_columns(weight, cols):
        return lax.all_to_all(weight, "fsdp", split_axis=1, concat_axis=0, tiled=True)

    gain_float = lax.all_gather(norm_gains, "fsdp", axis=1, tiled=True).astype(f32)
    depth = query_weight.shape[0]
    first_cols = jnp.concatenate(
        [
            query_weight.reshape(depth, size, q_cols),
            keyval_weight.reshape(depth, size, kv_cols),
            mamba_in[:, :INNER].reshape(depth, size, chan),
            mamba_in[:, INNER:].reshape(depth, size, chan),
        ],
        axis=2,
    ).transpose(1, 0, 2)
    first_mat = lax.all_to_all(first_cols, "fsdp", 0, 0, tiled=True).reshape(width, -1)
    ffn_cols = jnp.concatenate(
        [
            gate_weight.reshape(depth, size, ff_cols),
            up_weight.reshape(depth, size, ff_cols),
        ],
        axis=2,
    ).transpose(1, 0, 2)
    ffn_mat = lax.all_to_all(ffn_cols, "fsdp", 0, 0, tiled=True).reshape(width, -1)
    attn_mat = lax.all_gather(attn_proj, "fsdp", axis=0, tiled=True)
    qkv_mat = first_mat[:, : q_cols + kv_cols]
    entry_mat = first_mat[:, q_cols + kv_cols :]
    gate_mat, up_mat = ffn_mat[:, :ff_cols], ffn_mat[:, ff_cols:]

    stream_all = gather_rows(layer_in[0], size, 0)
    stream = layer_in[0].astype(f32)
    _, inv_in = norm_forward(stream, gain_float[0])
    normed_all, _ = norm_forward(stream_all.astype(f32), gain_float[0])
    normed_all = normed_all.astype(bf16)
    grads_all = gather_rows(out_grad[0], size, 1)

    qkv = jnp.dot(normed_all, qkv_mat, preferred_element_type=f32).astype(bf16)
    qkv = exchange(qkv.reshape(size, rows, -1), size, 2)
    queries = qkv[:, :, :q_cols].transpose(1, 0, 2).reshape(rows, H * HD)
    keyvals = qkv[:, :, q_cols:].transpose(1, 0, 2).reshape(rows, 2 * KV * HD)
    keyvals_all = gather_ctx(keyvals, n_ctx, 3).reshape(n_ctx * rows, 2 * KV * HD)
    query_groups = queries.reshape(rows, KV, group, HD).transpose(1, 0, 2, 3)
    key_groups = keyvals_all[:, : KV * HD].reshape(-1, KV, HD).transpose(1, 0, 2)
    value_groups = keyvals_all[:, KV * HD :].reshape(-1, KV, HD).transpose(1, 0, 2)

    def attend(parts):
        query_part, key_part, value_part = parts
        scores = (
            jnp.einsum("lgd,sd->gls", query_part, key_part, preferred_element_type=f32)
            * score_scale
        )
        scores = jnp.where(allowed[None], scores, -1e30)
        largest = jnp.max(scores, axis=-1, keepdims=True)
        expo = jnp.exp(scores - largest)
        total = jnp.sum(expo, axis=-1, keepdims=True)
        probs = (expo / total).astype(bf16)
        output = jnp.einsum("gls,sd->lgd", probs, value_part, preferred_element_type=f32)
        return (output, largest + jnp.log(total))

    attn_groups, log_totals = lax.map(attend, (query_groups, key_groups, value_groups))
    attn_rows = attn_groups.transpose(1, 0, 2, 3).reshape(rows, H * HD).astype(bf16)
    attn_out = jnp.dot(attn_rows, attn_mat, preferred_element_type=f32)
    attn_normed, inv_attn = norm_forward(attn_out, gain_float[1])

    entry = jnp.dot(normed_all, entry_mat, preferred_element_type=f32)
    mixer_in = entry[:, :chan].astype(bf16)
    gate_side = entry[:, chan:]
    mixer_blocks = mixer_in.reshape(size, 2, half_rows, chan)
    tails = mixer_blocks[:, :, half_rows - (CONV - 1) :]
    tails_all = gather_ctx(tails.reshape(-1, chan), n_ctx, 4)
    tails_all = tails_all.reshape(n_ctx, size, 2, CONV - 1, chan)

    def in_deal_order(values):
        return jnp.moveaxis(values, 2, 1).reshape((blocks_all,) + (size,) + values.shape[3:])

    def of_blocks(values, index):
        return jnp.moveaxis(jnp.take(values, index, axis=0), 0, 1)

    before_index = inverse[jnp.maximum(my_blocks - 1, 0)]
    has_before = my_blocks > 0
    prior_tail = jnp.where(
        has_before[None, :, None, None],
        of_blocks(in_deal_order(tails_all), before_index),
        jnp.zeros_like(tails),
    )
    padded = jnp.concatenate([prior_tail, mixer_blocks], axis=2).astype(f32)
    taps_float = conv_taps.astype(f32)
    conv_blocks_out = conv_bias.astype(f32) + sum(
        taps_float[offset] * padded[:, :, offset : offset + half_rows] for offset in range(CONV)
    )
    conv_out = conv_blocks_out.reshape(rows_all, chan)
    signal = jax.nn.silu(conv_out).astype(bf16)
    signal_float = signal.astype(f32)
    selected_part = jnp.dot(signal, select_proj, preferred_element_type=f32)
    selected = sum_rows(selected_part.astype(bf16), size, 5)
    step_low = selected[:, :RANK]
    writes = selected[:, RANK : RANK + NS].astype(f32)
    reads = selected[:, RANK + NS :].astype(f32)
    step_pre = jnp.dot(step_low, step_proj, preferred_element_type=f32) + step_bias.astype(f32)
    step_sizes = jax.nn.softplus(step_pre)
    rate = -jnp.exp(decay_log.astype(f32))
    pair = size * 2
    block_steps = step_sizes.reshape(pair, half_rows, chan)
    block_inputs = signal_float.reshape(pair, half_rows, chan)
    block_writes = writes.reshape(pair, half_rows, NS)
    block_reads = reads.reshape(pair, half_rows, NS)
    zero_state = jnp.zeros((pair, NS, chan), f32)
    _, local_end = block_scan(
        zero_state, rate, block_steps, block_inputs, block_writes, block_reads
    )
    step_totals = jnp.sum(block_steps, axis=1)
    ends_all = gather_ctx(
        jnp.concatenate([local_end, step_totals[:, None, :]], axis=1)
        .astype(bf16)
        .reshape(-1, chan),
        n_ctx,
        6,
    )
    ends_all = in_deal_order(ends_all.reshape(n_ctx, size, 2, NS + 1, chan)).astype(f32)
    ends_true = jnp.take(ends_all, inverse, axis=0)
    decays_true = jnp.exp(rate * ends_true[:, :, NS:])
    ends_true = ends_true[:, :, :NS]

    def link(carried, both):
        decay_part, end_part = both
        return (decay_part * carried + end_part, carried)

    link_zero = jnp.zeros((size, NS, chan), f32)
    _, starts_true = lax.scan(link, link_zero, (decays_true, ends_true))
    start_state = of_blocks(starts_true, my_blocks).reshape(pair, NS, chan)
    (scan_blocks, _), scan_pull = jax.vjp(
        block_scan, start_state, rate, block_steps, block_inputs, block_writes, block_reads
    )
    skip_float = skip_gain.astype(f32)
    scanned = scan_blocks.reshape(rows_all, chan) + skip_float * signal_float
    gate_act = jax.nn.silu(gate_side)
    mamba_rows = (scanned * gate_act).astype(bf16)
    mamba_part = jnp.dot(mamba_rows, mamba_proj, preferred_element_type=f32).astype(bf16)
    mamba_out = scatter_rows(mamba_part, size, 7)
    mamba_normed, inv_mamba = norm_forward(mamba_out, gain_float[2])
    middle = stream + 0.5 * (attn_normed + mamba_normed)
    ffn_normed, inv_ffn = norm_forward(middle, gain_float[3])
    ffn_low = gather_rows(ffn_normed.astype(bf16), size, 8)
    gate_pre = jnp.dot(ffn_low, gate_mat, preferred_element_type=f32)
    up_pre = jnp.dot(ffn_low, up_mat, preferred_element_type=f32)
    hidden = (jax.nn.silu(gate_pre) * up_pre).astype(bf16)
    down_part = jnp.dot(hidden, down_weight, preferred_element_type=f32).astype(bf16)
    result = middle + scatter_rows(down_part, size, 9)
    down_wgrad = jnp.einsum("lf,ld->fd", hidden, grads_all, preferred_element_type=f32)
    hidden_back = jnp.einsum("ld,fd->lf", grads_all, down_weight, preferred_element_type=f32)
    gate_back = (hidden_back * up_pre * silu_slope(gate_pre)).astype(bf16)
    up_back = (hidden_back * jax.nn.silu(gate_pre)).astype(bf16)
    gate_wgrad = jnp.einsum("ld,lf->df", ffn_low, gate_back, preferred_element_type=f32)
    up_wgrad = jnp.einsum("ld,lf->df", ffn_low, up_back, preferred_element_type=f32)
    ffn_back_part = jnp.einsum(
        "lf,df->ld", gate_back, gate_mat, preferred_element_type=f32
    ) + jnp.einsum("lf,df->ld", up_back, up_mat, preferred_element_type=f32)
    ffn_back = scatter_rows(ffn_back_part.astype(bf16), size, 10)
    middle_part, ffn_gain_grad = norm_backward(ffn_back, middle, inv_ffn, gain_float[3])
    middle_back = out_grad[0].astype(f32) + middle_part
    branch_back = 0.5 * middle_back
    attn_part, attn_gain_grad = norm_backward(branch_back, attn_out, inv_attn, gain_float[1])
    mamba_part_back, mamba_gain_grad = norm_backward(
        branch_back, mamba_out, inv_mamba, gain_float[2]
    )
    attn_back = attn_part.astype(bf16)
    mamba_back = gather_rows(mamba_part_back.astype(bf16), size, 11)
    attn_wgrad = jnp.einsum("lh,ld->hd", attn_rows, attn_back, preferred_element_type=f32)
    rows_back = jnp.einsum("ld,hd->lh", attn_back, attn_mat, preferred_element_type=f32).astype(
        bf16
    )
    mamba_wgrad = jnp.einsum("li,ld->id", mamba_rows, mamba_back, preferred_element_type=f32)
    mrows_back = jnp.einsum("ld,id->li", mamba_back, mamba_proj, preferred_element_type=f32)
    scan_back = mrows_back * gate_act
    side_back = mrows_back * scanned * silu_slope(gate_side)
    skip_grad = jnp.sum(scan_back * signal_float, axis=0)
    block_dout = scan_back.reshape(pair, half_rows, chan)
    local_back = scan_pull((block_dout, zero_state))[0]
    backs_all = gather_ctx(local_back.astype(bf16).reshape(-1, chan), n_ctx, 12)
    backs_all = in_deal_order(backs_all.reshape(n_ctx, size, 2, NS, chan)).astype(f32)
    backs_true = jnp.take(backs_all, inverse, axis=0)

    def link_back(grad_next, both):
        decay_part, back_part = both
        return (back_part + decay_part * grad_next, grad_next)

    _, ends_back_true = lax.scan(link_back, link_zero, (decays_true, backs_true), reverse=True)
    end_back = of_blocks(ends_back_true, my_blocks).reshape(pair, NS, chan)
    _, rate_back, steps_back, inputs_back, writes_back, reads_back = scan_pull(
        (block_dout, end_back)
    )
    decay_grad = rate_back * rate
    step_back = steps_back.reshape(rows_all, chan)
    signal_back = scan_back * skip_float + inputs_back.reshape(rows_all, chan)
    write_back = writes_back.reshape(rows_all, NS)
    read_back = reads_back.reshape(rows_all, NS)
    pre_back = (step_back * jax.nn.sigmoid(step_pre)).astype(bf16)
    step_wgrad = jnp.einsum("lr,li->ri", step_low, pre_back, preferred_element_type=f32)
    bias_grad = jnp.sum(pre_back.astype(f32), axis=0)
    rank_back = jnp.einsum("li,ri->lr", pre_back, step_proj, preferred_element_type=f32)
    select_back = sum_rows(
        jnp.concatenate([rank_back, write_back, read_back], axis=1).astype(bf16), size, 13
    )
    select_wgrad = jnp.einsum("li,lk->ik", signal, select_back, preferred_element_type=f32)
    signal_back = signal_back + jnp.einsum(
        "lk,ik->li", select_back, select_proj, preferred_element_type=f32
    )
    conv_back = signal_back * silu_slope(conv_out)
    conv_blocks = conv_back.reshape(size, 2, half_rows, chan)
    taps_grad = jnp.stack(
        [
            jnp.sum(conv_blocks * padded[:, :, offset : offset + half_rows], axis=(0, 1, 2))
            for offset in range(CONV)
        ]
    )
    shift_grad = jnp.sum(conv_back, axis=0)
    padded_back = sum(
        (
            jnp.pad(
                taps_float[offset] * conv_blocks,
                ((0, 0), (0, 0), (offset, CONV - 1 - offset), (0, 0)),
            )
            for offset in range(CONV)
        )
    )
    tail_back = jnp.where(has_before[None, :, None, None], padded_back[:, :, : CONV - 1], 0.0)
    tails_back_all = gather_ctx(tail_back.astype(bf16).reshape(-1, chan), n_ctx, 14)
    tails_back_all = in_deal_order(tails_back_all.reshape(n_ctx, size, 2, CONV - 1, chan))
    after_index = inverse[jnp.minimum(my_blocks + 1, blocks_all - 1)]
    has_after = my_blocks < blocks_all - 1
    incoming = jnp.where(
        has_after[None, :, None, None], of_blocks(tails_back_all, after_index).astype(f32), 0.0
    )
    mixer_back = padded_back[:, :, CONV - 1 :] + jnp.pad(
        incoming, ((0, 0), (0, 0), (half_rows - (CONV - 1), 0), (0, 0))
    )
    entry_back = jnp.concatenate([mixer_back.reshape(rows_all, chan), side_back], axis=1).astype(
        bf16
    )
    entry_wgrad = jnp.einsum("ld,lk->dk", normed_all, entry_back, preferred_element_type=f32)
    input_part = jnp.einsum("lk,dk->ld", entry_back, entry_mat, preferred_element_type=f32)

    dout_groups = rows_back.reshape(rows, KV, group, HD).transpose(1, 0, 2, 3)

    def attend_back(parts):
        query_part, key_part, value_part, dout_part, log_part = parts
        scores = (
            jnp.einsum("lgd,sd->gls", query_part, key_part, preferred_element_type=f32)
            * score_scale
        )
        scores = jnp.where(allowed[None], scores, -1e30)
        probs = jnp.exp(scores - log_part)
        value_grad = jnp.einsum(
            "gls,lgd->sd", probs.astype(bf16), dout_part, preferred_element_type=f32
        )
        prob_grad = jnp.einsum("lgd,sd->gls", dout_part, value_part, preferred_element_type=f32)
        centre = jnp.sum(probs * prob_grad, axis=-1, keepdims=True)
        score_grad = (probs * (prob_grad - centre)).astype(bf16)
        query_grad = (
            jnp.einsum("gls,sd->lgd", score_grad, key_part, preferred_element_type=f32)
            * score_scale
        )
        key_grad = (
            jnp.einsum("gls,lgd->sd", score_grad, query_part, preferred_element_type=f32)
            * score_scale
        )
        return (query_grad, key_grad, value_grad)

    query_grads, key_grads, value_grads = lax.map(
        attend_back, (query_groups, key_groups, value_groups, dout_groups, log_totals)
    )
    keyval_terms = jnp.concatenate(
        [
            key_grads.transpose(1, 0, 2).reshape(-1, KV * HD),
            value_grads.transpose(1, 0, 2).reshape(-1, KV * HD),
        ],
        axis=1,
    )
    keyval_parts = exchange(
        keyval_terms.astype(bf16).reshape(n_ctx, rows, 2 * KV * HD), n_ctx, 15, "ctx"
    )
    keyval_back = jnp.sum(keyval_parts.astype(f32), axis=0).astype(bf16)
    query_back = query_grads.transpose(1, 0, 2, 3).reshape(rows, H * HD).astype(bf16)
    qkv_back = jnp.concatenate(
        [
            query_back.reshape(rows, size, q_cols),
            keyval_back.reshape(rows, size, kv_cols),
        ],
        axis=2,
    ).transpose(1, 0, 2)
    qkv_back = exchange(qkv_back, size, 16).reshape(rows_all, -1)
    qkv_wgrad = jnp.einsum("ld,lk->dk", normed_all, qkv_back, preferred_element_type=f32)
    input_part = input_part + jnp.einsum(
        "lk,dk->ld", qkv_back, qkv_mat, preferred_element_type=f32
    )
    input_back = scatter_rows(input_part.astype(bf16), size, 17)
    stream_part, in_gain_grad = norm_backward(input_back, stream, inv_in, gain_float[0])
    stream_back = middle_back + stream_part
    gain_grad = jnp.stack([in_gain_grad, attn_gain_grad, mamba_gain_grad, ffn_gain_grad])

    def over_ctx(values):
        return lax.psum_scatter(
            values.astype(bf16), "ctx", scatter_dimension=0, tiled=True
        )

    def join(piece):
        return lax.all_gather(piece, "ctx", axis=0, tiled=True)

    def columns_home(wgrad):
        cols = wgrad.shape[1]
        cut = wgrad.reshape(size, n_ctx, depth // n_ctx, cols) if depth % n_ctx == 0 else None
        if cut is None:
            whole = lax.psum(wgrad.astype(bf16), "ctx")
            moved = lax.all_to_all(whole.reshape(size, depth, cols), "fsdp", 0, 0, tiled=True)
            return moved.transpose(1, 0, 2).astype(f32)
        piece = over_ctx(cut.transpose(1, 0, 2, 3).reshape(-1, cols))
        moved = lax.all_to_all(
            piece.reshape(size, depth // n_ctx, cols), "fsdp", 0, 0, tiled=True
        ).transpose(1, 0, 2)
        return join(moved).astype(f32)

    first_home = columns_home(jnp.concatenate([qkv_wgrad, entry_wgrad], axis=1))
    ffn_home = columns_home(jnp.concatenate([gate_wgrad, up_wgrad], axis=1))
    query_share = first_home[:, :, :q_cols].reshape(depth, -1)
    keyval_share = first_home[:, :, q_cols : q_cols + kv_cols].reshape(depth, -1)
    entry_share = jnp.concatenate(
        [
            first_home[:, :, q_cols + kv_cols : q_cols + kv_cols + chan].reshape(depth, -1),
            first_home[:, :, q_cols + kv_cols + chan :].reshape(depth, -1),
        ],
        axis=1,
    )
    gate_share = ffn_home[:, :, :ff_cols].reshape(depth, -1)
    up_share = ffn_home[:, :, ff_cols:].reshape(depth, -1)

    def all_ctx(values):
        return lax.psum(values.astype(bf16), "ctx").astype(f32)

    attn_share = all_ctx(
        lax.psum_scatter(attn_wgrad.astype(bf16), "fsdp", scatter_dimension=0, tiled=True)
    )
    gain_share = all_ctx(
        lax.psum_scatter(gain_grad.astype(bf16), "fsdp", scatter_dimension=1, tiled=True)
    )
    vectors = jnp.concatenate(
        [
            taps_grad,
            shift_grad[None],
            bias_grad[None],
            skip_grad[None],
            decay_grad,
            step_wgrad,
        ]
    )
    vectors = all_ctx(vectors)
    return (
        result.astype(bf16)[None],
        stream_back[None],
        gain_share,
        query_share,
        keyval_share,
        attn_share,
        entry_share,
        vectors[:CONV],
        vectors[CONV],
        vectors[CONV + 1],
        vectors[CONV + 2],
        vectors[CONV + 3 : CONV + 3 + NS],
        all_ctx(select_wgrad),
        vectors[CONV + 3 + NS :],
        all_ctx(mamba_wgrad),
        gate_share,
        up_share,
        all_ctx(down_wgrad),
    )


def solution(mesh):
    in_specs = (
        P("fsdp", "ctx", None),
        P("fsdp", "ctx", None),
        P("fsdp", None),
        P(),
        P(None, "fsdp"),
        P("fsdp", None),
        P("fsdp", None),
        P("fsdp", None),
        P("fsdp", None),
        P(None, "fsdp"),
        P("fsdp"),
        P("fsdp"),
        P("fsdp"),
        P(None, "fsdp"),
        P("fsdp", None),
        P(None, "fsdp"),
        P("fsdp", None),
        P("fsdp", None),
        P("fsdp", None),
        P("fsdp", None),
    )
    out_specs = (
        P("fsdp", "ctx", None),
        P("fsdp", "ctx", None),
        P(None, "fsdp"),
        P("fsdp", None),
        P("fsdp", None),
        P("fsdp", None),
        P("fsdp", None),
        P(None, "fsdp"),
        P("fsdp"),
        P("fsdp"),
        P("fsdp"),
        P(None, "fsdp"),
        P("fsdp", None),
        P(None, "fsdp"),
        P("fsdp", None),
        P("fsdp", None),
        P("fsdp", None),
        P("fsdp", None),
    )
    return jax.shard_map(
        on_device, mesh=mesh, in_specs=in_specs, out_specs=out_specs, check_vma=False
    )
```

time: 4960 us -> 1760 us (0.35)
  waiting for transfers between devices: 3700 us -> 33.8 us
  Pallas kernels: 0 us -> 689 us
  blocking collectives: 339 us -> 134 us
  local copies, waits for them, and re-layouts: 273 us -> 402 us
  other arithmetic: 378 us -> 306 us
  matrix products: 213 us -> 148 us
    unnamed x39 -> x8, waiting for transfers between devices: 1690 us -> 0.78 us
    all_gather x13 -> x3, waiting for transfers between devices: 1400 us -> 0.02 us  [the longest x1 0.02 us: on_device(): attn_mat = lax.all_gather(attn_proj, 'fsdp', axis=0, tiled=True)]
    pallas_call x0 -> x18, Pallas kernels: none -> 689 us  [the longest x4 301 us: gather_rows(): pl.pallas_call(kernel, out_shape=jax.ShapeDtypeStruct((size * rows, cols)...]
    reduce_scatter x4 -> x2, waiting for transfers between devices: 619 us -> 33 us  [over_ctx(): lax.psum_scatter(values.astype(bf16), 'ctx', scatter_dimension=0, tiled=T...]
    all_gather x14 -> x1, blocking collectives: 245 us -> 26.2 us  [on_device(): lax.all_gather(norm_gains, 'fsdp', axis=1, tiled=True).astype(f32)]
    reshape x8 -> x0, other arithmetic: 170 us -> none  [on_device(): piece.reshape(shape)]
    unnamed x305 -> x241, local copies, waits for them, and re-layouts: 84.8 us -> 14.1 us
    all_to_all x0 -> x2, blocking collectives: none -> 66.7 us  [columns_home(): lax.all_to_all(piece.reshape(size, depth // n_ctx, cols), 'fsdp', 0, 0, t...]
  transfers between devices with their start and end apart: 28 -> 9, of which waited for: 18 -> 2; matrix products, arithmetic and copies ran while one was open for 12% -> 29% of each run, Pallas kernels for 0% -> 30%
where the time goes in v1:
time: 1760 us; the launch traced here: 1750 us
  Pallas kernels  689 us (39%)
  local copies, waits for them, and re-layouts  402 us (23%)
  other arithmetic  306 us (17%)
  matrix products  148 us (8%)
  blocking collectives  134 us (8%)
  waiting for transfers between devices  33.8 us (2%)
    pallas_call x4, Pallas kernels, gather_rows(): pl.pallas_call(kernel, out_shape=jax.ShapeDtypeStruct((size * rows, cols)...  301 us
    pallas_call x4, Pallas kernels, scatter_rows(): pl.pallas_call(kernel, out_shape=jax.ShapeDtypeStruct((rows, cols), f32),...  180 us
    pallas_call x2, Pallas kernels, sum_rows(): pl.pallas_call(kernel, out_shape=jax.ShapeDtypeStruct(p.shape, bf16), in_...  104 us
    another operation x32, other arithmetic, one_piece(): jnp.cumsum(jnp.exp(-climbing) * pushed, axis=1)  101 us
    all_to_all x2, blocking collectives, columns_home(): lax.all_to_all(piece.reshape(size, depth // n_ctx, cols), 'fsdp', 0, 0, t...  66.7 us
    another operation x40, other arithmetic, one_piece(): climbing = jnp.cumsum(step_c[:, :, None, :] * rate, axis=1)  61.3 us
    pallas_call x3, Pallas kernels, exchange(): pl.pallas_call(kernel, out_shape=jax.ShapeDtypeStruct(x.shape, x.dtype),...  56.8 us
    pallas_call x5, Pallas kernels, gather_ctx(): pl.pallas_call(kernel, out_shape=jax.ShapeDtypeStruct((size,) + x.shape,...  47.2 us
  transfers between devices with their start and end apart: 9, of which 2 were waited for; matrix products, arithmetic and copies ran while one was open for 29% of the time, Pallas kernels for 30%

profile of v1, /device:TPU:0, one launch (start us, length us, event | category | flops | bytes accessed | tf_op | source)
XLA Modules:
  0.0 1745.5 jit_solution(17674355523085757322)
XLA Ops:
  49.0 185.2 %gather_rows.4 = bf16[1024,1600]{1,0:T(8,128)(2,1)} custom-call(bf16[128,1600]{1,0:T(8,128)(2,1)} %bitcast.482), custom_call_target="tpu_custom_call" | custom-call | tf_op jit(solution)/shard_map/gather_rows/pallas_call | solution.py:147
  234.3 26.2 %all-gather = bf16[8,200,4]{1,2,0:T(4,128)(2,1)S(1)} all-gather(bf16[1,200,4]{1,2,0:T(4,128)(2,1)S(1)} %bitcast.543), channel_id=1, replica_groups=mesh['ctx'=4,'fsdp'=8] {'fsdp'}, dimensions={0}, use_global_device_ids=true | all-gather | bytes 14400 | tf_op jit(solution)/shard_map/all_gather | solution.py:499
  283.8 38.6 %gather_rows.6 = bf16[1024,1600]{1,0:T(8,128)(2,1)} custom-call(bf16[128,1600]{1,0:T(8,128)(2,1)} %bitcast.503), custom_call_target="tpu_custom_call" | custom-call | tf_op jit(solution)/shard_map/gather_rows/pallas_call | solution.py:147
  372.0 80.6 %sum_rows.2 = bf16[1024,132]{1,0:T(8,128)(2,1)S(1)} custom-call(bf16[1024,132]{1,0:T(8,128)(2,1)S(1)} %copy.622.p_ref), custom_call_target="tpu_custom_call" | custom-call | tf_op jit(solution)/shard_map/sum_rows/pallas_call | solution.py:362
  470.4 54.7 %while.121 = (s32[]{:T(128)}, f32[16,16,400]{2,1,0:T(8,128)}, f32[8,16,8,400]{3,2,1,0:T(8,128)}, f32[16,400]{1,0:T(8,128)S(1)}, f32[8,16,8,16]{3,2,1,0:T(8,128)}, /*index=5*/f32[8,16,8,400]{3,2,1,0:T(8,128)}, s32[]{:T(128)}) while((s32[]{:T(128)}, f32[16,16,400]{2,1,0:T(8,128)}, f32[8,16,8,400]{3,2,1,0:T(8,128)}, f32[16,400]{1,0:T(8,128)S(1)}, ...), condition=%wide.region_13.15_spmd, body=%wide.region_10.14_spmd.sunk | while | flops 15001602 | bytes 16245885 | solution.py:440
  556.9 23.4 %while.126 = (s32[]{:T(128)}, f32[8,16,400]{2,1,0:T(8,128)S(1)}, f32[8,8,16,400]{3,2,1,0:T(8,128)}, f32[8,8,16,400]{3,2,1,0:T(8,128)}, f32[8,8,16,400]{3,1,2,0:T(8,128)}, /*index=5*/s32[]{:T(128)}, s32[]{:T(128)}) while((s32[]{:T(128)}, f32[8,16,400]{2,1,0:T(8,128)S(1)}, f32[8,8,16,400]{3,2,1,0:T(8,128)}, ...), condition=%wide.region_16.18_spmd.clone, body=%wide.region_15.17_spmd.clone.sunk | while | flops 204803 | bytes 1695852 | solution.py:623
  585.3 76.0 %while.122 = (s32[]{:T(128)}, f32[16,16,400]{2,1,0:T(8,128)S(1)}, f32[8,16,8,400]{3,1,2,0:T(8,128)}, f32[8,16,16,400]{3,2,1,0:T(8,128)}, f32[8,16,8,400]{3,2,1,0...) while((s32[]{:T(128)}, f32[16,16,400]{2,1,0:T(8,128)S(1)}, ...), condition=%wide.region_21.24_spmd, body=%wide.region_17.23_spmd.sunk | while | flops 18022400 | bytes 15025285 | solution.py:440
  666.2 18.2 %exchange.3 = bf16[8,128,280]{2,1,0:T(8,128)(2,1)} custom-call(bf16[8,128,280]{2,1,0:T(8,128)(2,1)} %bitcast.508), custom_call_target="tpu_custom_call" | custom-call | tf_op jit(solution)/shard_map/exchange/pallas_call | solution.py:318
  714.7 52.9 %scatter_rows.4 = f32[128,1600]{1,0:T(8,128)} custom-call(bf16[1024,1600]{1,0:T(8,128)(2,1)} %copy.644.p_ref), custom_call_target="tpu_custom_call" | custom-call | tf_op jit(solution)/shard_map/scatter_rows/pallas_call | solution.py:290
  806.2 43.7 %gather_rows.5 = bf16[1024,1600]{1,0:T(8,128)(2,1)} custom-call(bf16[128,1600]{1,0:T(8,128)(2,1)} %multiply_convert_fusion.11.x_ref), custom_call_target="tpu_custom_call" | custom-call | tf_op jit(solution)/shard_map/gather_rows/pallas_call | solution.py:147
  882.8 44.1 %scatter_rows.6 = f32[128,1600]{1,0:T(8,128)} custom-call(bf16[1024,1600]{1,0:T(8,128)(2,1)} %copy.648.p_ref), custom_call_target="tpu_custom_call" | custom-call | tf_op jit(solution)/shard_map/scatter_rows/pallas_call | solution.py:290
  940.5 40.4 %scatter_rows.5 = f32[128,1600]{1,0:T(8,128)} custom-call(bf16[1024,1600]{1,0:T(8,128)(2,1)} %copy.646.p_ref), custom_call_target="tpu_custom_call" | custom-call | tf_op jit(solution)/shard_map/scatter_rows/pallas_call | solution.py:290
  986.0 33.7 %gather_rows.7 = bf16[1024,1600]{1,0:T(8,128)(2,1)} custom-call(bf16[128,1600]{1,0:T(8,128)(2,1)} %get-tuple-element.1453.x_ref), custom_call_target="tpu_custom_call" | custom-call | tf_op jit(solution)/shard_map/gather_rows/pallas_call | solution.py:147
  1031.9 26.4 %while.123 = (s32[]{:T(128)}, f32[16,16,400]{2,1,0:T(8,128)S(1)}, f32[8,16,8,400]{3,1,2,0:T(8,128)}, f32[8,16,8,16]{3,1,2,0:T(8,128)}, f32[8,16,8,400]{3,1,2,0:T...) while((s32[]{:T(128)}, f32[16,16,400]{2,1,0:T(8,128)S(1)}, f32[8,16,8,400]{3,1,2,0:T(8,128)}, ...), condition=%wide.region_30.33_spmd, body=%wide.region_27.32_spmd.sunk | while | flops 9728003 | bytes 2917489 | solution.py:440
  1094.4 143.1 %while.128 = (s32[]{:T(128)}, f32[16,400]{1,0:T(8,128)S(1)}, f32[16,16,400]{2,1,0:T(8,128)S(1)}, f32[8,16,8,400]{3,1,2,0:T(8,128)}, f32[8,16,8,400]{3,1,2,0:T(8,...) while((s32[]{:T(128)}, f32[16,400]{1,0:T(8,128)S(1)}, ...), condition=%wide.region_44.47_spmd.clone, body=%wide.region_33.46_spmd.clone.sunk | while | flops 52431104 | bytes 39393492 | solution.py:440
  1247.2 23.6 %sum_rows.3 = bf16[1024,132]{1,0:T(8,128)(2,1)S(1)} custom-call(bf16[1024,132]{1,0:T(8,128)(2,1)S(1)} %pad_maximum_fusion.7.p_ref), custom_call_target="tpu_custom_call" | custom-call | tf_op jit(solution)/shard_map/sum_rows/pallas_call | solution.py:362
  1306.2 32.1 %while.125 = (s32[]{:T(128)}, bf16[5,128,5,64]{1,3,2,0:T(8,128)(2,1)S(1)}, bf16[5,512,64]{1,2,0:T(8,128)(2,1)S(1)}, bf16[5,512,64]{1,2,0:T(8,128)(2,1)S(1)}, bf1...) while((s32[]{:T(128)}, ...), condition=%wide.region_48.51_spmd.clone, body=%wide.region_46.50_spmd.clone.sunk | while | flops 212934016 | bytes 10934929 | solution.py:763
  1352.2 29.5 %exchange.5 = bf16[8,128,280]{2,1,0:T(8,128)(2,1)} custom-call(bf16[8,128,280]{2,1,0:T(8,128)(2,1)} %maximum_bitcast_fusion.1.x_ref), custom_call_target="tpu_custom_call" | custom-call | tf_op jit(solution)/shard_map/exchange/pallas_call | solution.py:318
  1471.0 16.8 reduce-scatter.7.cloned.1.call-done
  1489.2 30.7 %all_to_all.20 = bf16[8,50,1080]{2,1,0:T(8,128)(2,1)S(1)} all-to-all(bf16[8,50,1080]{2,1,0:T(8,128)(2,1)S(1)} %reshape.530), channel_id=1, replica_groups=mesh['ctx'=4,'fsdp'=8] {'fsdp'}, dimensions={0} | all-to-all | bytes 1728000 | tf_op jit(solution)/shard_map/all_to_all | solution.py:811
  1521.1 16.2 reduce-scatter.9.cloned.1.call-done
  1538.7 35.9 %all_to_all.21 = bf16[8,50,1376]{2,1,0:T(8,128)(2,1)S(1)} all-to-all(bf16[8,50,1376]{2,1,0:T(8,128)(2,1)S(1)} %reshape.535), channel_id=1, replica_groups=mesh['ctx'=4,'fsdp'=8] {'fsdp'}, dimensions={0} | all-to-all | bytes 2201600 | tf_op jit(solution)/shard_map/all_to_all | solution.py:811
  1590.4 42.2 %scatter_rows.7 = f32[128,1600]{1,0:T(8,128)} custom-call(bf16[1024,1600]{1,0:T(8,128)(2,1)} %copy.682.p_ref), custom_call_target="tpu_custom_call" | custom-call | tf_op jit(solution)/shard_map/scatter_rows/pallas_call | solution.py:290
  1636.9 35.0 %all-reduce.7 = bf16[4,1600]{1,0:T(4,128)(2,1)S(1)} all-reduce(bf16[4,1600]{1,0:T(4,128)(2,1)S(1)} %pad_maximum_fusion.9), channel_id=2, replica_groups=mesh['ctx'=4,'fsdp'=8] {'fsdp'}, use_global_device_ids=true, to_apply=%region_55.58.clone | all-reduce | flops 6400 | bytes 25600
  (997 shorter events, 953.4 us)
Async XLA Ops:
  7.2 853.8 %copy-start = (bf16[688,1600]{1,0:T(8,128)(2,1)S(1)}, bf16[688,1600]{1,0:T(8,128)(2,1)}, u32[]{:S(2)}) copy-start(bf16[688,1600]{1,0:T(8,128)(2,1)} %param.59) | copy-start | bytes 6604804
  39.8 291.1 %all-to-all-start = ((bf16[8,200,1080]{2,1,0:T(8,128)(2,1)}), bf16[8,200,1080]{2,1,0:T(8,128)(2,1)}, u32[]{:S(2)}, u32[]{:S(2)}) async-start(bf16[8,200,1080]{2,1,0:T(8,128)(2,1)} %bitcast.480), calls=%async_computation | async-start | bytes 7372800 | tf_op jit(solution)/shard_map/all_to_all | solution.py:510
  47.2 744.8 %all-gather.5.cloned.1.call-start = ((), (), s32[]{:S(2)}) async-start(), calls=%async_computation.7 | async-start | bytes 5990400 | tf_op jit(solution)/shard_map/all_gather | solution.py:519
  48.0 186.3 %copy-start.100 = (bf16[4,200]{1,0:T(4,128)(2,1)S(1)}, bf16[4,200]{1,0:T(4,128)(2,1)}, u32[]{:S(2)}) copy-start(bf16[4,200]{1,0:T(4,128)(2,1)} %param.44) | copy-start | bytes 4804
  48.0 212.6 %copy-start.93 = (s32[4,2]{0,1:T(2,128)S(1)}, s32[4,2]{0,1:T(2,128)}, u32[]{:S(2)}) copy-start(s32[4,2]{0,1:T(2,128)} %param.43) | copy-start | bytes 100
  48.0 213.3 %copy-start.108 = (s32[1,8]{1,0:T(1,128)S(1)}, s32[1,8]{1,0:T(1,128)}, u32[]{:S(2)}) copy-start(s32[1,8]{1,0:T(1,128)} %param.42) | copy-start | bytes 100
  48.0 213.5 %copy-start.102 = (bf16[400]{0:T(512)(128)(2,1)S(1)}, bf16[400]{0:T(512)(128)(2,1)}, u32[]{:S(2)}) copy-start(bf16[400]{0:T(512)(128)(2,1)} %param.51) | copy-start | bytes 2404
  48.0 214.4 %copy-start.103 = (bf16[400]{0:T(512)(128)(2,1)S(1)}, bf16[400]{0:T(512)(128)(2,1)}, u32[]{:S(2)}) copy-start(bf16[400]{0:T(512)(128)(2,1)} %param.50) | copy-start | bytes 2404
  48.1 214.4 %copy-start.84 = (bf16[16,400]{1,0:T(8,128)(2,1)S(1)}, bf16[16,400]{1,0:T(8,128)(2,1)}, u32[]{:S(2)}) copy-start(bf16[16,400]{1,0:T(8,128)(2,1)} %param.53) | copy-start | bytes 38404
  49.0 213.8 %copy-start.104 = (bf16[400]{0:T(512)(128)(2,1)S(1)}, bf16[400]{0:T(512)(128)(2,1)}, u32[]{:S(2)}) copy-start(bf16[400]{0:T(512)(128)(2,1)} %param.52) | copy-start | bytes 2404
  261.5 192.0 %copy-start.86 = (f32[400]{0:T(512)}, f32[400]{0:T(512)S(1)}, u32[]{:S(2)}) copy-start(f32[400]{0:T(512)S(1)} %convert_element_type.260) | copy-start | bytes 4804
  325.8 335.5 %copy-start.67 = (f32[1600]{0:T(1024)}, f32[1600]{0:T(1024)S(1)}, u32[]{:S(2)}) copy-start(f32[1600]{0:T(1024)S(1)} %get-tuple-element.1271) | copy-start | bytes 19204
  330.9 519.0 %all-to-all-start.1 = ((bf16[8,200,1376]{2,1,0:T(8,128)(2,1)}), bf16[8,200,1376]{2,1,0:T(8,128)(2,1)}, u32[]{:S(2)}, u32[]{:S(2)}) async-start(bf16[8,200,1376]{2,1,0:T(8,128)(2,1)} %copy.645), calls=%async_computation.1 | async-start | bytes 9011200 | tf_op jit(solution)/shard_map/all_to_all | solution.py:518
  335.5 1135.4 %reduce-scatter.11.cloned.1.call-start = ((), (), s32[]{:S(2)}) async-start(), calls=%async_computation.12 | async-start | bytes 5990400
  585.3 76.0 %copy-start.95 = (f32[1024]{0:T(1024)S(1)}, f32[1024]{0:T(1024)}, u32[]{:S(2)}) copy-start(f32[1024]{0:T(1024)} %copy-done.94) | copy-start | bytes 12292
  714.7 55.0 %copy-start.35 = (bf16[4,128,640]{2,1,0:T(8,128)(2,1)S(1)}, bf16[4,128,640]{2,1,0:T(8,128)(2,1)}, u32[]{:S(2)}) copy-start(bf16[4,128,640]{2,1,0:T(8,128)(2,1)} %gather_ctx.5) | copy-start | bytes 1966084
  1301.9 185.9 %reduce-scatter.7.cloned.1.call-start = ((), (), s32[]{:S(2)}) async-start(), calls=%async_computation.8 | async-start | bytes 4608000 | tf_op jit(solution)/shard_map/reduce_scatter | solution.py:796
  1413.1 124.2 %reduce-scatter.9.cloned.1.call-start = ((), (), s32[]{:S(2)}) async-start(), calls=%async_computation.10 | async-start | bytes 5632000 | tf_op jit(solution)/shard_map/reduce_scatter | solution.py:796
  1451.6 227.2 %all-reduce.12.cloned.1.call-start = ((), (), s32[]{:S(2)}) async-start(), calls=%async_computation.13 | async-start | bytes 9056256 | tf_op jit(solution)/shard_map/psum | solution.py:831
  1470.9 223.3 %all-gather.7.cloned.1.call-start = ((), (), s32[]{:S(2)}) async-start(), calls=%async_computation.9 | async-start | bytes 4608000 | tf_op jit(solution)/shard_map/all_gather | solution.py:801
  1521.0 197.1 %all-gather.9.cloned.1.call-start = ((), (), s32[]{:S(2)}) async-start(), calls=%async_computation.11 | async-start | bytes 5632000 | tf_op jit(solution)/shard_map/all_gather | solution.py:801
  1590.4 42.2 %copy-start.106 = (f32[128]{0:T(128)S(1)}, f32[128]{0:T(128)}, u32[]{:S(2)}) copy-start(f32[128]{0:T(128)} %get-tuple-element.1459) | copy-start | bytes 1540
  1590.4 42.2 %copy-start.17 = (bf16[1,128,1600]{2,1,0:T(8,128)(2,1)S(1)}, bf16[1,128,1600]{2,1,0:T(8,128)(2,1)}, u32[]{:S(2)}) copy-start(bf16[1,128,1600]{2,1,0:T(8,128)(2,1)} %copy.598) | copy-start | bytes 1228804
  1590.4 43.7 %copy-start.20 = (f32[128,1600]{1,0:T(8,128)S(1)}, f32[128,1600]{1,0:T(8,128)}, u32[]{:S(2)}) copy-start(f32[128,1600]{1,0:T(8,128)} %copy-done.19) | copy-start | bytes 2457604
  (108 other events, 872.2 us)
Sparse Core Ops, SparseCore 0:
  50.2 152.6 all-gather.4
  1302.0 141.9 reduce-scatter.10
  1447.3 40.4 reduce-scatter.6
  1490.8 46.4 reduce-scatter.8
  1541.2 91.9 all-reduce.11
  1635.2 31.5 all-gather.6
  1668.5 36.2 all-gather.8

commit v2 on v0

v2 whole, which is shorter than its diff:
```python
import functools
import math

import jax
import jax.numpy as jnp
from jax import lax
from jax.experimental import pallas as pl
from jax.experimental.pallas import tpu as pltpu
from jax.sharding import PartitionSpec as P

H = 25
KV = 5
HD = 64
INNER = 3200
NS = 16
RANK = 100
CONV = 4

EPS = 1e-06
score_scale = 0.125
MESH = pl.DeviceIdType.MESH
ANY = pl.BlockSpec(memory_space=pl.ANY)
VM = pl.BlockSpec(memory_space=pltpu.VMEM)
DMA = pltpu.SemaphoreType.DMA
f32 = jnp.float32
bf16 = jnp.bfloat16


def params(cid, vmem=None):
    return pltpu.CompilerParams(collective_id=cid, has_side_effects=True, vmem_limit_bytes=vmem)


def rcopy(src, dst, ssem, rsem, dev):
    return pltpu.make_async_remote_copy(
        src_ref=src, dst_ref=dst, send_sem=ssem, recv_sem=rsem, device_id=dev, device_id_type=MESH
    )


def norm_forward(values, gain):
    inverse = lax.rsqrt(jnp.mean(values * values, axis=-1, keepdims=True) + EPS)
    return (values * inverse * gain, inverse)


def norm_backward(grad, values, inverse, gain):
    normed = values * inverse
    gain_grad = jnp.sum(grad * normed, axis=0)
    scaled = grad * gain
    return (
        inverse * (scaled - normed * jnp.mean(scaled * normed, axis=-1, keepdims=True)),
        gain_grad,
    )


def silu_slope(values):
    sigma = jax.nn.sigmoid(values)
    return sigma * (1.0 + values * (1.0 - sigma))


UNROLL = 8


def steps(length, body, init):
    count = UNROLL if length % UNROLL == 0 else 1

    def some(i, carry):
        for j in range(count):
            carry = body(i * count + j, carry)
        return carry

    return lax.fori_loop(0, length // count, some, init)


def turn(refs, streams):
    return [ref.reshape(streams * ref.shape[-2], ref.shape[-1]) for ref in refs]


def spread(wr, at, out, first, streams, length):
    def body(o, carry):
        values = wr[pl.ds(o, streams, stride=length), :]
        for n in range(NS):
            out[o, n] = jnp.broadcast_to(values[:, first + n : first + n + 1], (streams, 128))
        return carry

    steps(length, body, 0)


def rows_of(ref, o, streams, length):
    return ref[pl.ds(o, streams, stride=length), :]


def scan_ends(dt, x, wr, rate2):
    everyone, _, length, chan = dt.shape
    streams = math.gcd(everyone, 8)

    def kernel(dt_ref, x_ref, wr_ref, rate_ref, o_ref, wb):
        dt_ref, x_ref, wr_ref = turn((dt_ref, x_ref, wr_ref), streams)

        @pl.when(pl.program_id(2) == 0)
        def _():
            spread(wr_ref, None, wb, 0, streams, length)

        rates = [rate_ref[n : n + 1, :] for n in range(NS)]

        def body(o, carry):
            total, states = carry
            step = rows_of(dt_ref, o, streams, length)
            pushed = step * rows_of(x_ref, o, streams, length)
            states = tuple(
                jnp.exp2(step * rates[n]) * states[n] + wb[o, n] * pushed for n in range(NS)
            )
            return (total + step, states)

        zero = jnp.zeros((streams, 128), f32)
        total, states = steps(length, body, (zero, (zero,) * NS))
        for n in range(NS):
            o_ref[n] = states[n].astype(bf16)
        o_ref[NS] = total.astype(bf16)

    tok = pl.BlockSpec((streams, None, length, 128), lambda b, g, c: (g, b, 0, c))
    return pl.pallas_call(
        kernel,
        grid=(2, everyone // streams, chan // 128),
        in_specs=[
            tok,
            tok,
            pl.BlockSpec((streams, None, length, 2 * NS), lambda b, g, c: (g, b, 0, 0)),
            pl.BlockSpec((NS, 128), lambda b, g, c: (0, c)),
        ],
        out_specs=pl.BlockSpec((None, NS + 1, streams, 128), lambda b, g, c: (b, 0, g, c)),
        out_shape=jax.ShapeDtypeStruct((2, NS + 1, everyone, chan), bf16),
        scratch_shapes=[pltpu.VMEM((length, NS, streams, 128), f32)],
        compiler_params=pltpu.CompilerParams(vmem_limit_bytes=60 << 20),
        name="scan_ends",
    )(dt, x, wr, rate2)


def scan_forward(order, dt, x, wr, rate2, ends):
    everyone, _, length, chan = dt.shape
    streams = math.gcd(everyone, 8)
    blocks = ends.shape[0]

    def kernel(order_ref, dt_ref, x_ref, wr_ref, rate_ref, ends_ref, y_ref, s_ref, wb, rb):
        dt_ref, x_ref, wr_ref = turn((dt_ref, x_ref, wr_ref), streams)
        y_ref = y_ref.reshape(streams * length, 128)
        blk = pl.program_id(0)

        @pl.when(pl.program_id(2) == 0)
        def _():
            spread(wr_ref, None, wb, 0, streams, length)
            spread(wr_ref, None, rb, NS, streams, length)

        rates = [rate_ref[n : n + 1, :] for n in range(NS)]

        def link(b, states):
            at = order_ref[b]
            total = ends_ref[at, NS].astype(f32)
            return tuple(
                jnp.exp2(total * rates[n]) * states[n] + ends_ref[at, n].astype(f32)
                for n in range(NS)
            )

        zero = jnp.zeros((streams, 128), f32)
        states = lax.fori_loop(0, order_ref[blocks + blk], link, (zero,) * NS)
        for n in range(NS):
            s_ref[n] = states[n]

        def body(o, states):
            step = rows_of(dt_ref, o, streams, length)
            pushed = step * rows_of(x_ref, o, streams, length)
            states = tuple(
                jnp.exp2(step * rates[n]) * states[n] + wb[o, n] * pushed for n in range(NS)
            )
            total = [rb[o, n] * states[n] for n in range(NS)]
            while len(total) > 1:
                total = [total[i] + total[i + 1] for i in range(0, len(total), 2)]
            y_ref[pl.ds(o, streams, stride=length), :] = total[0]
            return states

        steps(length, body, states)

    tok = pl.BlockSpec((streams, None, length, 128), lambda b, g, c, *_: (g, b, 0, c))
    return pl.pallas_call(
        kernel,
        grid_spec=pltpu.PrefetchScalarGridSpec(
            num_scalar_prefetch=1,
            grid=(2, everyone // streams, chan // 128),
            in_specs=[
                tok,
                tok,
                pl.BlockSpec((streams, None, length, 2 * NS), lambda b, g, c, *_: (g, b, 0, 0)),
                pl.BlockSpec((NS, 128), lambda b, g, c, *_: (0, c)),
                pl.BlockSpec((blocks, NS + 1, streams, 128), lambda b, g, c, *_: (0, 0, g, c)),
            ],
            out_specs=[
                tok,
                pl.BlockSpec((None, NS, streams, 128), lambda b, g, c, *_: (b, 0, g, c)),
            ],
            scratch_shapes=[pltpu.VMEM((length, NS, streams, 128), f32)] * 2,
        ),
        out_shape=[
            jax.ShapeDtypeStruct(dt.shape, f32),
            jax.ShapeDtypeStruct((2, NS, everyone, chan), f32),
        ],
        compiler_params=pltpu.CompilerParams(vmem_limit_bytes=60 << 20),
        name="scan_forward",
    )(order, dt, x, wr, rate2, ends)


def scan_backs(dt, g, wr, rate2):
    everyone, _, length, chan = dt.shape
    streams = math.gcd(everyone, 8)

    def kernel(dt_ref, g_ref, wr_ref, rate_ref, o_ref, rb):
        dt_ref, g_ref, wr_ref = turn((dt_ref, g_ref, wr_ref), streams)

        @pl.when(pl.program_id(2) == 0)
        def _():
            spread(wr_ref, None, rb, NS, streams, length)

        rates = [rate_ref[n : n + 1, :] for n in range(NS)]

        def body(i, carries):
            o = length - 1 - i
            step = rows_of(dt_ref, o, streams, length)
            grad = rows_of(g_ref, o, streams, length)
            return tuple(
                jnp.exp2(step * rates[n]) * (carries[n] + rb[o, n] * grad) for n in range(NS)
            )

        zero = jnp.zeros((streams, 128), f32)
        carries = steps(length, body, (zero,) * NS)
        for n in range(NS):
            o_ref[n] = carries[n].astype(bf16)

    tok = pl.BlockSpec((streams, None, length, 128), lambda b, g, c: (g, b, 0, c))
    return pl.pallas_call(
        kernel,
        grid=(2, everyone // streams, chan // 128),
        in_specs=[
            tok,
            tok,
            pl.BlockSpec((streams, None, length, 2 * NS), lambda b, g, c: (g, b, 0, 0)),
            pl.BlockSpec((NS, 128), lambda b, g, c: (0, c)),
        ],
        out_specs=pl.BlockSpec((None, NS, streams, 128), lambda b, g, c: (b, 0, g, c)),
        out_shape=jax.ShapeDtypeStruct((2, NS, everyone, chan), bf16),
        scratch_shapes=[pltpu.VMEM((length, NS, streams, 128), f32)],
        compiler_params=pltpu.CompilerParams(vmem_limit_bytes=60 << 20),
        name="scan_backs",
    )(dt, g, wr, rate2)


def scan_backward(order, dt, x, g, wr, rate2, starts, ends, backs):
    everyone, _, length, chan = dt.shape
    streams = math.gcd(everyone, 8)
    blocks = ends.shape[0]
    tiles = chan // 128

    def kernel(
        order_ref,
        dt_ref,
        x_ref,
        g_ref,
        wr_ref,
        rate_ref,
        start_ref,
        ends_ref,
        backs_ref,
        sb_ref,
        cw_ref,
        wrb_ref,
        dec_ref,
        wb,
        rb,
        kept,
        decays,
        wparts,
        rparts,
        sums,
    ):
        dt_ref, x_ref, g_ref, wr_ref = turn((dt_ref, x_ref, g_ref, wr_ref), streams)
        sb_ref, cw_ref, wrb_ref = turn((sb_ref, cw_ref, wrb_ref), streams)
        blk, tile = pl.program_id(0), pl.program_id(2)

        @pl.when(tile == 0)
        def _():
            spread(wr_ref, None, wb, 0, streams, length)
            spread(wr_ref, None, rb, NS, streams, length)
            sums[...] = jnp.zeros_like(sums)

        rates = [rate_ref[n : n + 1, :] for n in range(NS)]

        def forward(o, states):
            step = rows_of(dt_ref, o, streams, length)
            pushed = step * rows_of(x_ref, o, streams, length)
            new = []
            for n in range(NS):
                decay = jnp.exp2(step * rates[n])
                decays[o, n] = decay
                kept[o, n] = states[n]
                new.append(decay * states[n] + wb[o, n] * pushed)
            return tuple(new)

        last = steps(length, forward, tuple(start_ref[n] for n in range(NS)))
        for n in range(NS):
            kept[length, n] = last[n]

        def link(i, carries):
            at = order_ref[blocks - 1 - i]
            total = ends_ref[at, 0].astype(f32)
            return tuple(
                backs_ref[at, n].astype(f32) + jnp.exp2(total * rates[n]) * carries[n]
                for n in range(NS)
            )

        zero = jnp.zeros((streams, 128), f32)
        carries = lax.fori_loop(
            0, blocks - 1 - order_ref[blocks + blk], link, (zero,) * NS
        )
        for n in range(NS):
            dec_ref[n] = zero

        def body(i, carries):
            o = length - 1 - i
            step = rows_of(dt_ref, o, streams, length)
            value = rows_of(x_ref, o, streams, length)
            grad = rows_of(g_ref, o, streams, length)
            pushed = step * value
            slope, pulled, new = [], [], []
            at = pl.ds(pl.multiple_of(o * streams, streams), streams)
            for n in range(NS):
                full = carries[n] + rb[o, n] * grad
                moved = decays[o, n] * full
                new.append(moved)
                back = moved * kept[o, n]
                slope.append(back * rates[n])
                dec_ref[n] += back * step
                pulled.append(full * wb[o, n])
                wparts[at, n * 128 : (n + 1) * 128] = full * pushed
                rparts[at, n * 128 : (n + 1) * 128] = kept[o + 1, n] * grad
            while len(slope) > 1:
                slope = [slope[i] + slope[i + 1] for i in range(0, len(slope), 2)]
                pulled = [pulled[i] + pulled[i + 1] for i in range(0, len(pulled), 2)]
            sb_ref[pl.ds(o, streams, stride=length), :] = (
                slope[0] * 0.6931471805599453 + pulled[0] * value
            )
            cw_ref[pl.ds(o, streams, stride=length), :] = pulled[0]
            return tuple(new)

        steps(length, body, carries)
        source = lax.broadcasted_iota(jnp.int32, (NS * 128, 128), 0) // 128
        target = lax.broadcasted_iota(jnp.int32, (NS * 128, 128), 1)
        pick_w = jnp.where(source == target, 1.0, 0.0).astype(bf16)
        pick_r = jnp.where(source + NS == target, 1.0, 0.0).astype(bf16)
        sums[...] += jnp.dot(
            wparts[...].astype(bf16), pick_w, preferred_element_type=f32
        ) + jnp.dot(rparts[...].astype(bf16), pick_r, preferred_element_type=f32)

        @pl.when(tile == tiles - 1)
        def _():
            def out(o, carry):
                wrb_ref[pl.ds(o, streams, stride=length), :] = sums[
                    pl.ds(pl.multiple_of(o * streams, streams), streams), :
                ]
                return carry

            steps(length, out, 0)

    tok = pl.BlockSpec((streams, None, length, 128), lambda b, g, c, *_: (g, b, 0, c))
    state = pl.BlockSpec((None, NS, streams, 128), lambda b, g, c, *_: (b, 0, g, c))
    big = pltpu.VMEM((length, NS, streams, 128), f32)
    return pl.pallas_call(
        kernel,
        grid_spec=pltpu.PrefetchScalarGridSpec(
            num_scalar_prefetch=1,
            grid=(2, everyone // streams, tiles),
            in_specs=[
                tok,
                tok,
                tok,
                pl.BlockSpec((streams, None, length, 2 * NS), lambda b, g, c, *_: (g, b, 0, 0)),
                pl.BlockSpec((NS, 128), lambda b, g, c, *_: (0, c)),
                state,
                pl.BlockSpec((blocks, 1, streams, 128), lambda b, g, c, *_: (0, NS, g, c)),
                pl.BlockSpec((blocks, NS, streams, 128), lambda b, g, c, *_: (0, 0, g, c)),
            ],
            out_specs=[
                tok,
                tok,
                pl.BlockSpec((streams, None, length, 128), lambda b, g, c, *_: (g, b, 0, 0)),
                state,
            ],
            scratch_shapes=[
                big,
                big,
                pltpu.VMEM((length + 1, NS, streams, 128), f32),
                big,
                pltpu.VMEM((length * streams, NS * 128), f32),
                pltpu.VMEM((length * streams, NS * 128), f32),
                pltpu.VMEM((length * streams, 128), f32),
            ],
        ),
        out_shape=[
            jax.ShapeDtypeStruct(dt.shape, f32),
            jax.ShapeDtypeStruct(dt.shape, f32),
            jax.ShapeDtypeStruct((everyone, 2, length, 128), f32),
            jax.ShapeDtypeStruct((2, NS, everyone, chan), f32),
        ],
        compiler_params=pltpu.CompilerParams(vmem_limit_bytes=60 << 20),
        name="scan_backward",
    )(order, dt, x, g, wr, rate2, starts, ends, backs)


def up_to(value, step):
    return (value + step - 1) // step * step


def pack_columns(weights, cuts, offsets, total, size):
    depth = weights[0].shape[0]

    def kernel(*refs):
        o_ref = refs[-1]
        o_ref[...] = jnp.zeros_like(o_ref)
        for (which, first, cols), at in zip(cuts, offsets):
            for f in range(size):
                o_ref[f, :, at : at + cols] = refs[which][
                    :, first + f * cols : first + (f + 1) * cols
                ]

    return pl.pallas_call(
        kernel,
        out_shape=jax.ShapeDtypeStruct((size, depth, total), bf16),
        in_specs=[VM] * len(weights),
        out_specs=VM,
        compiler_params=pltpu.CompilerParams(vmem_limit_bytes=60 << 20),
        name="pack_columns",
    )(*weights)


def unpack_columns(home, cuts, offsets, shapes, quarter):
    n, size, depth, _ = home.shape

    def kernel(h_ref, *outs):
        for (which, first, cols), at in zip(cuts, offsets):
            for f in range(size):
                parts = []
                lo = at
                while lo < at + cols:
                    q, inside = divmod(lo, quarter)
                    hi = min(at + cols, (q + 1) * quarter)
                    parts.append((q, inside, hi - lo, lo - at))
                    lo = hi
                for q, inside, count, shift in parts:
                    to = first + f * cols + shift
                    outs[which][:, to : to + count] = h_ref[
                        q, f, :, inside : inside + count
                    ].astype(f32)

    return pl.pallas_call(
        kernel,
        out_shape=[jax.ShapeDtypeStruct(shape, f32) for shape in shapes],
        in_specs=[VM],
        out_specs=[VM] * len(shapes),
        compiler_params=pltpu.CompilerParams(vmem_limit_bytes=60 << 20),
        name="unpack_columns",
    )(home)


def weight_grad(x, dy, quarter):
    rows, width = x.shape
    n = dy.shape[1] // quarter

    def kernel(x_ref, y_ref, o_ref):
        o_ref[...] = lax.dot_general(
            x_ref[...], y_ref[...], (((0,), (0,)), ((), ())), preferred_element_type=f32
        ).astype(bf16)

    return pl.pallas_call(
        kernel,
        grid=(n,),
        in_specs=[
            pl.BlockSpec((rows, width), lambda q: (0, 0)),
            pl.BlockSpec((rows, quarter), lambda q: (0, q)),
        ],
        out_specs=pl.BlockSpec((None, width, quarter), lambda q: (q, 0, 0)),
        out_shape=jax.ShapeDtypeStruct((n, width, quarter), bf16),
        compiler_params=pltpu.CompilerParams(vmem_limit_bytes=60 << 20),
        name="weight_grad",
    )(x, dy)


class Job:
    def __init__(self, steps, ins, outs, scratch):
        self.steps, self.ins, self.outs, self.scratch = steps, ins, outs, scratch


class Place:
    def __init__(self, size):
        self.size, self.lanes = size, size // 2
        self.f, self.c = lax.axis_index("fsdp"), lax.axis_index("ctx")
        self.a, self.b = self.f // 2, lax.rem(self.f, 2)
        self.near = self.c + 1 - 2 * lax.rem(self.c, 2)
        self.far = lax.rem(self.c + 2, 4)
        self.other = lax.rem(self.near + 2, 4)

    def greet(self):
        bar = pltpu.get_barrier_semaphore()
        for d in range(1, self.size):
            peer = {"fsdp": lax.rem(self.f + d, self.size)}
            pl.semaphore_signal(bar, inc=1, device_id=peer, device_id_type=MESH)
        for peer in (self.near, self.far):
            pl.semaphore_signal(bar, inc=1, device_id={"ctx": peer}, device_id_type=MESH)
        pl.semaphore_wait(bar, self.size + 1)


def part(ref_list, jobs, field):
    out = []
    for job in jobs:
        count = len(getattr(job, field))
        out.append(ref_list[:count])
        ref_list = ref_list[count:]
    return out


def together(jobs, size, cid, name):
    n_in = sum(len(job.ins) for job in jobs)
    n_out = sum(len(job.outs) for job in jobs)

    def kernel(*refs):
        place = Place(size)
        place.greet()
        ins = part(refs[:n_in], jobs, "ins")
        outs = part(refs[n_in : n_in + n_out], jobs, "outs")
        scratch = part(refs[n_in + n_out :], jobs, "scratch")
        live = [job.steps(place, i, o, s) for job, i, o, s in zip(jobs, ins, outs, scratch)]
        while live:
            still = []
            for steps_ in live:
                try:
                    next(steps_)
                    still.append(steps_)
                except StopIteration:
                    pass
            live = still

    got = pl.pallas_call(
        kernel,
        out_shape=[shape for job in jobs for shape, _ in job.outs],
        in_specs=[spec for job in jobs for _, spec in job.ins],
        out_specs=[spec for job in jobs for _, spec in job.outs],
        scratch_shapes=[item for job in jobs for item in job.scratch],
        compiler_params=params(cid, 60 << 20),
        name=name,
    )(*[array for job in jobs for array, _ in job.ins])
    return part(got, jobs, "outs")


def like(shape, dtype):
    return jax.ShapeDtypeStruct(shape, dtype)


def gather_job(x, size):
    rows, cols = x.shape
    lanes = size // 2

    def run(p, ins, outs, scratch):
        (x_ref,), (o_ref,) = ins, outs
        lsem, up_s, up_r, dn_s, dn_r, px_s, px_r = scratch

        def piece(origin, b):
            return o_ref.at[pl.ds(pl.multiple_of((2 * origin + b) * rows, rows), rows)]

        def local():
            return pltpu.make_async_copy(x_ref, piece(p.a, p.b), lsem)

        def up(s):
            src = x_ref if s == 0 else piece(p.a - s, p.b)
            dev = {"fsdp": 2 * (p.a + 1) + p.b}
            return rcopy(src, piece(p.a - s, p.b), up_s.at[s], up_r.at[s], dev)

        def down(s):
            src = x_ref if s == 0 else piece(p.a + s, p.b)
            dev = {"fsdp": 2 * (p.a - 1) + p.b}
            return rcopy(src, piece(p.a + s, p.b), dn_s.at[s], dn_r.at[s], dev)

        def across(origin, src=None):
            src = piece(origin, p.b) if src is None else src
            dev = {"fsdp": 2 * p.a + 1 - p.b}
            return rcopy(src, piece(origin, p.b), px_s.at[origin], px_r.at[origin], dev)

        def came(ref, sem, dev):
            rcopy(ref, ref, sem, sem, dev).wait_recv()

        @pl.when(p.a < lanes - 1)
        def _():
            up(0).start()

        @pl.when(p.a > 0)
        def _():
            down(0).start()

        across(p.a, x_ref).start()
        local().start()
        yield
        for s in range(lanes - 1):
            @pl.when(p.a - 1 - s >= 0)
            def _():
                came(piece(p.a - 1 - s, p.b), up_r.at[s], {"fsdp": 2 * (p.a - 1) + p.b})

                @pl.when(p.a < lanes - 1)
                def _():
                    up(s + 1).start()

                across(p.a - 1 - s).start()

            @pl.when(p.a + 1 + s <= lanes - 1)
            def _():
                came(piece(p.a + 1 + s, p.b), dn_r.at[s], {"fsdp": 2 * (p.a + 1) + p.b})

                @pl.when(p.a > 0)
                def _():
                    down(s + 1).start()

                across(p.a + 1 + s).start()

            yield
        local().wait()
        for s in range(lanes - 1):
            @pl.when((p.a - s >= 0) & (p.a < lanes - 1))
            def _():
                up(s).wait_send()

            @pl.when((p.a + s <= lanes - 1) & (p.a > 0))
            def _():
                down(s).wait_send()

        for origin in range(lanes):
            across(origin).wait_send()
            came(piece(origin, 1 - p.b), px_r.at[origin], {"fsdp": 2 * p.a + 1 - p.b})

    return Job(
        run, [(x, ANY)], [(like((size * rows, cols), x.dtype), ANY)], [DMA] + [DMA((lanes,))] * 6
    )


def add_blocks(out, terms, dtype, rows):
    if rows % 16:
        total = terms[0][...].astype(f32)
        for ref in terms[1:]:
            total += ref[...].astype(f32)
        out[...] = total.astype(dtype)
        return
    step = 32 if rows % 32 == 0 else 16

    def body(i, carry):
        at = pl.ds(pl.multiple_of(i * step, step), step)
        total = terms[0][at, :].astype(f32)
        for ref in terms[1:]:
            total += ref[at, :].astype(f32)
        out[at, :] = total.astype(dtype)
        return carry

    lax.fori_loop(0, rows // step, body, 0)


def scatter_job(partial, size):
    rows, cols = partial.shape[1:]
    lanes = size // 2

    def run(p, ins, outs, scratch):
        (p_ref,), (o_ref,) = ins, outs
        xbuf, upb, dnb, up_s, up_r, dn_s, dn_r, px_s, px_r = scratch

        def across(dest):
            src = p_ref.at[2 * dest + 1 - p.b]
            dev = {"fsdp": 2 * p.a + 1 - p.b}
            return rcopy(src, xbuf.at[dest], px_s.at[dest], px_r.at[dest], dev)

        def up(dest):
            dev = {"fsdp": 2 * (p.a + 1) + p.b}
            return rcopy(xbuf.at[dest], upb.at[dest], up_s.at[dest], up_r.at[dest], dev)

        def down(dest):
            dev = {"fsdp": 2 * (p.a - 1) + p.b}
            return rcopy(xbuf.at[dest], dnb.at[dest], dn_s.at[dest], dn_r.at[dest], dev)

        def add_in(dest, extra):
            terms = [xbuf.at[dest], p_ref.at[2 * dest + p.b]]
            if extra is not None:
                terms.append(extra.at[dest])
            add_blocks(xbuf.at[dest], terms, bf16, rows)

        for d in range(lanes - 1, -1, -1):
            @pl.when(p.a + d <= lanes - 1)
            def _():
                across(p.a + d).start()

            if d > 0:
                @pl.when(p.a - d >= 0)
                def _():
                    across(p.a - d).start()

        yield
        for d in range(lanes - 1, 0, -1):
            @pl.when(p.a + d <= lanes - 1)
            def _():
                across(p.a + d).wait_recv()

                @pl.when(p.a > 0)
                def _():
                    up(p.a + d).wait_recv()
                    add_in(p.a + d, upb)

                @pl.when(p.a == 0)
                def _():
                    add_in(p.a + d, None)

                up(p.a + d).start()

            @pl.when(p.a - d >= 0)
            def _():
                across(p.a - d).wait_recv()

                @pl.when(p.a < lanes - 1)
                def _():
                    down(p.a - d).wait_recv()
                    add_in(p.a - d, dnb)

                @pl.when(p.a == lanes - 1)
                def _():
                    add_in(p.a - d, None)

                down(p.a - d).start()

            yield
        across(p.a).wait_recv()
        terms = [xbuf.at[p.a], p_ref.at[2 * p.a + p.b]]

        @pl.when(p.a == 0)
        def _():
            down(p.a).wait_recv()
            add_blocks(o_ref, terms + [dnb.at[p.a]], f32, rows)

        @pl.when(p.a == lanes - 1)
        def _():
            up(p.a).wait_recv()
            add_blocks(o_ref, terms + [upb.at[p.a]], f32, rows)

        @pl.when((p.a > 0) & (p.a < lanes - 1))
        def _():
            up(p.a).wait_recv()
            down(p.a).wait_recv()
            add_blocks(o_ref, terms + [upb.at[p.a], dnb.at[p.a]], f32, rows)

        for dest in range(lanes):
            across(dest).wait_send()

        for d in range(lanes - 1, 0, -1):
            @pl.when(p.a + d <= lanes - 1)
            def _():
                up(p.a + d).wait_send()

            @pl.when(p.a - d >= 0)
            def _():
                down(p.a - d).wait_send()

    return Job(
        run,
        [(partial, VM)],
        [(like((rows, cols), f32), VM)],
        [pltpu.VMEM((lanes, rows, cols), bf16)] * 3 + [DMA((lanes,))] * 6,
    )


def column_block(of, quarter):
    return pl.ds(pl.multiple_of(of * quarter, 128), quarter)


class Share:
    def __init__(self, p, view, count, sems):
        self.p, self.view, self.count = p, view, count
        self.fs, self.fr, self.ns, self.nr, self.hs, self.hr = sems

    def far(self, d, q):
        ref = self.view(d, q)
        return rcopy(ref, ref, self.fs.at[d], self.fr.at[d], {"ctx": self.p.far})

    def near(self, d, q):
        ref = self.view(d, q)
        return rcopy(ref, ref, self.ns.at[d], self.nr.at[d], {"ctx": self.p.near})

    def onward(self, d, q):
        ref = self.view(d, q)
        return rcopy(ref, ref, self.hs.at[d], self.hr.at[d], {"ctx": self.p.near})

    def send(self, d):
        self.far(d, self.p.c).start()
        self.near(d, self.p.c).start()

    def forward(self, d):
        self.far(d, self.p.far).wait_recv()
        self.onward(d, self.p.far).start()

    def finish(self):
        p = self.p
        for d in range(self.count):
            self.far(d, p.c).wait_send()
            self.near(d, p.c).wait_send()
            self.near(d, p.near).wait_recv()
            self.onward(d, p.far).wait_send()
            self.onward(d, p.other).wait_recv()


def share_sems(count):
    return [DMA((count,))] * 6


def move_job(packed, size, per_device=True):
    depth, total = packed.shape[-2:]
    quarter = total // 4

    def run(p, ins, outs, scratch):
        (p_ref,), (w_ref,) = ins, outs
        lsem, ws, wr = scratch[:3]

        def source(to):
            block = column_block(p.c, quarter)
            return p_ref.at[to, :, block] if per_device else p_ref.at[:, block]

        def view(d, q):
            return w_ref.at[lax.rem(p.f - d + size, size), :, column_block(q, quarter)]

        def local():
            return pltpu.make_async_copy(source(p.f), view(0, p.c), lsem)

        def move(d):
            to = lax.rem(p.f + d, size)
            return rcopy(source(to), view(0, p.c), ws.at[d], wr.at[d], {"fsdp": to})

        def came(d):
            ref = view(d, p.c)
            rcopy(ref, ref, ws.at[d], wr.at[d], {"fsdp": lax.rem(p.f + d, size)}).wait_recv()

        share = Share(p, view, size, scratch[3:])
        local().start()
        for d in range(1, size):
            move(d).start()
        yield
        local().wait()
        share.send(0)
        for d in range(1, size):
            came(d)
            share.send(d)
            if d % 2 == 0:
                yield
        for d in range(size):
            share.forward(d)
            if d % 4 == 3:
                yield
        share.finish()
        for d in range(1, size):
            move(d).wait_send()

    return Job(
        run,
        [(packed, ANY)],
        [(like((size, depth, total), packed.dtype), ANY)],
        [DMA, DMA((size,)), DMA((size,))] + share_sems(size),
    )


def spread_job(x, size):
    def run(p, ins, outs, scratch):
        (x_ref,), (o_ref,) = ins, outs
        lsem, ss, rs = scratch

        def copy(d):
            to = {"fsdp": lax.rem(p.f + d, size)}
            return rcopy(x_ref, o_ref.at[p.f], ss.at[d], rs.at[d], to)

        def local():
            return pltpu.make_async_copy(x_ref, o_ref.at[p.f], lsem)

        local().start()
        for d in range(1, size):
            copy(d).start()
        yield
        local().wait()
        for d in range(1, size):
            copy(d).wait()

    return Job(
        run,
        [(x, ANY)],
        [(like((size,) + x.shape, x.dtype), ANY)],
        [DMA, DMA((size,)), DMA((size,))],
    )


def exchange_job(x, size):
    def run(p, ins, outs, scratch):
        (x_ref,), (o_ref,) = ins, outs
        lsem, ss, rs = scratch

        def copy(d):
            to = lax.rem(p.f + d, size)
            return rcopy(x_ref.at[to], o_ref.at[p.f], ss.at[d], rs.at[d], {"fsdp": to})

        def local():
            return pltpu.make_async_copy(x_ref.at[p.f], o_ref.at[p.f], lsem)

        for d in range(1, size):
            copy(d).start()
        local().start()
        yield
        local().wait()
        for d in range(1, size):
            copy(d).wait()

    return Job(
        run, [(x, ANY)], [(like(x.shape, x.dtype), ANY)], [DMA, DMA((size,)), DMA((size,))]
    )


def ctx_gather_job(x):
    def run(p, ins, outs, scratch):
        (x_ref,), (o_ref,) = ins, outs
        share = Share(p, lambda d, q: o_ref.at[q], 1, scratch[1:])

        def local():
            return pltpu.make_async_copy(x_ref, o_ref.at[p.c], scratch[0])

        def first(to, ss, rs):
            return rcopy(x_ref, o_ref.at[p.c], ss.at[0], rs.at[0], {"ctx": to})

        first(p.far, share.fs, share.fr).start()
        first(p.near, share.ns, share.nr).start()
        local().start()
        yield
        share.forward(0)
        yield
        local().wait()
        share.finish()

    return Job(
        run, [(x, ANY)], [(like((4,) + x.shape, x.dtype), ANY)], [DMA] + share_sems(1)
    )


class Halve:
    def __init__(self, p, source, bufs, sems):
        self.p, self.source = p, source
        self.own, self.got, self.away, self.total = bufs
        self.ls, self.ns, self.nr, self.fs, self.fr = sems
        self.count, self.rows = self.total.shape[:2]

    def local(self, i):
        q = self.p.c if i == 0 else self.p.far
        return pltpu.make_async_copy(self.source(q), self.own.at[i], self.ls.at[i])

    def to_near(self, i):
        q = self.p.near if i == 0 else self.p.other
        return rcopy(
            self.source(q), self.got.at[i], self.ns.at[i], self.nr.at[i], {"ctx": self.p.near}
        )

    def to_far(self, j):
        return rcopy(
            self.own.at[1, j], self.away.at[j], self.fs.at[j], self.fr.at[j], {"ctx": self.p.far}
        )

    def start(self):
        for i in (1, 0):
            self.to_near(i).start()
            self.local(i).start()

    def send(self):
        self.local(1).wait()
        self.to_near(1).wait_recv()
        for j in range(self.count):
            own = self.own.at[1, j]
            add_blocks(own, [own, self.got.at[1, j]], bf16, self.rows)
            self.to_far(j).start()

    def mine(self):
        self.local(0).wait()
        self.to_near(0).wait_recv()

    def block(self, j):
        self.to_far(j).wait_recv()
        add_blocks(
            self.total.at[j],
            [self.own.at[0, j], self.got.at[0, j], self.away.at[j]],
            bf16,
            self.rows,
        )

    def finish(self):
        for i in range(2):
            self.to_near(i).wait_send()
        for j in range(self.count):
            self.to_far(j).wait_send()


def halve_scratch(count, rows, cols, total=True):
    return [
        pltpu.VMEM((2, count, rows, cols), bf16),
        pltpu.VMEM((2, count, rows, cols), bf16),
        pltpu.VMEM((count, rows, cols), bf16),
    ] + [pltpu.VMEM((count, rows, cols), bf16)] * total + [
        DMA((2,)),
        DMA((2,)),
        DMA((2,)),
        DMA((count,)),
        DMA((count,)),
    ]


def halve_job(x, columns=True):
    n, rows, cols = x.shape
    shape = (n, rows, cols // 4) if columns else (n // 4, rows, cols)

    def run(p, ins, outs, scratch):
        (x_ref,), (o_ref,) = ins, outs

        def source(q):
            if columns:
                return x_ref.at[:, :, column_block(q, shape[2])]
            return x_ref.at[pl.ds(q * shape[0], shape[0])]

        halve = Halve(p, source, list(scratch[:3]) + [o_ref], scratch[3:])
        halve.start()
        yield
        halve.send()
        yield
        halve.mine()
        for j in range(shape[0]):
            halve.block(j)
            if j % 2 == 1:
                yield
        halve.finish()

    return Job(run, [(x, ANY)], [(like(shape, bf16), VM)], halve_scratch(*shape, total=False))


def home_job(wgrad, size):
    _, depth, total = wgrad.shape
    quarter = total // 4

    def run(p, ins, outs, scratch):
        (w_ref,), (h_ref,) = ins, outs
        halve = Halve(
            p, lambda q: w_ref.at[:, :, column_block(q, quarter)], scratch[:4], scratch[4:9]
        )
        lsem, ws, wr = scratch[9:12]

        def view(d, q):
            return h_ref.at[lax.rem(p.f - d + size, size), :, column_block(q, quarter)]

        def local():
            return pltpu.make_async_copy(halve.total.at[p.f], view(0, p.c), lsem)

        def move(d):
            to = lax.rem(p.f + d, size)
            return rcopy(halve.total.at[to], view(0, p.c), ws.at[d], wr.at[d], {"fsdp": to})

        def came(d):
            ref = view(d, p.c)
            rcopy(ref, ref, ws.at[d], wr.at[d], {"fsdp": lax.rem(p.f + d, size)}).wait_recv()

        share = Share(p, view, size, scratch[12:])
        halve.start()
        yield
        halve.send()
        yield
        halve.mine()
        for j in range(size):
            halve.block(j)
            if j % 2 == 1:
                yield
        local().start()
        for d in range(1, size):
            move(d).start()
        yield
        local().wait()
        share.send(0)
        for d in range(1, size):
            came(d)
            share.send(d)
            if d % 2 == 0:
                yield
        for d in range(size):
            share.forward(d)
            if d % 4 == 3:
                yield
        share.finish()
        halve.finish()
        for d in range(1, size):
            move(d).wait_send()

    return Job(
        run,
        [(wgrad, ANY)],
        [(like((size, depth, total), bf16), ANY)],
        halve_scratch(size, depth, quarter)
        + [DMA, DMA((size,)), DMA((size,))]
        + share_sems(size),
    )


def ctx_sum_job(x):
    rows, cols = x.shape[0] // 4, x.shape[1]
    x = x.reshape(4, rows, cols)

    def run(p, ins, outs, scratch):
        (x_ref,), (o_ref,) = ins, outs
        halve = Halve(p, lambda q: x_ref.at[pl.ds(q, 1)], scratch[:4], scratch[4:9])
        share = Share(p, lambda d, q: o_ref.at[q], 1, scratch[10:])
        halve.start()
        yield
        halve.send()
        yield
        halve.mine()
        halve.block(0)
        local = pltpu.make_async_copy(halve.total.at[0], o_ref.at[p.c], scratch[9])
        local.start()
        local.wait()
        share.send(0)
        yield
        share.forward(0)
        yield
        share.finish()
        halve.finish()

    return Job(
        run,
        [(x, ANY)],
        [(like((4, rows, cols), bf16), ANY)],
        halve_scratch(1, rows, cols) + [DMA] + share_sems(1),
    )


def sum_job(partial, size):
    rows, tokens = partial.shape[0], partial.shape[1] // size

    def run(p, ins, outs, scratch):
        (p_ref,), (o_ref,) = ins, outs
        buf, ss, rs, gs, gr = scratch

        def at(i):
            return pl.ds(pl.multiple_of(i * tokens, 128), tokens)

        def first(d):
            to = lax.rem(p.f + d, size)
            return rcopy(p_ref.at[:, at(to)], buf.at[d], ss.at[d], rs.at[d], {"fsdp": to})

        def second(d):
            to = lax.rem(p.f + d, size)
            ref = o_ref.at[:, at(p.f)]
            return rcopy(ref, ref, gs.at[d], gr.at[d], {"fsdp": to})

        def came(d):
            ref = o_ref.at[:, at(lax.rem(p.f - d + size, size))]
            rcopy(ref, ref, gs.at[d], gr.at[d], {"fsdp": lax.rem(p.f + d, size)}).wait_recv()

        for d in range(1, size):
            first(d).start()
        yield
        total = p_ref[:, at(p.f)].astype(f32)
        for d in range(1, size):
            first(d).wait_recv()
            total += buf[d].astype(f32)
        o_ref[:, at(p.f)] = total.astype(bf16)
        for d in range(1, size):
            second(d).start()
        yield
        for d in range(1, size):
            came(d)
        for d in range(1, size):
            first(d).wait_send()
            second(d).wait_send()

    return Job(
        run,
        [(partial, VM)],
        [(like(partial.shape, bf16), VM)],
        [pltpu.VMEM((size, rows, tokens), bf16)] + [DMA((size,))] * 4,
    )


def all_sum_job(x, size):
    rows, cols = x.shape[1:]

    def run(p, ins, outs, scratch):
        (x_ref,), (o_ref,) = ins, outs
        buf, mid, far, ss, rs, ts, tr = scratch

        def copy(d):
            to = lax.rem(p.f + d, size)
            return rcopy(x_ref.at[to], buf.at[d], ss.at[d], rs.at[d], {"fsdp": to})

        def swap(i, to):
            return rcopy(mid.at[i], far.at[i], ts.at[i], tr.at[i], {"ctx": to})

        for d in range(1, size):
            copy(d).start()
        yield
        total = x_ref[p.f].astype(f32)
        for d in range(1, size):
            copy(d).wait_recv()
            total += buf[d].astype(f32)
        mid[0] = total.astype(bf16)
        swap(0, p.near).start()
        yield
        swap(0, p.near).wait_recv()
        mid[1] = (mid[0].astype(f32) + far[0].astype(f32)).astype(bf16)
        swap(1, p.far).start()
        yield
        swap(1, p.far).wait_recv()
        o_ref[...] = mid[1].astype(f32) + far[1].astype(f32)
        for d in range(1, size):
            copy(d).wait_send()
        swap(0, p.near).wait_send()
        swap(1, p.far).wait_send()

    return Job(
        run,
        [(x, VM)],
        [(like((rows, cols), f32), VM)],
        [pltpu.VMEM((size, rows, cols), bf16)]
        + [pltpu.VMEM((2, rows, cols), bf16)] * 2
        + [DMA((size,)), DMA((size,)), DMA((2,)), DMA((2,))],
    )


def column_grads(x, dy):
    return jnp.einsum("ld,lk->dk", x, dy, preferred_element_type=f32).astype(bf16)


def on_device(
    layer_in,
    out_grad,
    doc_lengths,
    block_deal,
    norm_gains,
    query_weight,
    keyval_weight,
    attn_proj,
    mamba_in,
    conv_taps,
    conv_bias,
    step_bias,
    skip_gain,
    decay_log,
    select_proj,
    step_proj,
    mamba_proj,
    gate_weight,
    up_weight,
    down_weight,
):
    size = lax.axis_size("fsdp")
    n_ctx = lax.axis_size("ctx")
    rows = layer_in.shape[1]
    half_rows = rows // 2
    width = layer_in.shape[2]
    blocks_all = 2 * n_ctx
    group = H // KV
    chan = INNER // size
    q_cols, kv_cols = H * HD // size, 2 * KV * HD // size
    ff_cols = gate_weight.shape[1] // size
    rows_all = size * rows
    ctx_place = lax.axis_index("ctx")
    deal_flat = block_deal.reshape(-1)
    my_blocks = lax.dynamic_slice_in_dim(block_deal, ctx_place, 1, 0)[0]
    offsets = jnp.arange(half_rows, dtype=jnp.int32)
    my_places = (my_blocks[:, None] * half_rows + offsets[None, :]).reshape(-1)
    key_places = (deal_flat[:, None] * half_rows + offsets[None, :]).reshape(-1)
    lengths = doc_lengths[0]
    starts = jnp.cumsum(lengths) - lengths

    def segment(places):
        return jnp.sum((places[:, None] >= starts[None, :]).astype(jnp.int32), axis=1)

    allowed = (key_places[None, :] <= my_places[:, None]) & (
        segment(key_places)[None, :] == segment(my_places)[:, None]
    )
    inverse = jnp.argsort(deal_flat)

    depth = query_weight.shape[0]
    chan_up, q_up, kv_up = up_to(chan, 128), up_to(q_cols, 128), up_to(kv_cols, 128)
    ff_up = up_to(ff_cols, 128)
    first_cuts = ((0, 0, q_cols), (1, 0, kv_cols), (2, 0, chan), (2, INNER, chan))
    first_at = (0, q_up, q_up + kv_up, q_up + kv_up + chan_up)
    first_total = up_to(q_up + kv_up + 2 * chan_up, 128 * n_ctx)
    ffn_cuts = ((0, 0, ff_cols), (1, 0, ff_cols))
    ffn_at = (0, ff_up)
    ffn_total = up_to(2 * ff_up, 128 * n_ctx)
    first_packed = pack_columns(
        (query_weight, keyval_weight, mamba_in), first_cuts, first_at, first_total, size
    )
    ffn_packed = pack_columns((gate_weight, up_weight), ffn_cuts, ffn_at, ffn_total, size)
    (stream_all,), (gain_all,), (first_mat,) = together(
        [gather_job(layer_in[0], size), spread_job(norm_gains, size), move_job(first_packed, size)],
        size,
        0,
        "start",
    )
    gain_float = jnp.moveaxis(gain_all, 0, 1).reshape(4, width).astype(f32)
    first_mat = first_mat.reshape(width, first_total)
    qkv_up = q_up + kv_up
    qkv_mat = first_mat[:, :qkv_up]
    entry_mat = first_mat[:, qkv_up : qkv_up + 2 * chan_up]
    ffn_quarter = ffn_total // n_ctx
    attn_wide = up_to(width, 128 * n_ctx)
    attn_packed = jnp.pad(attn_proj, ((0, 0), (0, attn_wide - width)))
    down_mat = jnp.pad(down_weight, ((0, ff_up - ff_cols), (0, 0)))
    more = chan_up - chan
    taps_mat = jnp.pad(conv_taps, ((0, 0), (0, more)))
    mamba_mat = jnp.pad(mamba_proj, ((0, more), (0, 0)))
    select_mat = jnp.pad(select_proj, ((0, more), (0, 0)))
    step_mat = jnp.pad(step_proj, ((0, 0), (0, more)))
    rate = -jnp.exp(jnp.pad(decay_log, ((0, 0), (0, more))).astype(f32))
    rate2 = rate * 1.4426950408889634
    shift_float, step_shift, skip_float = (
        jnp.pad(item, (0, more)).astype(f32) for item in (conv_bias, step_bias, skip_gain)
    )

    stream = layer_in[0].astype(f32)
    _, inv_in = norm_forward(stream, gain_float[0])
    normed_all, inv_all = norm_forward(stream_all.astype(f32), gain_float[0])
    normed_all = normed_all.astype(bf16)

    qkv = jnp.dot(normed_all, qkv_mat, preferred_element_type=f32).astype(bf16)
    ((qkv,),) = together([exchange_job(qkv.reshape(size, rows, -1), size)], size, 1, "qkv")
    queries = qkv[:, :, :q_cols].transpose(1, 0, 2).reshape(rows, H * HD)
    keyvals = qkv[:, :, q_up : q_up + kv_cols].transpose(1, 0, 2).reshape(rows, 2 * KV * HD)
    entry = jnp.dot(normed_all, entry_mat, preferred_element_type=f32)
    chan = chan_up
    mixer_in = entry[:, :chan].astype(bf16)
    gate_side = entry[:, chan:]
    mixer_blocks = mixer_in.reshape(size, 2, half_rows, chan)
    tails = mixer_blocks[:, :, half_rows - (CONV - 1) :]
    (keyvals_all,), (tails_all,) = together(
        [ctx_gather_job(keyvals), ctx_gather_job(tails.reshape(-1, chan))], size, 2, "edges"
    )
    keyvals_all = keyvals_all.reshape(n_ctx * rows, 2 * KV * HD)
    tails_all = tails_all.reshape(n_ctx, size, 2, CONV - 1, chan)

    def in_deal_order(values):
        return jnp.moveaxis(values, 2, 1).reshape((blocks_all,) + (size,) + values.shape[3:])

    def of_blocks(values, index):
        return jnp.moveaxis(jnp.take(values, index, axis=0), 0, 1)

    before_index = inverse[jnp.maximum(my_blocks - 1, 0)]
    has_before = my_blocks > 0
    prior_tail = jnp.where(
        has_before[None, :, None, None],
        of_blocks(in_deal_order(tails_all), before_index),
        jnp.zeros_like(tails),
    )
    padded = jnp.concatenate([prior_tail, mixer_blocks], axis=2).astype(f32)
    taps_float = taps_mat.astype(f32)
    conv_blocks_out = shift_float + sum(
        taps_float[offset] * padded[:, :, offset : offset + half_rows] for offset in range(CONV)
    )
    conv_out = conv_blocks_out.reshape(rows_all, chan)
    signal = jax.nn.silu(conv_out).astype(bf16)
    signal_float = signal.astype(f32)
    selected_part = jnp.einsum(
        "ik,li->kl", select_mat, signal, preferred_element_type=f32
    ).astype(bf16)
    ((selected,),) = together([sum_job(selected_part, size)], size, 3, "select")
    step_low = selected[:RANK].T
    write_read = selected[RANK:].astype(f32).T.reshape(size, 2, half_rows, 2 * NS)
    step_pre = jnp.dot(step_low, step_mat, preferred_element_type=f32) + step_shift
    step_sizes = jax.nn.softplus(step_pre)
    block_steps = step_sizes.reshape(size, 2, half_rows, chan)
    block_inputs = signal_float.reshape(size, 2, half_rows, chan)
    order = jnp.concatenate([inverse, my_blocks]).astype(jnp.int32)
    local_end = scan_ends(block_steps, block_inputs, write_read, rate2)
    (ends_all,), (grads_all,), (ffn_mat,), (attn_mat,) = together(
        [
            ctx_gather_job(local_end.reshape(-1, chan)),
            gather_job(out_grad[0], size),
            move_job(ffn_packed, size),
            move_job(attn_packed, size, False),
        ],
        size,
        4,
        "ends",
    )
    ffn_mat = ffn_mat.reshape(width, ffn_total)
    gate_mat, up_mat = ffn_mat[:, :ff_up], ffn_mat[:, ff_up : 2 * ff_up]
    attn_mat = attn_mat.reshape(width, attn_wide)[:, :width]
    ends_all = ends_all.reshape(blocks_all, NS + 1, size, chan)
    scan_blocks, start_state = scan_forward(
        order, block_steps, block_inputs, write_read, rate2, ends_all
    )
    scanned = scan_blocks.reshape(rows_all, chan) + skip_float * signal_float
    gate_act = jax.nn.silu(gate_side)
    mamba_rows = (scanned * gate_act).astype(bf16)
    mamba_part = jnp.dot(mamba_rows, mamba_mat, preferred_element_type=f32).astype(bf16)
    ((mamba_out,),) = together(
        [scatter_job(mamba_part.reshape(size, rows, width), size)], size, 5, "mamba_sum"
    )
    query_groups = queries.reshape(rows, KV, group, HD).transpose(1, 0, 2, 3)
    key_groups = keyvals_all[:, : KV * HD].reshape(-1, KV, HD).transpose(1, 0, 2)
    value_groups = keyvals_all[:, KV * HD :].reshape(-1, KV, HD).transpose(1, 0, 2)

    def attend(parts):
        query_part, key_part, value_part = parts
        scores = (
            jnp.einsum("lgd,sd->gls", query_part, key_part, preferred_element_type=f32)
            * score_scale
        )
        scores = jnp.where(allowed[None], scores, -1e30)
        largest = jnp.max(scores, axis=-1, keepdims=True)
        expo = jnp.exp(scores - largest)
        total = jnp.sum(expo, axis=-1, keepdims=True)
        probs = (expo / total).astype(bf16)
        output = jnp.einsum("gls,sd->lgd", probs, value_part, preferred_element_type=f32)
        return (output, largest + jnp.log(total))

    attn_groups, log_totals = lax.map(attend, (query_groups, key_groups, value_groups))
    attn_rows = attn_groups.transpose(1, 0, 2, 3).reshape(rows, H * HD).astype(bf16)
    attn_out = jnp.dot(attn_rows, attn_mat, preferred_element_type=f32)
    attn_normed, inv_attn = norm_forward(attn_out, gain_float[1])

    mamba_normed, inv_mamba = norm_forward(mamba_out, gain_float[2])
    middle = stream + 0.5 * (attn_normed + mamba_normed)
    ffn_normed, inv_ffn = norm_forward(middle, gain_float[3])
    ((ffn_low,),) = together(
        [gather_job(ffn_normed.astype(bf16), size)], size, 6, "ffn_rows"
    )
    gate_pre = jnp.dot(ffn_low, gate_mat, preferred_element_type=f32)
    up_pre = jnp.dot(ffn_low, up_mat, preferred_element_type=f32)
    hidden = (jax.nn.silu(gate_pre) * up_pre).astype(bf16)
    down_part = jnp.dot(hidden, down_mat, preferred_element_type=f32).astype(bf16)
    down_wgrad = jnp.einsum("lf,ld->fd", hidden, grads_all, preferred_element_type=f32)
    hidden_back = jnp.einsum("ld,fd->lf", grads_all, down_mat, preferred_element_type=f32)
    gate_back = (hidden_back * up_pre * silu_slope(gate_pre)).astype(bf16)
    up_back = (hidden_back * jax.nn.silu(gate_pre)).astype(bf16)
    ffn_wgrad = column_grads(ffn_low, jnp.concatenate([gate_back, up_back], axis=1))
    ffn_back_part = jnp.einsum(
        "lf,df->ld", gate_back, gate_mat, preferred_element_type=f32
    ) + jnp.einsum("lf,df->ld", up_back, up_mat, preferred_element_type=f32)
    (ffn_back,), (ffn_home,) = together(
        [
            scatter_job(ffn_back_part.astype(bf16).reshape(size, rows, width), size),
            home_job(ffn_wgrad.reshape(size, depth, -1), size),
        ],
        size,
        7,
        "ffn_sum",
    )
    middle_part, ffn_gain_grad = norm_backward(ffn_back, middle, inv_ffn, gain_float[3])
    middle_back = out_grad[0].astype(f32) + middle_part
    branch_back = 0.5 * middle_back
    attn_part, attn_gain_grad = norm_backward(branch_back, attn_out, inv_attn, gain_float[1])
    mamba_part_back, mamba_gain_grad = norm_backward(
        branch_back, mamba_out, inv_mamba, gain_float[2]
    )
    attn_back = attn_part.astype(bf16)
    attn_wgrad = jnp.einsum("lh,ld->hd", attn_rows, attn_back, preferred_element_type=f32)
    attn_wgrad = jnp.pad(attn_wgrad.astype(bf16), ((0, 0), (0, attn_wide - width)))
    (mamba_back,), (down_out,), (down_share,), (attn_quarter,) = together(
        [
            gather_job(mamba_part_back.astype(bf16), size),
            scatter_job(down_part.reshape(size, rows, width), size),
            ctx_sum_job(down_wgrad.astype(bf16)),
            halve_job(attn_wgrad.reshape(size, depth, attn_wide)),
        ],
        size,
        8,
        "mamba_rows",
    )
    result = middle + down_out
    rows_back = jnp.einsum("ld,hd->lh", attn_back, attn_mat, preferred_element_type=f32).astype(
        bf16
    )
    mamba_wgrad = jnp.einsum("li,ld->id", mamba_rows, mamba_back, preferred_element_type=f32)
    mrows_back = jnp.einsum("ld,id->li", mamba_back, mamba_mat, preferred_element_type=f32)
    scan_back = mrows_back * gate_act
    side_back = mrows_back * scanned * silu_slope(gate_side)
    skip_grad = jnp.sum(scan_back * signal_float, axis=0)
    block_dout = scan_back.reshape(size, 2, half_rows, chan)
    local_back = scan_backs(block_steps, block_dout, write_read, rate2)
    (backs_all,), (attn_piece,), (mamba_share,) = together(
        [
            ctx_gather_job(local_back.reshape(-1, chan)),
            scatter_job(attn_quarter, size),
            ctx_sum_job(mamba_wgrad.astype(bf16)),
        ],
        size,
        9,
        "backs",
    )
    backs_all = backs_all.reshape(blocks_all, NS, size, chan)
    step_back, carry_writes, read_write_back, decay_sums = scan_backward(
        order, block_steps, block_inputs, block_dout, write_read, rate2, start_state, ends_all, backs_all
    )
    decay_grad = rate * jnp.sum(decay_sums, axis=(0, 2))
    step_back = step_back.reshape(rows_all, chan)
    signal_back = scan_back * skip_float + step_sizes * carry_writes.reshape(rows_all, chan)
    read_write_back = read_write_back.reshape(rows_all, 128)[:, : 2 * NS]
    pre_back = (step_back * jax.nn.sigmoid(step_pre)).astype(bf16)
    step_wgrad = jnp.einsum("lr,li->ri", step_low, pre_back, preferred_element_type=f32)
    bias_grad = jnp.sum(pre_back.astype(f32), axis=0)
    rank_back = jnp.einsum("li,ri->lr", pre_back, step_mat, preferred_element_type=f32)
    select_part = jnp.concatenate([rank_back, read_write_back], axis=1).astype(bf16).T
    (select_back,), (attn_home,) = together(
        [sum_job(select_part, size), ctx_gather_job(attn_piece.astype(bf16))],
        size,
        10,
        "select_back",
    )
    select_back = select_back.T
    select_wgrad = jnp.einsum("li,lk->ik", signal, select_back, preferred_element_type=f32)
    signal_back = signal_back + jnp.einsum(
        "lk,ik->li", select_back, select_mat, preferred_element_type=f32
    )
    conv_back = signal_back * silu_slope(conv_out)
    conv_blocks = conv_back.reshape(size, 2, half_rows, chan)
    taps_grad = jnp.stack(
        [
            jnp.sum(conv_blocks * padded[:, :, offset : offset + half_rows], axis=(0, 1, 2))
            for offset in range(CONV)
        ]
    )
    shift_grad = jnp.sum(conv_back, axis=0)
    padded_back = sum(
        (
            jnp.pad(
                taps_float[offset] * conv_blocks,
                ((0, 0), (0, 0), (offset, CONV - 1 - offset), (0, 0)),
            )
            for offset in range(CONV)
        )
    )
    tail_back = jnp.where(has_before[None, :, None, None], padded_back[:, :, : CONV - 1], 0.0)
    dout_groups = rows_back.reshape(rows, KV, group, HD).transpose(1, 0, 2, 3)

    def attend_back(parts):
        query_part, key_part, value_part, dout_part, log_part = parts
        scores = (
            jnp.einsum("lgd,sd->gls", query_part, key_part, preferred_element_type=f32)
            * score_scale
        )
        scores = jnp.where(allowed[None], scores, -1e30)
        probs = jnp.exp(scores - log_part)
        value_grad = jnp.einsum(
            "gls,lgd->sd", probs.astype(bf16), dout_part, preferred_element_type=f32
        )
        prob_grad = jnp.einsum("lgd,sd->gls", dout_part, value_part, preferred_element_type=f32)
        centre = jnp.sum(probs * prob_grad, axis=-1, keepdims=True)
        score_grad = (probs * (prob_grad - centre)).astype(bf16)
        query_grad = (
            jnp.einsum("gls,sd->lgd", score_grad, key_part, preferred_element_type=f32)
            * score_scale
        )
        key_grad = (
            jnp.einsum("gls,lgd->sd", score_grad, query_part, preferred_element_type=f32)
            * score_scale
        )
        return (query_grad, key_grad, value_grad)

    query_grads, key_grads, value_grads = lax.map(
        attend_back, (query_groups, key_groups, value_groups, dout_groups, log_totals)
    )
    keyval_terms = jnp.concatenate(
        [
            key_grads.transpose(1, 0, 2).reshape(-1, KV * HD),
            value_grads.transpose(1, 0, 2).reshape(-1, KV * HD),
        ],
        axis=1,
    )
    (tails_back_all,), (keyval_back,) = together(
        [
            ctx_gather_job(tail_back.astype(bf16).reshape(-1, chan)),
            halve_job(keyval_terms.astype(bf16).reshape(n_ctx, rows, 2 * KV * HD), False),
        ],
        size,
        11,
        "edges_back",
    )
    keyval_back = keyval_back[0]
    query_back = query_grads.transpose(1, 0, 2, 3).reshape(rows, H * HD).astype(bf16)
    qkv_back = jnp.concatenate(
        [
            jnp.pad(query_back.reshape(rows, size, q_cols), ((0, 0), (0, 0), (0, q_up - q_cols))),
            jnp.pad(
                keyval_back.reshape(rows, size, kv_cols), ((0, 0), (0, 0), (0, kv_up - kv_cols))
            ),
        ],
        axis=2,
    ).transpose(1, 0, 2)
    tails_back_all = in_deal_order(tails_back_all.reshape(n_ctx, size, 2, CONV - 1, chan))
    after_index = inverse[jnp.minimum(my_blocks + 1, blocks_all - 1)]
    has_after = my_blocks < blocks_all - 1
    incoming = jnp.where(
        has_after[None, :, None, None], of_blocks(tails_back_all, after_index).astype(f32), 0.0
    )
    mixer_back = padded_back[:, :, CONV - 1 :] + jnp.pad(
        incoming, ((0, 0), (0, 0), (half_rows - (CONV - 1), 0), (0, 0))
    )
    entry_back = jnp.concatenate([mixer_back.reshape(rows_all, chan), side_back], axis=1).astype(
        bf16
    )
    input_part = jnp.einsum("lk,dk->ld", entry_back, entry_mat, preferred_element_type=f32)

    ((qkv_back,),) = together([exchange_job(qkv_back, size)], size, 12, "qkv_back")
    qkv_back = qkv_back.reshape(rows_all, -1)
    first_back = [qkv_back, entry_back]
    if first_total > qkv_up + 2 * chan_up:
        first_back.append(jnp.zeros((rows_all, first_total - qkv_up - 2 * chan_up), bf16))
    first_wgrad = column_grads(normed_all, jnp.concatenate(first_back, axis=1))
    input_part = input_part + jnp.einsum(
        "lk,dk->ld", qkv_back, qkv_mat, preferred_element_type=f32
    )
    low_part = input_part.astype(bf16)
    normed_float = stream_all.astype(f32) * inv_all
    in_gain_grad = jnp.sum(low_part.astype(f32) * normed_float, axis=0)
    gain_grad = jnp.stack([in_gain_grad, attn_gain_grad, mamba_gain_grad, ffn_gain_grad])
    gain_parts = jnp.moveaxis(gain_grad.reshape(4, size, -1), 1, 0).astype(bf16)
    small = jnp.concatenate(
        [
            taps_grad,
            shift_grad[None],
            bias_grad[None],
            skip_grad[None],
            decay_grad,
            step_wgrad,
            select_wgrad.T,
        ]
    )
    n_small = small.shape[0]
    small = jnp.pad(small, ((0, up_to(n_small, 64) - n_small), (0, 0))).astype(bf16)
    (input_back,), (first_home,), (small,), (gain_share,) = together(
        [
            scatter_job(low_part.reshape(size, rows, width), size),
            home_job(first_wgrad.reshape(size, depth, first_total), size),
            ctx_sum_job(small),
            all_sum_job(gain_parts, size),
        ],
        size,
        13,
        "finish",
    )
    stream_part, _ = norm_backward(input_back, stream, inv_in, gain_float[0])
    stream_back = middle_back + stream_part
    gate_share, up_share = unpack_columns(
        ffn_home[None], ffn_cuts, ffn_at, (gate_weight.shape, up_weight.shape), ffn_total
    )
    query_share, keyval_share, entry_share = unpack_columns(
        first_home[None],
        first_cuts,
        first_at,
        (query_weight.shape, keyval_weight.shape, mamba_in.shape),
        first_total,
    )
    chan = conv_bias.shape[0]
    vectors = small.reshape(-1, chan_up)[:, :chan].astype(f32)
    attn_share = jnp.moveaxis(attn_home, 0, 1).reshape(depth, attn_wide)[:, :width].astype(f32)
    mamba_share = mamba_share.reshape(-1, width)[:chan].astype(f32)
    down_share = down_share.reshape(-1, width)[:ff_cols].astype(f32)
    return (
        result.astype(bf16)[None],
        stream_back[None],
        gain_share,
        query_share,
        keyval_share,
        attn_share,
        entry_share,
        vectors[:CONV],
        vectors[CONV],
        vectors[CONV + 1],
        vectors[CONV + 2],
        vectors[CONV + 3 : CONV + 3 + NS],
        vectors[CONV + 3 + NS + RANK : n_small].T,
        vectors[CONV + 3 + NS : CONV + 3 + NS + RANK],
        mamba_share,
        gate_share,
        up_share,
        down_share,
    )


def solution(mesh):
    in_specs = (
        P("fsdp", "ctx", None),
        P("fsdp", "ctx", None),
        P("fsdp", None),
        P(),
        P(None, "fsdp"),
        P("fsdp", None),
        P("fsdp", None),
        P("fsdp", None),
        P("fsdp", None),
        P(None, "fsdp"),
        P("fsdp"),
        P("fsdp"),
        P("fsdp"),
        P(None, "fsdp"),
        P("fsdp", None),
        P(None, "fsdp"),
        P("fsdp", None),
        P("fsdp", None),
        P("fsdp", None),
        P("fsdp", None),
    )
    out_specs = (
        P("fsdp", "ctx", None),
        P("fsdp", "ctx", None),
        P(None, "fsdp"),
        P("fsdp", None),
        P("fsdp", None),
        P("fsdp", None),
        P("fsdp", None),
        P(None, "fsdp"),
        P("fsdp"),
        P("fsdp"),
        P("fsdp"),
        P(None, "fsdp"),
        P("fsdp", None),
        P(None, "fsdp"),
        P("fsdp", None),
        P("fsdp", None),
        P("fsdp", None),
        P("fsdp", None),
    )
    return jax.shard_map(
        on_device, mesh=mesh, in_specs=in_specs, out_specs=out_specs, check_vma=False
    )
```

time: 4960 us -> 1150 us (0.23)
  waiting for transfers between devices: 3700 us -> 0 us
  Pallas kernels: 0 us -> 840 us
  blocking collectives: 339 us -> 0 us
  other arithmetic: 378 us -> 52.3 us
  local copies, waits for them, and re-layouts: 273 us -> 88 us
  matrix products: 213 us -> 150 us
    unnamed x39 -> x0, waiting for transfers between devices: 1690 us -> none
    all_gather x13 -> x0, waiting for transfers between devices: 1400 us -> none  [the longest x1 387 us: on_device(): lax.all_gather(mamba_in, 'fsdp', axis=0, tiled=True)]
    pallas_call x0 -> x22, Pallas kernels: none -> 840 us  [the longest x14 703 us: together(): pl.pallas_call(kernel, out_shape=[shape for job in jobs for shape, _ in j...]
    reduce_scatter x4 -> x0, waiting for transfers between devices: 619 us -> none  [the longest x1 355 us: on_device(): lax.psum_scatter(down_wgrad.astype(jnp.bfloat16), 'fsdp', scatter_dimensi...]
    all_gather x14 -> x0, blocking collectives: 245 us -> none  [the longest x1 36.5 us: on_device(): lax.all_gather(select_proj, 'fsdp', axis=0, tiled=True)]
    reshape x8 -> x1, other arithmetic: 170 us -> 0.9 us  [on_device(): selected[RANK:].astype(f32).T.reshape(size, 2, half_rows, 2 * NS)]
    another operation x78 -> x6, other arithmetic: 111 us -> 0.6 us  [the longest x32 61.8 us: one_piece(): jnp.cumsum(jnp.exp(-climbing) * pushed, axis=1)]
    unnamed x4 -> x0, blocking collectives: 93.8 us -> none
  transfers between devices with their start and end apart: 28 -> 0, of which waited for: 18 -> 0; matrix products, arithmetic and copies ran while one was open for 12% -> 0% of each run, Pallas kernels for 0% -> 0%
where the time goes in v2:
time: 1150 us; the launch traced here: 1130 us
  Pallas kernels  840 us (73%)
  matrix products  150 us (13%)
  local copies, waits for them, and re-layouts  88 us (8%)
  other arithmetic  52.3 us (5%)
    pallas_call x14, Pallas kernels, together(): pl.pallas_call(kernel, out_shape=[shape for job in jobs for shape, _ in j...  703 us
    pallas_call x1, Pallas kernels, scan_backward(): pl.pallas_call(kernel, grid_spec=pltpu.PrefetchScalarGridSpec(num_scalar_...  56.8 us
    pallas_call x1, Pallas kernels, scan_forward(): pl.pallas_call(kernel, grid_spec=pltpu.PrefetchScalarGridSpec(num_scalar_...  24.7 us

profile of v2, /device:TPU:0, one launch (start us, length us, event | category | flops | bytes accessed | tf_op | source)
XLA Modules:
  0.0 1133.8 jit_solution(2240777483438071186)
XLA Ops:
  8.5 78.6 %start.1 = (bf16[1024,1600]{1,0:T(8,128)(2,1)}, bf16[8,4,200]{2,1,0:T(4,128)(2,1)}, bf16[8,200,1536]{2,1,0:T(8,128)(2,1)}) custom-call(bf16[128,1600]{1,0:T(8,128)(2,1)} %bitcast.330, bf16[4,200]{1,0:T(4,128)(2,1)} %refs_1_.4, bf16[8,200,1536]{2,1,0:T(8,128)(2,1)} %pack_columns.2.refs_2_), custom_call_target="tpu_custom_call" | custom-call | tf_op jit(solution)/shard_map/start/pallas_call | solution.py:546
  105.1 16.9 %qkv.1 = bf16[8,128,384]{2,1,0:T(8,128)(2,1)} custom-call(bf16[8,128,384]{2,1,0:T(8,128)(2,1)} %bitcast.366), custom_call_target="tpu_custom_call" | custom-call | tf_op jit(solution)/shard_map/qkv/pallas_call | solution.py:546
  124.0 16.1 %edges.1 = (bf16[4,128,640]{2,1,0:T(8,128)(2,1)}, bf16[4,48,512]{2,1,0:T(8,128)(2,1)}) custom-call(bf16[128,640]{1,0:T(8,128)(2,1)} %copy.116.refs_0_, bf16[48,512]{1,0:T(8,128)(2,1)} %reshape.429.refs_1_), custom_call_target="tpu_custom_call" | custom-call | tf_op jit(solution)/shard_map/edges/pallas_call | solution.py:546
  151.3 16.9 %select.32 = bf16[132,1024]{1,0:T(8,128)(2,1)} custom-call(bf16[132,1024]{1,0:T(8,128)(2,1)} %convolution_convert_fusion.8.refs_0_), custom_call_target="tpu_custom_call" | custom-call | tf_op jit(solution)/shard_map/select/pallas_call | solution.py:546
  175.0 15.8 %scan_ends.1 = bf16[2,17,8,512]{3,2,1,0:T(8,128)(2,1)} custom-call(f32[8,2,64,512]{3,2,1,0:T(8,128)} %bitcast.317, f32[8,2,64,512]{3,2,1,0:T(8,128)} %get-tuple-element.379.x_ref, f32[8,2,64,32]{3,2,1,0:T(8,128)} %bitcast.326, f32[16,512]{1,0:T(8,128)} %fusion.130.rate_ref), custom_call_target="tpu_custom_call" | custom-call | tf_op jit(solution)/shard_map/scan_ends/pallas_call | solution.py:120
  198.7 119.1 %ends.1 = (bf16[4,272,512]{2,1,0:T(8,128)(2,1)}, bf16[1024,1600]{1,0:T(8,128)(2,1)}, bf16[8,200,1536]{2,1,0:T(8,128)(2,1)}, bf16[8,200,2048]{2,1,0:T(8,128)(2,1)}) custom-call(bf16[272,512]{1,0:T(8,128)(2,1)} %bitcast.356, bf16[128,1600]{1,0:T(8,128)(2,1)} %bitcast.346, bf16[8,200,1536]{2,1,0:T(8,128)(2,1)} %pack_columns.3.refs_2_, ...), custom_call_target="tpu_custom_call" | custom-call | tf_op jit(solution)/shard_map/ends/pallas_call | solution.py:546
  324.3 10.1 while.28
  343.2 24.7 %scan_forward.1 = (f32[8,2,64,512]{3,2,1,0:T(8,128)}, f32[2,16,8,512]{3,2,1,0:T(8,128)}) custom-call(s32[10]{0:T(128)} %pad_add_fusion.1.order_ref, f32[8,2,64,512]{3,2,1,0:T(8,128)} %bitcast.318, f32[8,2,64,512]{3,2,1,0:T(8,128)} %get-tuple-element.379.x_ref, f32[8,2,64,32]{3,2,1,0:T(8,128)} %bitcast.327, f32[16,512]{1,0:T(8,128)} %fusion.130.rate_ref, ...), custom_call_target="tpu_custom_call" | custom-call | tf_op jit(solution)/shard_map/scan_forward/pallas_call | solution.py:182
  376.1 19.3 %copy.127 = bf16[1024,1600]{1,0:T(8,128)(2,1)} copy(bf16[1024,1600]{0,1:T(8,128)(2,1)} %convolution_convert_fusion.4) | data formatting | bytes 6553600 | tf_op jit(solution)/shard_map/convert_element_type | solution.py:1404
  395.5 51.8 %mamba_sum.1 = f32[128,1600]{1,0:T(8,128)} custom-call(bf16[8,128,1600]{2,1,0:T(8,128)(2,1)} %bitcast.322), custom_call_target="tpu_custom_call" | custom-call | tf_op jit(solution)/shard_map/mamba_sum/pallas_call | solution.py:546
  451.9 40.5 %ffn_rows.1 = bf16[1024,1600]{1,0:T(8,128)(2,1)} custom-call(bf16[128,1600]{1,0:T(8,128)(2,1)} %multiply_convert_fusion.9.refs_0_), custom_call_target="tpu_custom_call" | custom-call | tf_op jit(solution)/shard_map/ffn_rows/pallas_call | solution.py:546
  508.5 7.7 convolution_convert_fusion.1
  528.4 77.0 %ffn_sum.1 = (f32[128,1600]{1,0:T(8,128)}, bf16[8,200,1536]{2,1,0:T(8,128)(2,1)}) custom-call(bf16[8,128,1600]{2,1,0:T(8,128)(2,1)} %bitcast.324, bf16[8,200,1536]{2,1,0:T(8,128)(2,1)} %bitcast.341), custom_call_target="tpu_custom_call" | custom-call | tf_op jit(solution)/shard_map/ffn_sum/pallas_call | solution.py:546
  613.3 30.2 %while.29 = (s32[]{:T(128)}, bf16[5,128,5,64]{1,3,2,0:T(8,128)(2,1)S(1)}, bf16[5,512,64]{1,2,0:T(8,128)(2,1)}, bf16[5,512,64]{1,2,0:T(8,128)(2,1)}, bf16[5,512,6...) while((s32[]{:T(128)}, ...), condition=%wide.region_18.20_spmd.clone, body=%wide.region_16.19_spmd.clone.sunk | while | flops 212934016 | bytes 10936457 | solution.py:1569
  671.6 100.6 %mamba_rows.1 = (bf16[1024,1600]{1,0:T(8,128)(2,1)}, f32[128,1600]{1,0:T(8,128)}, bf16[4,192,1600]{2,1,0:T(8,128)(2,1)}, bf16[8,200,512]{2,1,0:T(8,128)(2,1)}) custom-call(bf16[128,1600]{1,0:T(8,128)(2,1)} %get-tuple-element.394.refs_0_, bf16[8,128,1600]{2,1,0:T(8,128)(2,1)} %bitcast.323, bf16[4,192,1600]{2,1,0:T(8,128)(2,1)} %bitcast.331, ...), custom_call_target="tpu_custom_call" | custom-call | tf_op jit(solution)/shard_map/mamba_rows/pallas_call | solution.py:546
  778.4 8.9 fusion.83
  787.3 15.3 %scan_backs.1 = bf16[2,16,8,512]{3,2,1,0:T(8,128)(2,1)} custom-call(f32[8,2,64,512]{3,2,1,0:T(8,128)} %bitcast.319, f32[8,2,64,512]{3,2,1,0:T(8,128)} %bitcast.332, f32[8,2,64,32]{3,2,1,0:T(8,128)} %bitcast.328, f32[16,512]{1,0:T(8,128)} %fusion.130.rate_ref), custom_call_target="tpu_custom_call" | custom-call | tf_op jit(solution)/shard_map/scan_backs/pallas_call | solution.py:236
  802.6 35.2 %backs.1 = (bf16[4,256,512]{2,1,0:T(8,128)(2,1)}, f32[200,512]{1,0:T(8,128)}, bf16[4,128,1600]{2,1,0:T(8,128)(2,1)}) custom-call(bf16[256,512]{1,0:T(8,128)(2,1)} %bitcast.360, bf16[8,200,512]{2,1,0:T(8,128)(2,1)} %get-tuple-element.165.refs_1_, bf16[4,128,1600]{2,1,0:T(8,128)(2,1)} %bitcast.335), custom_call_target="tpu_custom_call" | custom-call | tf_op jit(solution)/shard_map/backs/pallas_call | solution.py:546
  837.8 56.8 %scan_backward.1 = (f32[8,2,64,512]{3,2,1,0:T(8,128)}, f32[8,2,64,512]{3,2,1,0:T(8,128)}, f32[8,2,64,128]{3,2,1,0:T(8,128)}, f32[2,16,8,512]{3,2,1,0:T(8,128)}) custom-call(s32[10]{0:T(128)} %pad_add_fusion.1.order_ref, f32[8,2,64,512]{3,2,1,0:T(8,128)} %bitcast.320, f32[8,2,64,512]{3,2,1,0:T(8,128)} %get-tuple-element.379.x_ref, ...), custom_call_target="tpu_custom_call" | custom-call | tf_op jit(solution)/shard_map/scan_backward/pallas_call | solution.py:372
  903.2 18.7 %select_back.1 = (bf16[132,1024]{1,0:T(8,128)(2,1)}, bf16[4,200,512]{2,1,0:T(8,128)(2,1)}) custom-call(bf16[132,1024]{1,0:T(8,128)(2,1)} %maximum_bitcast_fusion.refs_0_, bf16[200,512]{1,0:T(8,128)(2,1)} %convert_element_type.260.refs_1_), custom_call_target="tpu_custom_call" | custom-call | tf_op jit(solution)/shard_map/select_back/pallas_call | solution.py:546
  932.5 13.2 %edges_back.1 = (bf16[4,48,512]{2,1,0:T(8,128)(2,1)}, bf16[1,128,640]{2,1,0:T(8,128)(2,1)}) custom-call(bf16[48,512]{1,0:T(8,128)(2,1)} %reshape.458.refs_0_, bf16[4,128,640]{2,1,0:T(8,128)(2,1)} %pad_maximum_fusion.refs_1_), custom_call_target="tpu_custom_call" | custom-call | tf_op jit(solution)/shard_map/edges_back/pallas_call | solution.py:546
  951.0 16.4 %qkv_back.1 = bf16[8,128,384]{2,1,0:T(8,128)(2,1)} custom-call(bf16[8,128,384]{2,1,0:T(8,128)(2,1)} %fusion.117.refs_0_), custom_call_target="tpu_custom_call" | custom-call | tf_op jit(solution)/shard_map/qkv_back/pallas_call | solution.py:546
  993.1 9.8 convolution_convert_fusion
  1002.9 101.7 %finish.1 = (f32[128,1600]{1,0:T(8,128)}, bf16[8,200,1536]{2,1,0:T(8,128)(2,1)}, bf16[4,64,512]{2,1,0:T(8,128)(2,1)}, f32[4,200]{1,0:T(4,128)}) custom-call(bf16[8,128,1600]{2,1,0:T(8,128)(2,1)} %bitcast.325, bf16[8,200,1536]{2,1,0:T(8,128)(2,1)} %bitcast.340, bf16[4,64,512]{2,1,0:T(8,128)(2,1)} %bitcast.361, bf16[8,4,200]{2,1,0:T(4,128)(2,1)} %maximum_bitcast_fusion.1.refs_3_), custom_call_target="tpu_custom_call" | custom-call | tf_op jit(solution)/shard_map/finish/pallas_call | solution.py:546
  (419 shorter events, 269.2 us)
Async XLA Ops:
  88.0 11.9 %copy-start.48 = (f32[1600]{0:T(1024)}, f32[1600]{0:T(1024)S(1)}, u32[]{:S(2)}) copy-start(f32[1600]{0:T(1024)S(1)} %mul.447) | copy-start | bytes 19204
  90.9 9.0 copy-start.60
  105.1 36.2 %copy-start.68 = (s32[4,2]{0,1:T(2,128)S(1)}, s32[4,2]{0,1:T(2,128)}, u32[]{:S(2)}) copy-start(s32[4,2]{0,1:T(2,128)} %param.29) | copy-start | bytes 100
  148.3 219.7 %copy-start.3 = (f32[8,2,64,512]{3,2,1,0:T(8,128)}, f32[8,2,64,512]{3,2,1,0:T(8,128)S(1)}, u32[]{:S(2)}) copy-start(f32[8,2,64,512]{3,2,1,0:T(8,128)S(1)} %get-tuple-element.380) | copy-start | bytes 6291460
  148.3 20.0 %copy-start.73 = (bf16[400]{0:T(512)(128)(2,1)S(1)}, bf16[400]{0:T(512)(128)(2,1)}, u32[]{:S(2)}) copy-start(bf16[400]{0:T(512)(128)(2,1)} %param.37) | copy-start | bytes 2404
  148.3 20.0 %copy-start.46 = (bf16[100,400]{0,1:T(8,128)(2,1)S(1)}, bf16[100,400]{0,1:T(8,128)(2,1)}, u32[]{:S(2)}) copy-start(bf16[100,400]{0,1:T(8,128)(2,1)} %param.41) | copy-start | bytes 240004
  175.0 15.8 %copy-start.42 = (bf16[1,128,1600]{1,2,0:T(8,128)(2,1)S(1)}, bf16[1,128,1600]{1,2,0:T(8,128)(2,1)}, u32[]{:S(2)}) copy-start(bf16[1,128,1600]{1,2,0:T(8,128)(2,1)} %param.27) | copy-start | bytes 1228804
  343.2 24.7 %copy-start.74 = (bf16[400]{0:T(512)(128)(2,1)S(1)}, bf16[400]{0:T(512)(128)(2,1)}, u32[]{:S(2)}) copy-start(bf16[400]{0:T(512)(128)(2,1)} %param.38) | copy-start | bytes 2404
  395.5 53.3 %copy-start.7 = (f32[128,1600]{1,0:T(8,128)S(1)}, f32[128,1600]{1,0:T(8,128)}, u32[]{:S(2)}) copy-start(f32[128,1600]{1,0:T(8,128)} %copy.126) | copy-start | bytes 2457604
  395.5 53.3 %copy-start.10 = (bf16[1,128,1600]{2,1,0:T(8,128)(2,1)S(1)}, bf16[1,128,1600]{2,1,0:T(8,128)(2,1)}, u32[]{:S(2)}) copy-start(bf16[1,128,1600]{2,1,0:T(8,128)(2,1)} %copy.114) | copy-start | bytes 1228804
  498.4 17.8 %slice-start = ((s8[4915200]{0:T(1024)(128)(4,1)}), s8[4194304]{0:T(1024)(128)(4,1)S(1)}, s32[]{:S(2)}) async-start(s8[4915200]{0:T(1024)(128)(4,1)} %bitcast.392), calls=%async_computation | async-start | bytes 8388608
  501.4 14.7 %slice-start.1 = ((s8[4915200]{0:T(1024)(128)(4,1)}), s8[720896]{0:T(1024)(128)(4,1)S(1)}, s32[]{:S(2)}) async-start(s8[4915200]{0:T(1024)(128)(4,1)} %bitcast.392), calls=%async_computation.1 | async-start | bytes 1441792
  528.4 78.6 %copy-start.21 = (bf16[1,128,1600]{2,1,0:T(8,128)(2,1)S(1)}, bf16[1,128,1600]{2,1,0:T(8,128)(2,1)}, u32[]{:S(2)}) copy-start(bf16[1,128,1600]{2,1,0:T(8,128)(2,1)} %copy.125) | copy-start | bytes 1228804
  671.6 100.6 %copy-start.37 = (bf16[1024,512]{1,0:T(8,128)(2,1)S(1)}, bf16[1024,512]{1,0:T(8,128)(2,1)}, u32[]{:S(2)}) copy-start(bf16[1024,512]{1,0:T(8,128)(2,1)} %copy-done.36) | copy-start | bytes 3145732
  837.8 56.8 %copy-start.30 = (f32[1024,512]{1,0:T(8,128)S(1)}, f32[1024,512]{1,0:T(8,128)}, u32[]{:S(2)}) copy-start(f32[1024,512]{1,0:T(8,128)} %get-tuple-element.405) | copy-start | bytes 6291460
  837.8 56.8 %copy-start.63 = (f32[512]{0:T(512)S(1)}, f32[512]{0:T(512)}, u32[]{:S(2)}) copy-start(f32[512]{0:T(512)} %copy-done.62) | copy-start | bytes 6148
  897.5 24.4 %copy-start.1 = (f32[8,2,67,512]{3,2,1,0:T(8,128)S(1)}, f32[8,2,67,512]{3,2,1,0:T(8,128)}, u32[]{:S(2)}) copy-start(f32[8,2,67,512]{3,2,1,0:T(8,128)} %copy-done) | copy-start | bytes 6586372
  948.9 18.5 %copy-start.44 = (bf16[4,48,512]{2,1,0:T(8,128)(2,1)S(1)}, bf16[4,48,512]{2,1,0:T(8,128)(2,1)}, u32[]{:S(2)}) copy-start(bf16[4,48,512]{2,1,0:T(8,128)(2,1)} %get-tuple-element.175) | copy-start | bytes 589828
  948.9 18.7 %copy-start.77 = (s32[2]{0:T(128)S(1)}, s32[2]{0:T(128)}, u32[]{:S(2)}) copy-start(s32[2]{0:T(128)} %get-tuple-element.323) | copy-start | bytes 28
  948.9 20.0 %copy-start.71 = (pred[2]{0:T(512)(128)(4,1)S(1)}, pred[2]{0:T(512)(128)(4,1)}, u32[]{:S(2)}) copy-start(pred[2]{0:T(512)(128)(4,1)} %get-tuple-element.402) | copy-start | bytes 10
  980.5 7.5 copy-start.16
  980.5 7.5 copy-start.33
  1104.7 6.3 copy-start.19
  1125.7 7.1 copy-start.69
  (63 other events, 228.4 us)

commit v3 on v2

v3 whole, which is shorter than its diff:
```python
import functools
import math

import jax
import jax.numpy as jnp
from jax import lax
from jax.experimental import pallas as pl
from jax.experimental.pallas import tpu as pltpu
from jax.sharding import PartitionSpec as P

H = 25
KV = 5
HD = 64
INNER = 3200
NS = 16
RANK = 100
CONV = 4

EPS = 1e-06
score_scale = 0.125
MESH = pl.DeviceIdType.MESH
ANY = pl.BlockSpec(memory_space=pl.ANY)
VM = pl.BlockSpec(memory_space=pltpu.VMEM)
DMA = pltpu.SemaphoreType.DMA
f32 = jnp.float32
bf16 = jnp.bfloat16


def params(cid, vmem=None):
    return pltpu.CompilerParams(collective_id=cid, has_side_effects=True, vmem_limit_bytes=vmem)


def rcopy(src, dst, ssem, rsem, dev):
    return pltpu.make_async_remote_copy(
        src_ref=src, dst_ref=dst, send_sem=ssem, recv_sem=rsem, device_id=dev, device_id_type=MESH
    )


def norm_forward(values, gain):
    inverse = lax.rsqrt(jnp.mean(values * values, axis=-1, keepdims=True) + EPS)
    return (values * inverse * gain, inverse)


def norm_backward(grad, values, inverse, gain):
    normed = values * inverse
    gain_grad = jnp.sum(grad * normed, axis=0)
    scaled = grad * gain
    return (
        inverse * (scaled - normed * jnp.mean(scaled * normed, axis=-1, keepdims=True)),
        gain_grad,
    )


def silu_slope(values):
    sigma = jax.nn.sigmoid(values)
    return sigma * (1.0 + values * (1.0 - sigma))


def up_to(value, step):
    return (value + step - 1) // step * step


def pack_columns(refs, out, cuts, offsets, size):
    out[...] = jnp.zeros_like(out)
    for (which, first, cols), at in zip(cuts, offsets):
        for f in range(size):
            out[f, :, at : at + cols] = refs[which][:, first + f * cols : first + (f + 1) * cols]


def unpack_pieces(home, outs, cuts, offsets, size):
    for (which, first, cols), at in zip(cuts, offsets):
        for f in range(size):
            outs[which][:, first + f * cols : first + (f + 1) * cols] = home[
                f, :, at : at + cols
            ].astype(f32)


def unpack_columns(home, cuts, offsets, shapes, size):
    def kernel(h_ref, *outs):
        unpack_pieces(h_ref, outs, cuts, offsets, size)

    return pl.pallas_call(
        kernel,
        out_shape=[jax.ShapeDtypeStruct(shape, f32) for shape in shapes],
        in_specs=[VM],
        out_specs=[VM] * len(shapes),
        compiler_params=pltpu.CompilerParams(vmem_limit_bytes=60 << 20),
        name="unpack_columns",
    )(home)


class Job:
    def __init__(self, steps, ins, outs, scratch):
        self.steps, self.ins, self.outs, self.scratch = steps, ins, outs, scratch


class Place:
    def __init__(self, size):
        self.size, self.lanes = size, size // 2
        self.f, self.c = lax.axis_index("fsdp"), lax.axis_index("ctx")
        self.a, self.b = self.f // 2, lax.rem(self.f, 2)
        self.near = self.c + 1 - 2 * lax.rem(self.c, 2)
        self.far = lax.rem(self.c + 2, 4)
        self.other = lax.rem(self.near + 2, 4)

    def greet(self):
        bar = pltpu.get_barrier_semaphore()
        for d in range(1, self.size):
            peer = {"fsdp": lax.rem(self.f + d, self.size)}
            pl.semaphore_signal(bar, inc=1, device_id=peer, device_id_type=MESH)
        for peer in (self.near, self.far):
            pl.semaphore_signal(bar, inc=1, device_id={"ctx": peer}, device_id_type=MESH)
        pl.semaphore_wait(bar, self.size + 1)


def part(ref_list, jobs, field):
    out = []
    for job in jobs:
        count = len(getattr(job, field))
        out.append(ref_list[:count])
        ref_list = ref_list[count:]
    return out


class Moving:
    def __init__(self, live):
        self.live = live

    def step(self, which):
        if which < len(self.live) and self.live[which] is not None:
            try:
                next(self.live[which])
            except StopIteration:
                self.live[which] = None

    def drain(self):
        while any(item is not None for item in self.live):
            for which in range(len(self.live)):
                self.step(which)


def together(jobs, size, cid, name, order=()):
    n_in = sum(len(job.ins) for job in jobs)
    n_out = sum(len(job.outs) for job in jobs)

    def kernel(*refs):
        place = Place(size)
        place.greet()
        ins = part(refs[:n_in], jobs, "ins")
        outs = part(refs[n_in : n_in + n_out], jobs, "outs")
        scratch = part(refs[n_in + n_out :], jobs, "scratch")
        moving = Moving(
            [job.steps(place, i, o, s) for job, i, o, s in zip(jobs, ins, outs, scratch)]
        )
        for which in order:
            moving.step(which)
        moving.drain()

    got = pl.pallas_call(
        kernel,
        out_shape=[shape for job in jobs for shape, _ in job.outs],
        in_specs=[spec for job in jobs for _, spec in job.ins],
        out_specs=[spec for job in jobs for _, spec in job.outs],
        scratch_shapes=[item for job in jobs for item in job.scratch],
        compiler_params=params(cid, 60 << 20),
        name=name,
    )(*[array for job in jobs for array, _ in job.ins])
    return part(got, jobs, "outs")


def like(shape, dtype):
    return jax.ShapeDtypeStruct(shape, dtype)


def gather_job(x, size, shared=False):
    rows, cols = x.shape
    lanes = size // 2

    def run(p, ins, outs, scratch):
        (x_ref,), (o_ref,) = ins, outs
        lsem, up_s, up_r, dn_s, dn_r, px_s, px_r = scratch[:7]

        def view(i, q):
            return o_ref.at[i, :, column_block(q, cols // 4)]

        def piece(origin, b):
            i = 2 * origin + b
            return view(i, p.c) if shared else o_ref.at[i]

        def own():
            return x_ref.at[:, column_block(p.c, cols // 4)] if shared else x_ref

        share = Share(p, view, size, scratch[7:]) if shared else None

        def local():
            return pltpu.make_async_copy(own(), piece(p.a, p.b), lsem)

        def up(s):
            src = own() if s == 0 else piece(p.a - s, p.b)
            dev = {"fsdp": 2 * (p.a + 1) + p.b}
            return rcopy(src, piece(p.a - s, p.b), up_s.at[s], up_r.at[s], dev)

        def down(s):
            src = own() if s == 0 else piece(p.a + s, p.b)
            dev = {"fsdp": 2 * (p.a - 1) + p.b}
            return rcopy(src, piece(p.a + s, p.b), dn_s.at[s], dn_r.at[s], dev)

        def across(origin, src=None):
            src = piece(origin, p.b) if src is None else src
            dev = {"fsdp": 2 * p.a + 1 - p.b}
            return rcopy(src, piece(origin, p.b), px_s.at[origin], px_r.at[origin], dev)

        def came(ref, sem, dev):
            rcopy(ref, ref, sem, sem, dev).wait_recv()

        def arrived(origin, b, src=None):
            if shared:
                share.send(2 * origin + b, src)

        local().start()

        @pl.when(p.a < lanes - 1)
        def _():
            up(0).start()

        @pl.when(p.a > 0)
        def _():
            down(0).start()

        across(p.a, own()).start()
        if shared:
            arrived(p.a, p.b, own())
        yield
        for s in range(lanes - 1):
            @pl.when(p.a - 1 - s >= 0)
            def _():
                came(piece(p.a - 1 - s, p.b), up_r.at[s], {"fsdp": 2 * (p.a - 1) + p.b})

                @pl.when(p.a < lanes - 1)
                def _():
                    up(s + 1).start()

                across(p.a - 1 - s).start()
                arrived(p.a - 1 - s, p.b)

            @pl.when(p.a + 1 + s <= lanes - 1)
            def _():
                came(piece(p.a + 1 + s, p.b), dn_r.at[s], {"fsdp": 2 * (p.a + 1) + p.b})

                @pl.when(p.a > 0)
                def _():
                    down(s + 1).start()

                across(p.a + 1 + s).start()
                arrived(p.a + 1 + s, p.b)

            yield
        local().wait()
        for origin in range(lanes):
            came(piece(origin, 1 - p.b), px_r.at[origin], {"fsdp": 2 * p.a + 1 - p.b})
            arrived(origin, 1 - p.b)
        if shared:
            yield
            for i in range(size):
                share.forward(i)
            yield
            share.finish()
        for s in range(lanes - 1):
            @pl.when((p.a - s >= 0) & (p.a < lanes - 1))
            def _():
                up(s).wait_send()

            @pl.when((p.a + s <= lanes - 1) & (p.a > 0))
            def _():
                down(s).wait_send()

        for origin in range(lanes):
            across(origin).wait_send()

    return Job(
        run,
        [(x, ANY)],
        [(like((size, rows, cols), x.dtype), ANY)],
        [DMA] + [DMA((lanes,))] * 6 + (share_sems(size) if shared else []),
    )


def add_blocks(out, terms, dtype, rows):
    if rows % 16:
        total = terms[0][...].astype(f32)
        for ref in terms[1:]:
            total += ref[...].astype(f32)
        out[...] = total.astype(dtype)
        return
    step = 32 if rows % 32 == 0 else 16

    def body(i, carry):
        at = pl.ds(pl.multiple_of(i * step, step), step)
        total = terms[0][at, :].astype(f32)
        for ref in terms[1:]:
            total += ref[at, :].astype(f32)
        out[at, :] = total.astype(dtype)
        return carry

    lax.fori_loop(0, rows // step, body, 0)


def scatter_job(partial, size, held=None):
    rows, cols = partial.shape[1:]
    lanes = size // 2

    def run(p, ins, outs, scratch):
        (o_ref,) = outs
        p_ref = held[0] if held is not None else ins[0]
        xbuf, upb, dnb, up_s, up_r, dn_s, dn_r, px_s, px_r = scratch[:9]

        def own(dest):
            return p_ref.at[2 * dest + p.b] if held is not None else scratch[9].at[dest]

        def local(dest):
            return pltpu.make_async_copy(
                p_ref.at[2 * dest + p.b], scratch[9].at[dest], scratch[10].at[dest]
            )

        def across(dest):
            src = p_ref.at[2 * dest + 1 - p.b]
            dev = {"fsdp": 2 * p.a + 1 - p.b}
            return rcopy(src, xbuf.at[dest], px_s.at[dest], px_r.at[dest], dev)

        def up(dest):
            dev = {"fsdp": 2 * (p.a + 1) + p.b}
            return rcopy(xbuf.at[dest], upb.at[dest], up_s.at[dest], up_r.at[dest], dev)

        def down(dest):
            dev = {"fsdp": 2 * (p.a - 1) + p.b}
            return rcopy(xbuf.at[dest], dnb.at[dest], dn_s.at[dest], dn_r.at[dest], dev)

        def add_in(dest, extra):
            terms = [xbuf.at[dest], own(dest)]
            if extra is not None:
                terms.append(extra.at[dest])
            add_blocks(xbuf.at[dest], terms, bf16, rows)

        if held is None:
            for dest in range(lanes):
                local(dest).start()
        for d in range(lanes - 1, -1, -1):
            @pl.when(p.a + d <= lanes - 1)
            def _():
                across(p.a + d).start()

            if d > 0:
                @pl.when(p.a - d >= 0)
                def _():
                    across(p.a - d).start()

        yield
        if held is None:
            for dest in range(lanes):
                local(dest).wait()
        for d in range(lanes - 1, 0, -1):
            @pl.when(p.a + d <= lanes - 1)
            def _():
                across(p.a + d).wait_recv()

                @pl.when(p.a > 0)
                def _():
                    up(p.a + d).wait_recv()
                    add_in(p.a + d, upb)

                @pl.when(p.a == 0)
                def _():
                    add_in(p.a + d, None)

                up(p.a + d).start()

            @pl.when(p.a - d >= 0)
            def _():
                across(p.a - d).wait_recv()

                @pl.when(p.a < lanes - 1)
                def _():
                    down(p.a - d).wait_recv()
                    add_in(p.a - d, dnb)

                @pl.when(p.a == lanes - 1)
                def _():
                    add_in(p.a - d, None)

                down(p.a - d).start()

            yield
        across(p.a).wait_recv()
        terms = [xbuf.at[p.a], own(p.a)]

        @pl.when(p.a == 0)
        def _():
            down(p.a).wait_recv()
            add_blocks(o_ref, terms + [dnb.at[p.a]], f32, rows)

        @pl.when(p.a == lanes - 1)
        def _():
            up(p.a).wait_recv()
            add_blocks(o_ref, terms + [upb.at[p.a]], f32, rows)

        @pl.when((p.a > 0) & (p.a < lanes - 1))
        def _():
            up(p.a).wait_recv()
            down(p.a).wait_recv()
            add_blocks(o_ref, terms + [upb.at[p.a], dnb.at[p.a]], f32, rows)

        for dest in range(lanes):
            across(dest).wait_send()

        for d in range(lanes - 1, 0, -1):
            @pl.when(p.a + d <= lanes - 1)
            def _():
                up(p.a + d).wait_send()

            @pl.when(p.a - d >= 0)
            def _():
                down(p.a - d).wait_send()

    return Job(
        run,
        [(partial, ANY)] if held is None else [],
        [(like((rows, cols), f32), VM)],
        [pltpu.VMEM((lanes, rows, cols), bf16)] * 3
        + [DMA((lanes,))] * 6
        + ([pltpu.VMEM((lanes, rows, cols), bf16), DMA((lanes,))] if held is None else []),
    )


def column_block(of, quarter):
    return pl.ds(pl.multiple_of(of * quarter, 128), quarter)


class Share:
    def __init__(self, p, view, count, sems):
        self.p, self.view, self.count = p, view, count
        self.fs, self.fr, self.ns, self.nr, self.hs, self.hr = sems

    def far(self, d, q, src=None):
        ref = self.view(d, q)
        src = ref if src is None else src
        return rcopy(src, ref, self.fs.at[d], self.fr.at[d], {"ctx": self.p.far})

    def near(self, d, q, src=None):
        ref = self.view(d, q)
        src = ref if src is None else src
        return rcopy(src, ref, self.ns.at[d], self.nr.at[d], {"ctx": self.p.near})

    def onward(self, d, q):
        ref = self.view(d, q)
        return rcopy(ref, ref, self.hs.at[d], self.hr.at[d], {"ctx": self.p.near})

    def send(self, d, src=None):
        self.far(d, self.p.c, src).start()
        self.near(d, self.p.c, src).start()

    def forward(self, d):
        self.far(d, self.p.far).wait_recv()
        self.onward(d, self.p.far).start()

    def finish(self):
        p = self.p
        for d in range(self.count):
            self.far(d, p.c).wait_send()
            self.near(d, p.c).wait_send()
            self.near(d, p.near).wait_recv()
            self.onward(d, p.far).wait_send()
            self.onward(d, p.other).wait_recv()


def share_sems(count):
    return [DMA((count,))] * 6


def move_job(packed, size, held=None):
    depth, total = packed.shape[-2:]
    quarter = total // 4

    def run(p, ins, outs, scratch):
        (w_ref,) = outs
        p_ref = held[0] if held is not None else ins[0]
        lsem, ws, wr = scratch[:3]

        def source(to):
            return p_ref.at[to, :, column_block(p.c, quarter)]

        def view(d, q):
            return w_ref.at[lax.rem(p.f - d + size, size), :, column_block(q, quarter)]

        def local():
            return pltpu.make_async_copy(source(p.f), view(0, p.c), lsem)

        def move(d):
            to = lax.rem(p.f + d, size)
            return rcopy(source(to), view(0, p.c), ws.at[d], wr.at[d], {"fsdp": to})

        def came(d):
            ref = view(d, p.c)
            rcopy(ref, ref, ws.at[d], wr.at[d], {"fsdp": lax.rem(p.f + d, size)}).wait_recv()

        share = Share(p, view, size, scratch[3:])
        local().start()
        for d in range(1, size):
            move(d).start()
        share.send(0, source(p.f))
        yield
        for d in range(1, size):
            came(d)
            share.send(d)
            if d % 2 == 0:
                yield
        for d in range(size):
            share.forward(d)
            if d % 4 == 3:
                yield
        local().wait()
        share.finish()
        for d in range(1, size):
            move(d).wait_send()

    return Job(
        run,
        [(packed, ANY)] if held is None else [],
        [(like((size, depth, total), packed.dtype), ANY)],
        [DMA, DMA((size,)), DMA((size,))] + share_sems(size),
    )


def spread_job(x, size):
    def run(p, ins, outs, scratch):
        (x_ref,), (o_ref,) = ins, outs
        lsem, ss, rs = scratch

        def copy(d):
            to = {"fsdp": lax.rem(p.f + d, size)}
            return rcopy(x_ref, o_ref.at[p.f], ss.at[d], rs.at[d], to)

        def local():
            return pltpu.make_async_copy(x_ref, o_ref.at[p.f], lsem)

        local().start()
        for d in range(1, size):
            copy(d).start()
        yield
        local().wait()
        for d in range(1, size):
            copy(d).wait()

    return Job(
        run,
        [(x, ANY)],
        [(like((size,) + x.shape, x.dtype), ANY)],
        [DMA, DMA((size,)), DMA((size,))],
    )


def exchange_job(x, size, rows=None):
    blocks = x.shape if rows is None else (size, rows, x.shape[1] // size)

    def run(p, ins, outs, scratch):
        (x_ref,), (o_ref,) = ins, outs
        lsem, ss, rs = scratch

        def block(to):
            if rows is None:
                return x_ref.at[to]
            return x_ref.at[:rows, column_block(to, blocks[2])]

        def copy(d):
            to = lax.rem(p.f + d, size)
            return rcopy(block(to), o_ref.at[p.f], ss.at[d], rs.at[d], {"fsdp": to})

        def local():
            return pltpu.make_async_copy(block(p.f), o_ref.at[p.f], lsem)

        local().start()
        for d in range(1, size):
            copy(d).start()
        yield
        local().wait()
        for d in range(1, size):
            copy(d).wait()

    return Job(
        run, [(x, ANY)], [(like(blocks, x.dtype), ANY)], [DMA, DMA((size,)), DMA((size,))]
    )


def ctx_gather_job(x):
    def run(p, ins, outs, scratch):
        (x_ref,), (o_ref,) = ins, outs
        share = Share(p, lambda d, q: o_ref.at[q], 1, scratch[1:])

        def local():
            return pltpu.make_async_copy(x_ref, o_ref.at[p.c], scratch[0])

        def first(to, ss, rs):
            return rcopy(x_ref, o_ref.at[p.c], ss.at[0], rs.at[0], {"ctx": to})

        local().start()
        first(p.far, share.fs, share.fr).start()
        first(p.near, share.ns, share.nr).start()
        yield
        share.forward(0)
        yield
        local().wait()
        share.finish()

    return Job(
        run, [(x, ANY)], [(like((4,) + x.shape, x.dtype), ANY)], [DMA] + share_sems(1)
    )


class Halve:
    def __init__(self, p, source, bufs, sems):
        self.p, self.source = p, source
        self.own, self.got, self.away, self.total = bufs
        self.ls, self.ns, self.nr, self.fs, self.fr = sems
        self.count, self.rows = self.total.shape[:2]

    def local(self, i):
        q = self.p.c if i == 0 else self.p.far
        return pltpu.make_async_copy(self.source(q), self.own.at[i], self.ls.at[i])

    def to_near(self, i):
        q = self.p.near if i == 0 else self.p.other
        return rcopy(
            self.source(q), self.got.at[i], self.ns.at[i], self.nr.at[i], {"ctx": self.p.near}
        )

    def index(self, k):
        return lax.rem(self.p.f + k, self.count) if self.count == self.p.size else k

    def to_far(self, k):
        j = self.index(k)
        return rcopy(
            self.own.at[1, j], self.away.at[j], self.fs.at[k], self.fr.at[k], {"ctx": self.p.far}
        )

    def start(self):
        for i in (1, 0):
            self.local(i).start()
        for i in (1, 0):
            self.to_near(i).start()

    def send(self):
        self.local(1).wait()
        self.to_near(1).wait_recv()
        for k in range(self.count):
            own = self.own.at[1, self.index(k)]
            add_blocks(own, [own, self.got.at[1, self.index(k)]], bf16, self.rows)
            self.to_far(k).start()

    def mine(self):
        self.local(0).wait()
        self.to_near(0).wait_recv()

    def block(self, k):
        self.to_far(k).wait_recv()
        j = self.index(k)
        add_blocks(
            self.total.at[j],
            [self.own.at[0, j], self.got.at[0, j], self.away.at[j]],
            bf16,
            self.rows,
        )

    def finish(self):
        for i in range(2):
            self.to_near(i).wait_send()
        for j in range(self.count):
            self.to_far(j).wait_send()


def halve_scratch(count, rows, cols, total=True):
    return [
        pltpu.VMEM((2, count, rows, cols), bf16),
        pltpu.VMEM((2, count, rows, cols), bf16),
        pltpu.VMEM((count, rows, cols), bf16),
    ] + [pltpu.VMEM((count, rows, cols), bf16)] * total + [
        DMA((2,)),
        DMA((2,)),
        DMA((2,)),
        DMA((count,)),
        DMA((count,)),
    ]


def halve_job(x, columns=True):
    n, rows, cols = x.shape
    shape = (n, rows, cols // 4) if columns else (n // 4, rows, cols)

    def run(p, ins, outs, scratch):
        (x_ref,), (o_ref,) = ins, outs

        def source(q):
            if columns:
                return x_ref.at[:, :, column_block(q, shape[2])]
            return x_ref.at[pl.ds(q * shape[0], shape[0])]

        halve = Halve(p, source, list(scratch[:3]) + [o_ref], scratch[3:])
        halve.start()
        yield
        halve.send()
        yield
        halve.mine()
        for j in range(shape[0]):
            halve.block(j)
            if j % 2 == 1:
                yield
        halve.finish()

    return Job(run, [(x, ANY)], [(like(shape, bf16), VM)], halve_scratch(*shape, total=False))


def home_job(wgrad, size):
    _, depth, total = wgrad.shape
    quarter = total // 4

    def run(p, ins, outs, scratch):
        (w_ref,), (h_ref,) = ins, outs
        halve = Halve(
            p, lambda q: w_ref.at[:, :, column_block(q, quarter)], scratch[:4], scratch[4:9]
        )
        lsem, ws, wr = scratch[9:12]

        def view(d, q):
            return h_ref.at[lax.rem(p.f - d + size, size), :, column_block(q, quarter)]

        def local():
            return pltpu.make_async_copy(halve.total.at[p.f], view(0, p.c), lsem)

        def move(d):
            to = lax.rem(p.f + d, size)
            return rcopy(halve.total.at[to], view(0, p.c), ws.at[d], wr.at[d], {"fsdp": to})

        def came(d):
            ref = view(d, p.c)
            rcopy(ref, ref, ws.at[d], wr.at[d], {"fsdp": lax.rem(p.f + d, size)}).wait_recv()

        share = Share(p, view, size, scratch[12:])
        halve.start()
        yield
        halve.send()
        yield
        halve.mine()
        for k in range(size):
            halve.block(k)
            if k == 0:
                local().start()
                share.send(0, halve.total.at[p.f])
            else:
                move(k).start()
            if k % 2 == 1:
                yield
        for d in range(1, size):
            came(d)
            share.send(d)
            if d % 2 == 0:
                yield
        for d in range(size):
            share.forward(d)
            if d % 4 == 3:
                yield
        local().wait()
        share.finish()
        halve.finish()
        for d in range(1, size):
            move(d).wait_send()

    return Job(
        run,
        [(wgrad, ANY)],
        [(like((size, depth, total), bf16), ANY)],
        halve_scratch(size, depth, quarter)
        + [DMA, DMA((size,)), DMA((size,))]
        + share_sems(size),
    )


def deliver_job(piece, size):
    _, depth, quarter = piece.shape

    def run(p, ins, outs, scratch):
        (x_ref,), (h_ref,) = ins, outs
        lsem, ws, wr = scratch[:3]

        def view(d, q):
            return h_ref.at[lax.rem(p.f - d + size, size), :, column_block(q, quarter)]

        def local():
            return pltpu.make_async_copy(x_ref.at[p.f], view(0, p.c), lsem)

        def move(d):
            to = lax.rem(p.f + d, size)
            return rcopy(x_ref.at[to], view(0, p.c), ws.at[d], wr.at[d], {"fsdp": to})

        def came(d):
            ref = view(d, p.c)
            rcopy(ref, ref, ws.at[d], wr.at[d], {"fsdp": lax.rem(p.f + d, size)}).wait_recv()

        share = Share(p, view, size, scratch[3:])
        local().start()
        for d in range(1, size):
            move(d).start()
        share.send(0, x_ref.at[p.f])
        yield
        for d in range(1, size):
            came(d)
            share.send(d)
            if d % 4 == 3:
                yield
        for d in range(size):
            share.forward(d)
            if d % 4 == 3:
                yield
        local().wait()
        share.finish()
        for d in range(1, size):
            move(d).wait_send()

    return Job(
        run,
        [(piece, ANY)],
        [(like((size, depth, 4 * quarter), bf16), ANY)],
        [DMA, DMA((size,)), DMA((size,))] + share_sems(size),
    )


def ctx_sum_job(x):
    rows, cols = x.shape[0] // 4, x.shape[1]
    x = x.reshape(4, rows, cols)

    def run(p, ins, outs, scratch):
        (x_ref,), (o_ref,) = ins, outs
        halve = Halve(p, lambda q: x_ref.at[pl.ds(q, 1)], scratch[:4], scratch[4:9])
        share = Share(p, lambda d, q: o_ref.at[q], 1, scratch[10:])
        halve.start()
        yield
        halve.send()
        yield
        halve.mine()
        halve.block(0)
        share.send(0, halve.total.at[0])

        def local():
            return pltpu.make_async_copy(halve.total.at[0], o_ref.at[p.c], scratch[9])

        local().start()
        yield
        share.forward(0)
        yield
        local().wait()
        share.finish()
        halve.finish()

    return Job(
        run,
        [(x, ANY)],
        [(like((4, rows, cols), bf16), ANY)],
        halve_scratch(1, rows, cols) + [DMA] + share_sems(1),
    )


def sum_job(partial, size):
    rows, tokens = partial.shape[0], partial.shape[1] // size

    def run(p, ins, outs, scratch):
        (p_ref,), (o_ref,) = ins, outs
        buf, ss, rs, gs, gr = scratch

        def at(i):
            return pl.ds(pl.multiple_of(i * tokens, 128), tokens)

        def first(d):
            to = lax.rem(p.f + d, size)
            return rcopy(p_ref.at[:, at(to)], buf.at[d], ss.at[d], rs.at[d], {"fsdp": to})

        def second(d):
            to = lax.rem(p.f + d, size)
            ref = o_ref.at[:, at(p.f)]
            return rcopy(ref, ref, gs.at[d], gr.at[d], {"fsdp": to})

        def came(d):
            ref = o_ref.at[:, at(lax.rem(p.f - d + size, size))]
            rcopy(ref, ref, gs.at[d], gr.at[d], {"fsdp": lax.rem(p.f + d, size)}).wait_recv()

        for d in range(1, size):
            first(d).start()
        yield
        total = p_ref[:, at(p.f)].astype(f32)
        for d in range(1, size):
            first(d).wait_recv()
            total += buf[d].astype(f32)
        o_ref[:, at(p.f)] = total.astype(bf16)
        for d in range(1, size):
            second(d).start()
        yield
        for d in range(1, size):
            came(d)
        for d in range(1, size):
            first(d).wait_send()
            second(d).wait_send()

    return Job(
        run,
        [(partial, VM)],
        [(like(partial.shape, bf16), VM)],
        [pltpu.VMEM((size, rows, tokens), bf16)] + [DMA((size,))] * 4,
    )


def all_sum_job(x, size, held):
    rows, cols = x.shape[1:]

    def run(p, ins, outs, scratch):
        (o_ref,), x_ref = outs, held[0]
        buf, mid, far, ss, rs, ts, tr = scratch

        def copy(d):
            to = lax.rem(p.f + d, size)
            return rcopy(x_ref.at[to], buf.at[d], ss.at[d], rs.at[d], {"fsdp": to})

        def swap(i, to):
            return rcopy(mid.at[i], far.at[i], ts.at[i], tr.at[i], {"ctx": to})

        for d in range(1, size):
            copy(d).start()
        yield
        total = x_ref[p.f]
        for d in range(1, size):
            copy(d).wait_recv()
            total += buf[d]
        mid[0] = total
        swap(0, p.near).start()
        yield
        swap(0, p.near).wait_recv()
        mid[1] = mid[0] + far[0]
        swap(1, p.far).start()
        yield
        swap(1, p.far).wait_recv()
        o_ref[...] = mid[1] + far[1]
        for d in range(1, size):
            copy(d).wait_send()
        swap(0, p.near).wait_send()
        swap(1, p.far).wait_send()

    return Job(
        run,
        [],
        [(like((rows, cols), f32), VM)],
        [pltpu.VMEM((size, rows, cols), f32)]
        + [pltpu.VMEM((2, rows, cols), f32)] * 2
        + [DMA((size,)), DMA((size,)), DMA((2,)), DMA((2,))],
    )


UNROLL = 8
LN2 = 0.6931471805599453


def steps(length, body, init):
    count = UNROLL if length % UNROLL == 0 else 1

    def some(i, carry):
        for j in range(count):
            carry = body(i * count + j, carry)
        return carry

    return lax.fori_loop(0, length // count, some, init)


class Scan:
    def __init__(self, streams, length, chan):
        self.width = math.gcd(streams, 8)
        self.groups, self.tiles, self.length = streams // self.width, chan // 128, length
        self.pieces = 2 * self.groups * self.tiles

    def piece(self, i):
        tile = lax.rem(i, self.tiles)
        rest = i // self.tiles
        return lax.rem(rest, self.groups), rest // self.groups, tile

    def lanes(self, tile):
        return pl.ds(pl.multiple_of(tile * 128, 128), 128)

    def rows(self, group, block, o):
        first = group * (self.width * 2 * self.length) + block * self.length + o
        return pl.ds(first, self.width, stride=2 * self.length)

    def spread(self, wr, group, block, out, column):
        def body(o, carry):
            values = wr[self.rows(group, block, o), :]
            for n in range(NS):
                out[o, n] = jnp.broadcast_to(
                    values[:, column + n : column + n + 1], (self.width, 128)
                )
            return carry

        steps(self.length, body, 0)

    def tiled(self):
        return pltpu.VMEM((self.tiles, self.groups * self.width * 2 * self.length, 128), f32)

    def tile_copies(self, flat, tiled, sems, out=False):
        copies = []
        for t in range(self.tiles):
            there = flat.at[:, t * 128 : (t + 1) * 128]
            pair = (tiled.at[t], there) if out else (there, tiled.at[t])
            copies.append(pltpu.make_async_copy(*pair, sems.at[t]))
        return copies

    def zero(self):
        return jnp.zeros((self.width, 128), f32)

    def link(self, order, b, ends, group, lanes, rates):
        at = order[b]
        total = ends[at, group, NS, :, lanes].astype(f32)
        return at, [jnp.exp2(total * rate) for rate in rates]

    def link_shape(self, blocks, chan, extra):
        return (blocks, self.groups, NS + extra, self.width, chan)


def hosted(loops, jobs, size, cid, name, ins, outs, scratch, plan):
    n_in, n_out = len(ins), len(outs)
    job_in = sum(len(job.ins) for job in jobs)
    job_out = sum(len(job.outs) for job in jobs)

    def kernel(*refs):
        place = Place(size)
        place.greet()
        own_in, refs = refs[:n_in], refs[n_in:]
        ins_, refs = part(refs[:job_in], jobs, "ins"), refs[job_in:]
        own_out, refs = refs[:n_out], refs[n_out:]
        outs_, refs = part(refs[:job_out], jobs, "outs"), refs[job_out:]
        own_scratch, refs = refs[: len(scratch)], refs[len(scratch) :]
        scratch_ = part(refs, jobs, "scratch")
        moving = Moving(
            [job.steps(place, i, o, s) for job, i, o, s in zip(jobs, ins_, outs_, scratch_)]
        )
        for at, stage in enumerate(loops(place, own_in, own_out, own_scratch)):
            for which in plan.get(at, ()):
                moving.step(which)
            if callable(stage):
                stage()
                continue
            count, body = stage

            def whole(i, carry):
                body(i)
                for k in range(count):
                    if plan.get((at, k)):
                        @pl.when(i == k)
                        def _():
                            for which in plan[at, k]:
                                moving.step(which)

                return carry

            lax.fori_loop(0, count, whole, 0)
        for which in plan.get("end", ()):
            moving.step(which)
        moving.drain()

    got = pl.pallas_call(
        kernel,
        out_shape=[shape for shape, _ in outs] + [shape for job in jobs for shape, _ in job.outs],
        in_specs=[spec for _, spec in ins] + [spec for job in jobs for _, spec in job.ins],
        out_specs=[spec for _, spec in outs] + [spec for job in jobs for _, spec in job.outs],
        scratch_shapes=list(scratch) + [item for job in jobs for item in job.scratch],
        compiler_params=params(cid, 63 << 20),
        name=name,
    )(*[array for array, _ in ins], *[array for job in jobs for array, _ in job.ins])
    return got[:n_out], part(got[n_out:], jobs, "outs")


SM = pl.BlockSpec(memory_space=pltpu.SMEM)


def scan_forward(order, dt, x, wr, rate2, streams, jobs, size, cid, plan):
    chan = dt.shape[1]
    scan = Scan(streams, dt.shape[0] // streams // 2, chan)
    blocks = order.shape[0] - 2
    length = scan.length

    def loops(p, ins, outs, scratch):
        order_ref, dt_flat, x_flat, wr_ref, rate_ref = ins
        y_flat, s_ref, ends_ref = outs
        wb, rb, dt_ref, x_ref, y_ref, dt_sem, x_sem, y_sem = scratch[:8]
        share = Share(p, lambda d, q: ends_ref.at[pl.ds(2 * q, 2)], 1, scratch[8:])

        def load():
            copies = scan.tile_copies(dt_flat, dt_ref, dt_sem)
            copies += scan.tile_copies(x_flat, x_ref, x_sem)
            for copy in copies:
                copy.start()
            for copy in copies:
                copy.wait()

        def store():
            copies = scan.tile_copies(y_flat, y_ref, y_sem, True)
            for copy in copies:
                copy.start()
            for copy in copies:
                copy.wait()

        def ends(i):
            group, block, tile = scan.piece(i)
            lanes = scan.lanes(tile)

            @pl.when(tile == 0)
            def _():
                scan.spread(wr_ref, group, block, wb, 0)

            rates = [rate_ref[n : n + 1, lanes] for n in range(NS)]

            def body(o, carry):
                total, states = carry
                at = scan.rows(group, block, o)
                step = dt_ref[tile, at, :]
                pushed = step * x_ref[tile, at, :]
                states = tuple(
                    jnp.exp2(step * rates[n]) * states[n] + wb[o, n] * pushed for n in range(NS)
                )
                return (total + step, states)

            total, states = steps(length, body, (scan.zero(), (scan.zero(),) * NS))
            mine = 2 * p.c + block
            for n in range(NS):
                ends_ref[mine, group, n, :, lanes] = states[n].astype(bf16)
            ends_ref[mine, group, NS, :, lanes] = total.astype(bf16)

        def send():
            share.send(0)

        def arrive():
            share.forward(0)
            share.finish()

        def forward(i):
            group, block, tile = scan.piece(i)
            lanes = scan.lanes(tile)

            @pl.when(tile == 0)
            def _():
                scan.spread(wr_ref, group, block, wb, 0)
                scan.spread(wr_ref, group, block, rb, NS)

            rates = [rate_ref[n : n + 1, lanes] for n in range(NS)]
            mine = order_ref[blocks + block]

            def link(b, states):
                at, decays = scan.link(order_ref, b, ends_ref, group, lanes, rates)
                return tuple(
                    jnp.where(
                        b < mine,
                        decays[n] * states[n] + ends_ref[at, group, n, :, lanes].astype(f32),
                        states[n],
                    )
                    for n in range(NS)
                )

            states = lax.fori_loop(0, blocks - 1, link, (scan.zero(),) * NS)
            for n in range(NS):
                s_ref[block, group, n, :, lanes] = states[n]

            def body(o, states):
                at = scan.rows(group, block, o)
                step = dt_ref[tile, at, :]
                pushed = step * x_ref[tile, at, :]
                states = tuple(
                    jnp.exp2(step * rates[n]) * states[n] + wb[o, n] * pushed for n in range(NS)
                )
                total = [rb[o, n] * states[n] for n in range(NS)]
                while len(total) > 1:
                    total = [total[j] + total[j + 1] for j in range(0, len(total), 2)]
                y_ref[tile, at, :] = total[0]
                return states

            steps(length, body, states)

        return [load, (scan.pieces, ends), send, arrive, (scan.pieces, forward), store]

    spread = pltpu.VMEM((length, NS, scan.width, 128), f32)
    return hosted(
        loops,
        jobs,
        size,
        cid,
        "scan_forward",
        [(order, SM), (dt, ANY), (x, ANY), (wr, VM), (rate2, VM)],
        [
            (like(dt.shape, f32), ANY),
            (like(scan.link_shape(2, chan, 0), f32), VM),
            (like(scan.link_shape(blocks, chan, 1), bf16), VM),
        ],
        [spread, spread] + [scan.tiled()] * 3 + [DMA((scan.tiles,))] * 3 + share_sems(1),
        plan,
    )


def scan_backward(order, dt, x, g, wr, rate2, starts, ends, streams, jobs, size, cid, plan):
    chan = dt.shape[1]
    scan = Scan(streams, dt.shape[0] // streams // 2, chan)
    blocks = order.shape[0] - 2
    length, width = scan.length, scan.width

    def loops(p, ins, outs, scratch):
        order_ref, dt_flat, x_flat, g_flat, wr_ref, rate_ref, start_ref, ends_ref = ins
        sb_flat, cw_flat, wrb_ref, dec_ref = outs
        backs_ref, wb, rb, kept, decays, wparts, rparts, sums = scratch[:8]
        dt_ref, x_ref, g_ref, sb_ref, cw_ref, dt_sem, x_sem, g_sem, sb_sem, cw_sem = scratch[8:18]
        share = Share(p, lambda d, q: backs_ref.at[pl.ds(2 * q, 2)], 1, scratch[18:])

        def load():
            copies = scan.tile_copies(dt_flat, dt_ref, dt_sem)
            copies += scan.tile_copies(x_flat, x_ref, x_sem)
            copies += scan.tile_copies(g_flat, g_ref, g_sem)
            for copy in copies:
                copy.start()
            for copy in copies:
                copy.wait()

        def store():
            copies = scan.tile_copies(sb_flat, sb_ref, sb_sem, True)
            copies += scan.tile_copies(cw_flat, cw_ref, cw_sem, True)
            for copy in copies:
                copy.start()
            for copy in copies:
                copy.wait()

        def backs(i):
            group, block, tile = scan.piece(i)
            lanes = scan.lanes(tile)

            @pl.when(tile == 0)
            def _():
                scan.spread(wr_ref, group, block, rb, NS)

            rates = [rate_ref[n : n + 1, lanes] for n in range(NS)]

            def body(j, carries):
                o = length - 1 - j
                at = scan.rows(group, block, o)
                step = dt_ref[tile, at, :]
                grad = g_ref[tile, at, :]
                return tuple(
                    jnp.exp2(step * rates[n]) * (carries[n] + rb[o, n] * grad) for n in range(NS)
                )

            carries = steps(length, body, (scan.zero(),) * NS)
            mine = 2 * p.c + block
            for n in range(NS):
                backs_ref[mine, group, n, :, lanes] = carries[n].astype(bf16)

        def send():
            share.send(0)

        def arrive():
            share.forward(0)
            share.finish()

        def backward(i):
            group, block, tile = scan.piece(i)
            lanes = scan.lanes(tile)

            @pl.when(tile == 0)
            def _():
                scan.spread(wr_ref, group, block, wb, 0)
                scan.spread(wr_ref, group, block, rb, NS)
                sums[...] = jnp.zeros_like(sums)

            rates = [rate_ref[n : n + 1, lanes] for n in range(NS)]

            def forward(o, states):
                at = scan.rows(group, block, o)
                step = dt_ref[tile, at, :]
                pushed = step * x_ref[tile, at, :]
                new = []
                for n in range(NS):
                    decay = jnp.exp2(step * rates[n])
                    decays[o, n] = decay
                    kept[o, n] = states[n]
                    new.append(decay * states[n] + wb[o, n] * pushed)
                return tuple(new)

            first = tuple(start_ref[block, group, n, :, lanes] for n in range(NS))
            last = steps(length, forward, first)
            for n in range(NS):
                kept[length, n] = last[n]

            mine = order_ref[blocks + block]

            def link(j, carries):
                b = blocks - 1 - j
                at, decay = scan.link(order_ref, b, ends_ref, group, lanes, rates)
                return tuple(
                    jnp.where(
                        b > mine,
                        backs_ref[at, group, n, :, lanes].astype(f32) + decay[n] * carries[n],
                        carries[n],
                    )
                    for n in range(NS)
                )

            carries = lax.fori_loop(0, blocks - 1, link, (scan.zero(),) * NS)
            for n in range(NS):
                dec_ref[block, group, n, :, lanes] = scan.zero()

            def body(j, carries):
                o = length - 1 - j
                at = scan.rows(group, block, o)
                step = dt_ref[tile, at, :]
                value = x_ref[tile, at, :]
                grad = g_ref[tile, at, :]
                pushed = step * value
                slope, pulled, new = [], [], []
                to = pl.ds(pl.multiple_of(o * width, width), width)
                for n in range(NS):
                    full = carries[n] + rb[o, n] * grad
                    moved = decays[o, n] * full
                    new.append(moved)
                    back = moved * kept[o, n]
                    slope.append(back * rates[n])
                    dec_ref[block, group, n, :, lanes] += back * step
                    pulled.append(full * wb[o, n])
                    wparts[to, n * 128 : (n + 1) * 128] = full * pushed
                    rparts[to, n * 128 : (n + 1) * 128] = kept[o + 1, n] * grad
                while len(slope) > 1:
                    slope = [slope[j] + slope[j + 1] for j in range(0, len(slope), 2)]
                    pulled = [pulled[j] + pulled[j + 1] for j in range(0, len(pulled), 2)]
                sb_ref[tile, at, :] = slope[0] * LN2 + pulled[0] * value
                cw_ref[tile, at, :] = pulled[0]
                return tuple(new)

            steps(length, body, carries)
            source = lax.broadcasted_iota(jnp.int32, (NS * 128, 128), 0) // 128
            target = lax.broadcasted_iota(jnp.int32, (NS * 128, 128), 1)
            pick_w = jnp.where(source == target, 1.0, 0.0).astype(bf16)
            pick_r = jnp.where(source + NS == target, 1.0, 0.0).astype(bf16)
            sums[...] += jnp.dot(
                wparts[...].astype(bf16), pick_w, preferred_element_type=f32
            ) + jnp.dot(rparts[...].astype(bf16), pick_r, preferred_element_type=f32)

            @pl.when(tile == scan.tiles - 1)
            def _():
                def out(o, carry):
                    wrb_ref[scan.rows(group, block, o), :] = sums[
                        pl.ds(pl.multiple_of(o * width, width), width), :
                    ]
                    return carry

                steps(length, out, 0)

        return [load, (scan.pieces, backs), send, arrive, (scan.pieces, backward), store]

    spread = pltpu.VMEM((length, NS, width, 128), f32)
    parts = pltpu.VMEM((length * width, NS * 128), f32)
    return hosted(
        loops,
        jobs,
        size,
        cid,
        "scan_backward",
        [
            (order, SM), (dt, ANY), (x, ANY), (g, ANY), (wr, VM), (rate2, VM), (starts, VM), (ends, VM),
        ],
        [
            (like(dt.shape, f32), ANY),
            (like(dt.shape, f32), ANY),
            (like((dt.shape[0], 128), f32), VM),
            (like(scan.link_shape(2, chan, 0), f32), VM),
        ],
        [
            pltpu.VMEM(scan.link_shape(blocks, chan, 0), bf16),
            spread,
            spread,
            pltpu.VMEM((length + 1, NS, width, 128), f32),
            spread,
            parts,
            parts,
            pltpu.VMEM((length * width, 128), f32),
        ]
        + [scan.tiled()] * 5
        + [DMA((scan.tiles,))] * 5
        + share_sems(1),
        plan,
    )


def attention_forward(q_t, k, v_t, bias_t, jobs, size, cid, plan):
    rows = q_t.shape[1]
    group = H // KV

    def loops(p, ins, outs, scratch):
        q_ref, k_ref, v_ref, bias_ref = ins
        o_ref, log_ref = outs

        def head(h):
            at = pl.ds(pl.multiple_of(h * HD, HD), HD)
            g = h // group
            scores = (
                jnp.dot(k_ref[g], q_ref[at, :], preferred_element_type=f32) * score_scale
                + bias_ref[...]
            )
            largest = jnp.max(scores, axis=0, keepdims=True)
            expo = jnp.exp(scores - largest)
            total = jnp.sum(expo, axis=0, keepdims=True)
            probs = (expo * (1.0 / total)).astype(bf16)
            values = v_ref[pl.ds(pl.multiple_of(g * HD, HD), HD), :]
            o_ref[at, :] = jnp.dot(values, probs, preferred_element_type=f32).astype(bf16)
            log_ref[pl.ds(h, 1), :] = largest + jnp.log(total)

        return [(H, head)]

    return hosted(
        loops,
        jobs,
        size,
        cid,
        "attention_forward",
        [(q_t, VM), (k, VM), (v_t, VM), (bias_t, VM)],
        [(like(q_t.shape, bf16), VM), (like((H, rows), f32), VM)],
        [],
        plan,
    )


def attention_backward(q_t, k, k_t, v, bias_t, log_total, dout_t, jobs, size, cid, plan):
    group = H // KV
    keys = k.shape[1]

    def loops(p, ins, outs, scratch):
        q_ref, k_ref, kt_ref, v_ref, bias_ref, log_ref, do_ref = ins
        dq_ref, dkv_ref = outs
        contract = (((1,), (1,)), ((), ()))

        def zero():
            dkv_ref[...] = jnp.zeros_like(dkv_ref)

        def head(h):
            at = pl.ds(pl.multiple_of(h * HD, HD), HD)
            g = h // group
            to_k = pl.ds(pl.multiple_of(g * HD, HD), HD)
            to_v = pl.ds(pl.multiple_of((KV + g) * HD, HD), HD)
            query, dout = q_ref[at, :], do_ref[at, :]
            scores = (
                jnp.dot(k_ref[g], query, preferred_element_type=f32) * score_scale + bias_ref[...]
            )
            probs = jnp.exp(scores - log_ref[pl.ds(h, 1), :])
            back = jnp.dot(v_ref[g], dout, preferred_element_type=f32)
            centre = jnp.sum(probs * back, axis=0, keepdims=True)
            score_back = (probs * (back - centre)).astype(bf16)
            dq_ref[at, :] = (
                jnp.dot(kt_ref[to_k, :], score_back, preferred_element_type=f32) * score_scale
            ).astype(bf16)
            dkv_ref[to_k, :] += score_scale * lax.dot_general(
                query, score_back, contract, preferred_element_type=f32
            )
            dkv_ref[to_v, :] += lax.dot_general(
                dout, probs.astype(bf16), contract, preferred_element_type=f32
            )

        return [zero, (H, head)]

    return hosted(
        loops,
        jobs,
        size,
        cid,
        "attention_backward",
        [
            (q_t, VM), (k, VM), (k_t, VM), (v, VM), (bias_t, VM), (log_total, VM), (dout_t, VM),
        ],
        [(like(q_t.shape, bf16), VM), (like((2 * KV * HD, keys), f32), VM)],
        [],
        plan,
    )


def start_exchange(rows_in, gains, first, ffn, first_pack, ffn_pack, size, cid):
    depth = first[0].shape[0]
    n_first = len(first)
    weights = list(first) + list(ffn)
    (first_cuts, first_at, first_total), (ffn_cuts, ffn_at, ffn_total) = first_pack, ffn_pack
    held = []

    def loops(p, ins, outs, scratch):
        (packed_ref,) = outs
        mine, sems = scratch[1 : 1 + len(weights)], scratch[-1]
        held.append(scratch[0])

        def load(which):
            return pltpu.make_async_copy(ins[which], mine[which], sems.at[which])

        def begin():
            for which in range(len(weights)):
                load(which).start()

        def pack_first():
            for which in range(n_first):
                load(which).wait()
            pack_columns(mine[:n_first], scratch[0], first_cuts, first_at, size)

        def pack_ffn():
            for which in range(n_first, len(weights)):
                load(which).wait()
            pack_columns(mine[n_first:], packed_ref, ffn_cuts, ffn_at, size)

        return [begin, pack_first, pack_ffn]

    packed = like((size, depth, first_total), bf16)
    return hosted(
        loops,
        [gather_job(rows_in, size), spread_job(gains, size), move_job(packed, size, held)],
        size,
        cid,
        "start",
        [(item, ANY) for item in weights],
        [(like((size, depth, ffn_total), bf16), VM)],
        [pltpu.VMEM(packed.shape, bf16)]
        + [pltpu.VMEM(item.shape, bf16) for item in weights]
        + [DMA((len(weights),))],
        PLAN_START,
    )


def ffn_sums(low, back, hidden, grads, jobs, size, cid):
    rows, width = low.shape
    total, units = back.shape[1], hidden.shape[1]
    depth, quarter = width // size, total // 4
    contract = (((0,), (0,)), ((), ()))

    def loops(p, ins, outs, scratch):
        low_ref, back_ref, hidden_ref, grads_ref = ins
        quarter_ref, down_ref = outs
        whole = scratch[0]
        halve = Halve(
            p,
            lambda q: whole.at[:, :, column_block(q, quarter)],
            list(scratch[1:4]) + [quarter_ref],
            scratch[4:],
        )

        def tile(i):
            lanes = column_block(i, 128)
            got = lax.dot_general(
                low_ref[...], back_ref[:, lanes], contract, preferred_element_type=f32
            )
            for f in range(size):
                whole[f, :, lanes] = got[f * depth : (f + 1) * depth, :].astype(bf16)

        def down_tile(i):
            lanes = column_block(i, 128)
            down_ref[pl.ds(pl.multiple_of(i * 128, 128), 128), :] = lax.dot_general(
                hidden_ref[:, lanes], grads_ref[...], contract, preferred_element_type=f32
            ).astype(bf16)

        def sums():
            halve.mine()
            for k in range(size):
                halve.block(k)
            halve.finish()

        return [
            (total // 128, tile), halve.start, halve.send, (units // 128, down_tile), sums,
        ]

    return hosted(
        loops,
        jobs,
        size,
        cid,
        "ffn_sums",
        [(low, VM), (back, VM), (hidden, VM), (grads, VM)],
        [(like((size, depth, quarter), bf16), VM), (like((units, width), bf16), VM)],
        [pltpu.VMEM((size, depth, total), bf16)] + halve_scratch(size, depth, quarter, False),
        PLAN_FFN,
    )


def finish(wgrad, back, mat, normed, gain, gain_rows, small, ffn_home, ffn_pack, shapes, size, cid):
    rows_all, total = back.shape
    width = mat.shape[0]
    rows = rows_all // size
    cuts, offsets = ffn_pack
    held_rows, held_gains = [], []
    contract = (((1,), (1,)), ((), ()))
    n_out = len(shapes)

    def loops(p, ins, outs, scratch):
        back_ref, mat_ref, normed_ref, gain_ref, gain_rows_ref, home_ref = ins
        part_ref, total_ref, gains_ref, home_sem, out_sem, home_in = scratch[:6]
        laid = scratch[6:]
        held_rows.append(part_ref)
        held_gains.append(gains_ref)

        def fetch():
            return pltpu.make_async_copy(home_ref, home_in, home_sem)

        def store(i):
            return pltpu.make_async_copy(laid[i], outs[i], out_sem.at[i])

        def begin():
            fetch().start()
            total_ref[...] = jnp.zeros_like(total_ref)

        def block(i):
            at = pl.ds(pl.multiple_of(i * rows, rows), rows)
            got = lax.dot_general(
                back_ref[at, :], mat_ref[...], contract, preferred_element_type=f32
            ).astype(bf16)
            part_ref[i] = got
            product = got.astype(f32) * normed_ref[at, :].astype(f32)
            total_ref[...] += jnp.sum(product, axis=0, keepdims=True)

        def gains():
            gains_ref[...] = gain_rows_ref[...]
            first = (total_ref[...] / gain_ref[...]).astype(f32)
            cols = width // size
            for f in range(size):
                gains_ref[f, 0:1, :] = first[:, f * cols : (f + 1) * cols]

        def lay_out():
            fetch().wait()
            unpack_pieces(home_in, laid, cuts, offsets, size)
            for i in range(n_out):
                store(i).start()

        def stored():
            for i in range(n_out):
                store(i).wait()

        return [begin, (size, block), gains, lay_out, stored]

    part_shape = like((size, rows, width), bf16)
    return hosted(
        loops,
        [
            scatter_job(part_shape, size, held_rows),
            home_job(wgrad, size),
            ctx_sum_job(small),
            all_sum_job(gain_rows, size, held_gains),
        ],
        size,
        cid,
        "finish",
        [(back, VM), (mat, VM), (normed, VM), (gain, VM), (gain_rows, VM), (ffn_home, ANY)],
        [(like(shape, f32), ANY) for shape in shapes],
        [
            pltpu.VMEM(part_shape.shape, bf16),
            pltpu.VMEM((1, width), f32),
            pltpu.VMEM(gain_rows.shape, f32),
            DMA,
            DMA((n_out,)),
            pltpu.VMEM(ffn_home.shape, bf16),
        ]
        + [pltpu.VMEM(shape, f32) for shape in shapes],
        PLAN_FINISH,
    )


PLAN_START = {1: (0, 1), 2: (0, 2), "end": (0, 2)}
PLAN_FORWARD = {
    1: (2, 1),
    (1, 3): (2,),
    (1, 6): (2,),
    2: (0,),
    (4, 0): (2, 1, 1, 1),
    (4, 1): (0, 2),
    (4, 3): (0, 1),
    (4, 5): (0, 1, 2),
    (4, 7): (0,),
}
PLAN_ATTEND = {0: (0,), (0, 6): (0,), (0, 14): (0,), (0, 22): (0,)}
PLAN_FFN = {0: (0,), (0, 7): (0,), 1: (0,), (3, 1): (0,)}
PLAN_ATTEND_BACK = {
    0: (0, 1),
    (1, 5): (1,),
    (1, 9): (0,),
    (1, 16): (0,),
    "end": (0, 1, 1, 1, 0),
}
PLAN_FINISH = {
    1: (1,),
    (1, 1): (1,),
    (1, 3): (1,),
    (1, 5): (1,),
    (1, 7): (1,),
    2: (1, 0, 2),
    3: (0, 1, 3, 2),
    4: (0, 1, 3, 1, 0, 2),
    "end": (1, 1, 0, 3),
}
PLAN_BACKWARD = {
    1: (4, 0, 3),
    (1, 3): (3,),
    (1, 4): (4,),
    (1, 7): (4,),
    3: (),
    (4, 0): (4, 0),
    (4, 1): (4, 1, 0, 3),
    (4, 2): (1, 0, 2),
    (4, 3): (1, 0, 2),
    (4, 4): (1, 0, 3),
    (4, 5): (1, 2),
    (4, 6): (1, 3),
    (4, 7): (2,),
}


def column_grads(x, dy):
    return jnp.einsum("ld,lk->dk", x, dy, preferred_element_type=f32).astype(bf16)


def on_device(
    layer_in,
    out_grad,
    doc_lengths,
    block_deal,
    norm_gains,
    query_weight,
    keyval_weight,
    attn_proj,
    mamba_in,
    conv_taps,
    conv_bias,
    step_bias,
    skip_gain,
    decay_log,
    select_proj,
    step_proj,
    mamba_proj,
    gate_weight,
    up_weight,
    down_weight,
):
    size = lax.axis_size("fsdp")
    n_ctx = lax.axis_size("ctx")
    rows = layer_in.shape[1]
    half_rows = rows // 2
    width = layer_in.shape[2]
    blocks_all = 2 * n_ctx
    group = H // KV
    chan = INNER // size
    q_cols, kv_cols = H * HD // size, 2 * KV * HD // size
    ff_cols = gate_weight.shape[1] // size
    rows_all = size * rows
    ctx_place = lax.axis_index("ctx")
    deal_flat = block_deal.reshape(-1)
    my_blocks = lax.dynamic_slice_in_dim(block_deal, ctx_place, 1, 0)[0]
    offsets = jnp.arange(half_rows, dtype=jnp.int32)
    my_places = (my_blocks[:, None] * half_rows + offsets[None, :]).reshape(-1)
    key_places = (deal_flat[:, None] * half_rows + offsets[None, :]).reshape(-1)
    lengths = doc_lengths[0]
    starts = jnp.cumsum(lengths) - lengths

    def segment(places):
        return jnp.sum((places[:, None] >= starts[None, :]).astype(jnp.int32), axis=1)

    allowed = (key_places[:, None] <= my_places[None, :]) & (
        segment(key_places)[:, None] == segment(my_places)[None, :]
    )
    bias_t = jnp.where(allowed, 0.0, -1e30).astype(f32)
    inverse = jnp.argsort(deal_flat)

    depth = query_weight.shape[0]
    chan_up, qkv_up = up_to(chan, 128), up_to(q_cols + kv_cols, 128)
    ff_up = up_to(ff_cols, 128)
    first_cuts = ((0, 0, q_cols), (1, 0, kv_cols), (2, 0, chan), (2, INNER, chan))
    first_at = (0, q_cols, qkv_up, qkv_up + chan_up)
    first_total = up_to(qkv_up + 2 * chan_up, 128 * n_ctx)
    ffn_cuts = ((0, 0, ff_cols), (1, 0, ff_cols))
    ffn_at = (0, ff_up)
    ffn_total = up_to(2 * ff_up, 128 * n_ctx)
    (ffn_packed,), ((stream_all,), (gain_all,), (first_mat,)) = start_exchange(
        layer_in[0],
        norm_gains,
        (query_weight, keyval_weight, mamba_in),
        (gate_weight, up_weight),
        (first_cuts, first_at, first_total),
        (ffn_cuts, ffn_at, ffn_total),
        size,
        0,
    )
    stream_all = stream_all.reshape(rows_all, width)
    gain_float = jnp.moveaxis(gain_all, 0, 1).reshape(4, width).astype(f32)
    first_mat = first_mat.reshape(width, first_total)
    qkv_mat = first_mat[:, :qkv_up]
    entry_mat = first_mat[:, qkv_up : qkv_up + 2 * chan_up]
    ffn_quarter = ffn_total // n_ctx
    attn_wide = up_to(width, 128 * n_ctx)
    attn_packed = jnp.pad(attn_proj, ((0, 0), (0, attn_wide - width)))
    down_mat = jnp.pad(down_weight, ((0, ff_up - ff_cols), (0, 0)))
    more = chan_up - chan
    taps_mat = jnp.pad(conv_taps, ((0, 0), (0, more)))
    mamba_mat = jnp.pad(mamba_proj, ((0, more), (0, 0)))
    select_mat = jnp.pad(select_proj, ((0, more), (0, 0)))
    step_mat = jnp.pad(step_proj, ((0, 0), (0, more)))
    rate = -jnp.exp(jnp.pad(decay_log, ((0, 0), (0, more))).astype(f32))
    rate2 = rate * 1.4426950408889634
    shift_float, step_shift, skip_float = (
        jnp.pad(item, (0, more)).astype(f32) for item in (conv_bias, step_bias, skip_gain)
    )

    stream = layer_in[0].astype(f32)
    _, inv_in = norm_forward(stream, gain_float[0])
    normed_all, inv_all = norm_forward(stream_all.astype(f32), gain_float[0])
    normed_all = normed_all.astype(bf16)

    qkv_t = jnp.einsum("dk,ld->kl", qkv_mat, normed_all, preferred_element_type=f32).astype(bf16)
    entry = jnp.dot(normed_all, entry_mat, preferred_element_type=f32)
    chan = chan_up
    mixer_in = entry[:, :chan].astype(bf16)
    gate_side = entry[:, chan:]
    mixer_blocks = mixer_in.reshape(size, 2, half_rows, chan)
    tails = mixer_blocks[:, :, half_rows - (CONV - 1) :]
    (qkv,), (tails_all,) = together(
        [exchange_job(qkv_t, size, up_to(q_cols + kv_cols, 8)), ctx_gather_job(tails.reshape(-1, chan))],
        size,
        1,
        "edges",
    )
    query_t = qkv[:, :q_cols].reshape(H * HD, rows)
    keyval_t = qkv[:, q_cols : q_cols + kv_cols].reshape(2 * KV * HD, rows)
    tails_all = tails_all.reshape(n_ctx, size, 2, CONV - 1, chan)

    def in_deal_order(values):
        return jnp.moveaxis(values, 2, 1).reshape((blocks_all,) + (size,) + values.shape[3:])

    def of_blocks(values, index):
        return jnp.moveaxis(jnp.take(values, index, axis=0), 0, 1)

    before_index = inverse[jnp.maximum(my_blocks - 1, 0)]
    has_before = my_blocks > 0
    prior_tail = jnp.where(
        has_before[None, :, None, None],
        of_blocks(in_deal_order(tails_all), before_index),
        jnp.zeros_like(tails),
    )
    padded = jnp.concatenate([prior_tail, mixer_blocks], axis=2).astype(f32)
    taps_float = taps_mat.astype(f32)
    conv_blocks_out = shift_float + sum(
        taps_float[offset] * padded[:, :, offset : offset + half_rows] for offset in range(CONV)
    )
    conv_out = conv_blocks_out.reshape(rows_all, chan)
    signal = jax.nn.silu(conv_out).astype(bf16)
    signal_float = signal.astype(f32)
    selected_part = jnp.einsum(
        "ik,li->kl", select_mat, signal, preferred_element_type=f32
    ).astype(bf16)
    (selected,), (keyvals_all,) = together(
        [sum_job(selected_part, size), ctx_gather_job(keyval_t)], size, 3, "select"
    )
    keyvals_t = keyvals_all.transpose(1, 0, 2).reshape(2 * KV * HD, n_ctx * rows)
    keyvals = keyvals_t.reshape(2 * KV, HD, n_ctx * rows).transpose(0, 2, 1)
    key_groups, value_groups = keyvals[:KV], keyvals[KV:]
    step_low = selected[:RANK].T
    write_read = jnp.pad(selected[RANK:], ((0, 128 - 2 * NS), (0, 0))).T.astype(f32)
    step_pre = jnp.dot(step_low, step_mat, preferred_element_type=f32) + step_shift
    step_sizes = jax.nn.softplus(step_pre)
    order = jnp.concatenate([inverse, my_blocks]).astype(jnp.int32)
    (scan_rows, start_state, ends_all), ((grads_all,), (ffn_mat,), (attn_mat,)) = scan_forward(
        order,
        step_sizes,
        signal_float,
        write_read,
        rate2,
        size,
        [
            gather_job(out_grad[0], size),
            move_job(ffn_packed, size),
            gather_job(attn_packed, size, True),
        ],
        size,
        4,
        PLAN_FORWARD,
    )
    grads_all = grads_all.reshape(rows_all, width)
    ffn_mat = ffn_mat.reshape(width, ffn_total)
    gate_mat, up_mat = ffn_mat[:, :ff_up], ffn_mat[:, ff_up : 2 * ff_up]
    attn_mat = attn_mat.reshape(width, attn_wide)[:, :width]
    scanned = scan_rows + skip_float * signal_float
    gate_act = jax.nn.silu(gate_side)
    mamba_rows = (scanned * gate_act).astype(bf16)
    mamba_part = jnp.dot(mamba_rows, mamba_mat, preferred_element_type=f32).astype(bf16)
    (attn_rows_t, log_totals), ((mamba_out,),) = attention_forward(
        query_t,
        key_groups,
        keyvals_t[KV * HD :],
        bias_t,
        [scatter_job(mamba_part.reshape(size, rows, width), size)],
        size,
        5,
        PLAN_ATTEND,
    )
    attn_out = jnp.einsum("hl,hd->ld", attn_rows_t, attn_mat, preferred_element_type=f32)
    attn_normed, inv_attn = norm_forward(attn_out, gain_float[1])

    mamba_normed, inv_mamba = norm_forward(mamba_out, gain_float[2])
    middle = stream + 0.5 * (attn_normed + mamba_normed)
    ffn_normed, inv_ffn = norm_forward(middle, gain_float[3])
    ((ffn_low,),) = together(
        [gather_job(ffn_normed.astype(bf16), size)], size, 6, "ffn_rows"
    )
    ffn_low = ffn_low.reshape(rows_all, width)
    gate_pre = jnp.dot(ffn_low, gate_mat, preferred_element_type=f32)
    up_pre = jnp.dot(ffn_low, up_mat, preferred_element_type=f32)
    hidden = (jax.nn.silu(gate_pre) * up_pre).astype(bf16)
    down_part = jnp.dot(hidden, down_mat, preferred_element_type=f32).astype(bf16)
    hidden_back = jnp.einsum("ld,fd->lf", grads_all, down_mat, preferred_element_type=f32)
    gate_back = (hidden_back * up_pre * silu_slope(gate_pre)).astype(bf16)
    up_back = (hidden_back * jax.nn.silu(gate_pre)).astype(bf16)
    ffn_back_part = jnp.einsum(
        "lf,df->ld", gate_back, gate_mat, preferred_element_type=f32
    ) + jnp.einsum("lf,df->ld", up_back, up_mat, preferred_element_type=f32)
    ffn_back_low = jnp.concatenate([gate_back, up_back], axis=1)
    ffn_back_low = jnp.pad(ffn_back_low, ((0, 0), (0, ffn_total - 2 * ff_up)))
    ffn_jobs = [scatter_job(ffn_back_part.astype(bf16).reshape(size, rows, width), size)]
    fits = size <= 8
    (ffn_quarter_sum, down_wgrad), ffn_back = ffn_sums(
        ffn_low, ffn_back_low, hidden, grads_all, ffn_jobs * fits, size, 7
    )
    if not fits:
        ffn_back = together(ffn_jobs, size, 14, "ffn_sum")
    ffn_back = ffn_back[0][0]
    middle_part, ffn_gain_grad = norm_backward(ffn_back, middle, inv_ffn, gain_float[3])
    middle_back = out_grad[0].astype(f32) + middle_part
    branch_back = 0.5 * middle_back
    attn_part, attn_gain_grad = norm_backward(branch_back, attn_out, inv_attn, gain_float[1])
    mamba_part_back, mamba_gain_grad = norm_backward(
        branch_back, mamba_out, inv_mamba, gain_float[2]
    )
    attn_back = attn_part.astype(bf16)
    attn_wgrad = jnp.einsum("hl,ld->hd", attn_rows_t, attn_back, preferred_element_type=f32)
    attn_wgrad = jnp.pad(attn_wgrad.astype(bf16), ((0, 0), (0, attn_wide - width)))
    dout_t = jnp.einsum("hd,ld->hl", attn_mat, attn_back, preferred_element_type=f32).astype(bf16)
    (query_back_t, keyval_terms), ((mamba_back,), (attn_quarter,)) = (
        attention_backward(
            query_t,
            key_groups,
            keyvals_t[: KV * HD],
            value_groups,
            bias_t,
            log_totals,
            dout_t,
            [
                gather_job(mamba_part_back.astype(bf16), size),
                halve_job(attn_wgrad.reshape(size, depth, attn_wide)),
            ],
            size,
            8,
            PLAN_ATTEND_BACK,
        )
    )
    mamba_back = mamba_back.reshape(rows_all, width)
    mamba_wgrad = jnp.einsum("li,ld->id", mamba_rows, mamba_back, preferred_element_type=f32)
    mrows_back = jnp.einsum("ld,id->li", mamba_back, mamba_mat, preferred_element_type=f32)
    scan_back = mrows_back * gate_act
    side_back = mrows_back * scanned * silu_slope(gate_side)
    skip_grad = jnp.sum(scan_back * signal_float, axis=0)
    down_jobs = [scatter_job(down_part.reshape(size, rows, width), size)]
    (
        (step_back, carry_writes, read_write_back, decay_sums),
        ((ffn_home,), (attn_piece,), (mamba_share,), (down_share,), *down_out),
    ) = scan_backward(
        order,
        step_sizes,
        signal_float,
        scan_back,
        write_read,
        rate2,
        start_state,
        ends_all,
        size,
        [
            deliver_job(ffn_quarter_sum, size),
            scatter_job(attn_quarter, size),
            ctx_sum_job(mamba_wgrad.astype(bf16)),
            ctx_sum_job(down_wgrad),
        ]
        + down_jobs * fits,
        size,
        9,
        PLAN_BACKWARD,
    )
    if not fits:
        down_out = together(down_jobs, size, 15, "down_sum")
    result = middle + down_out[0][0]
    decay_grad = rate * jnp.sum(decay_sums, axis=(0, 1, 3))
    signal_back = scan_back * skip_float + step_sizes * carry_writes
    read_write_back = read_write_back[:, : 2 * NS]
    pre_back = (step_back * jax.nn.sigmoid(step_pre)).astype(bf16)
    step_wgrad = jnp.einsum("lr,li->ri", step_low, pre_back, preferred_element_type=f32)
    bias_grad = jnp.sum(pre_back.astype(f32), axis=0)
    rank_back = jnp.einsum("li,ri->lr", pre_back, step_mat, preferred_element_type=f32)
    select_part = jnp.concatenate([rank_back, read_write_back], axis=1).astype(bf16).T
    (select_back,), (attn_home,), (keyval_back,) = together(
        [
            sum_job(select_part, size),
            ctx_gather_job(attn_piece.astype(bf16)),
            halve_job(keyval_terms.astype(bf16)[None]),
        ],
        size,
        10,
        "select_back",
    )
    select_back = select_back.T
    select_wgrad = jnp.einsum("li,lk->ik", signal, select_back, preferred_element_type=f32)
    signal_back = signal_back + jnp.einsum(
        "lk,ik->li", select_back, select_mat, preferred_element_type=f32
    )
    conv_back = signal_back * silu_slope(conv_out)
    conv_blocks = conv_back.reshape(size, 2, half_rows, chan)
    taps_grad = jnp.stack(
        [
            jnp.sum(conv_blocks * padded[:, :, offset : offset + half_rows], axis=(0, 1, 2))
            for offset in range(CONV)
        ]
    )
    shift_grad = jnp.sum(conv_back, axis=0)
    padded_back = sum(
        (
            jnp.pad(
                taps_float[offset] * conv_blocks,
                ((0, 0), (0, 0), (offset, CONV - 1 - offset), (0, 0)),
            )
            for offset in range(CONV)
        )
    )
    tail_back = jnp.where(has_before[None, :, None, None], padded_back[:, :, : CONV - 1], 0.0)
    keyval_back_t = keyval_back.reshape(size, kv_cols, rows)
    qkv_back_t = jnp.concatenate([query_back_t.reshape(size, q_cols, rows), keyval_back_t], axis=1)
    pad_rows = up_to(q_cols + kv_cols, 8) - q_cols - kv_cols
    qkv_back_t = jnp.pad(qkv_back_t, ((0, 0), (0, pad_rows), (0, 0)))
    (tails_back_all,), (qkv_back,) = together(
        [ctx_gather_job(tail_back.astype(bf16).reshape(-1, chan)), exchange_job(qkv_back_t, size)],
        size,
        11,
        "edges_back",
    )
    qkv_back = qkv_back.transpose(0, 2, 1).reshape(rows_all, -1)
    qkv_back = jnp.pad(qkv_back, ((0, 0), (0, qkv_up - qkv_back.shape[1])))
    tails_back_all = in_deal_order(tails_back_all.reshape(n_ctx, size, 2, CONV - 1, chan))
    after_index = inverse[jnp.minimum(my_blocks + 1, blocks_all - 1)]
    has_after = my_blocks < blocks_all - 1
    incoming = jnp.where(
        has_after[None, :, None, None], of_blocks(tails_back_all, after_index).astype(f32), 0.0
    )
    mixer_back = padded_back[:, :, CONV - 1 :] + jnp.pad(
        incoming, ((0, 0), (0, 0), (half_rows - (CONV - 1), 0), (0, 0))
    )
    entry_back = jnp.concatenate([mixer_back.reshape(rows_all, chan), side_back], axis=1).astype(
        bf16
    )
    first_back = [qkv_back, entry_back]
    if first_total > qkv_up + 2 * chan_up:
        first_back.append(jnp.zeros((rows_all, first_total - qkv_up - 2 * chan_up), bf16))
    first_back = jnp.concatenate(first_back, axis=1)
    first_wgrad = column_grads(normed_all, first_back)
    gain_rows = jnp.stack(
        [jnp.zeros_like(attn_gain_grad), attn_gain_grad, mamba_gain_grad, ffn_gain_grad]
    )
    gain_rows = jnp.moveaxis(gain_rows.reshape(4, size, -1), 1, 0)
    small = jnp.concatenate(
        [
            taps_grad,
            shift_grad[None],
            bias_grad[None],
            skip_grad[None],
            decay_grad,
            step_wgrad,
            select_wgrad.T,
        ]
    )
    n_small = small.shape[0]
    small = jnp.pad(small, ((0, up_to(n_small, 64) - n_small), (0, 0))).astype(bf16)
    (gate_share, up_share), ((input_back,), (first_home,), (small,), (gain_share,)) = finish(
        first_wgrad.reshape(size, depth, first_total),
        first_back,
        first_mat,
        normed_all,
        gain_float[:1],
        gain_rows,
        small,
        ffn_home,
        (ffn_cuts, ffn_at),
        (gate_weight.shape, up_weight.shape),
        size,
        13,
    )
    stream_part, _ = norm_backward(input_back, stream, inv_in, gain_float[0])
    stream_back = middle_back + stream_part
    query_share, keyval_share, entry_share = unpack_columns(
        first_home,
        first_cuts,
        first_at,
        (query_weight.shape, keyval_weight.shape, mamba_in.shape),
        size,
    )
    chan = conv_bias.shape[0]
    vectors = small.reshape(-1, chan_up)[:, :chan].astype(f32)
    attn_share = jnp.moveaxis(attn_home, 0, 1).reshape(depth, attn_wide)[:, :width].astype(f32)
    mamba_share = mamba_share.reshape(-1, width)[:chan].astype(f32)
    down_share = down_share.reshape(-1, width)[:ff_cols].astype(f32)
    return (
        result.astype(bf16)[None],
        stream_back[None],
        gain_share,
        query_share,
        keyval_share,
        attn_share,
        entry_share,
        vectors[:CONV],
        vectors[CONV],
        vectors[CONV + 1],
        vectors[CONV + 2],
        vectors[CONV + 3 : CONV + 3 + NS],
        vectors[CONV + 3 + NS + RANK : n_small].T,
        vectors[CONV + 3 + NS : CONV + 3 + NS + RANK],
        mamba_share,
        gate_share,
        up_share,
        down_share,
    )


def solution(mesh):
    in_specs = (
        P("fsdp", "ctx", None),
        P("fsdp", "ctx", None),
        P("fsdp", None),
        P(),
        P(None, "fsdp"),
        P("fsdp", None),
        P("fsdp", None),
        P("fsdp", None),
        P("fsdp", None),
        P(None, "fsdp"),
        P("fsdp"),
        P("fsdp"),
        P("fsdp"),
        P(None, "fsdp"),
        P("fsdp", None),
        P(None, "fsdp"),
        P("fsdp", None),
        P("fsdp", None),
        P("fsdp", None),
        P("fsdp", None),
    )
    out_specs = (
        P("fsdp", "ctx", None),
        P("fsdp", "ctx", None),
        P(None, "fsdp"),
        P("fsdp", None),
        P("fsdp", None),
        P("fsdp", None),
        P("fsdp", None),
        P(None, "fsdp"),
        P("fsdp"),
        P("fsdp"),
        P("fsdp"),
        P(None, "fsdp"),
        P("fsdp", None),
        P(None, "fsdp"),
        P("fsdp", None),
        P("fsdp", None),
        P("fsdp", None),
        P("fsdp", None),
    )
    return jax.shard_map(
        on_device, mesh=mesh, in_specs=in_specs, out_specs=out_specs, check_vma=False
    )
```

time: 1150 us -> 911 us (0.79)
  Pallas kernels: 840 us -> 692 us
  matrix products: 150 us -> 80.4 us
  local copies, waits for them, and re-layouts: 88 us -> 71.2 us
    pallas_call x14 -> x5, Pallas kernels: 703 us -> 109 us  [together(): pl.pallas_call(kernel, out_shape=[shape for job in jobs for shape, _ in j...]
    pallas_call x6 -> x7, Pallas kernels: 124 us -> 577 us  [hosted(): pl.pallas_call(kernel, out_shape=[shape for shape, _ in outs] + [shape fo...]
    dot_general x42 -> x4, matrix products: 66.5 us -> 13.6 us  [the longest x1 4.88 us: on_device(): jnp.einsum('dk,ld->kl', qkv_mat, normed_all, preferred_element_type=f32)]
    convert_element_type x1, local copies, waits for them, and re-layouts: 19.3 us -> 5.46 us  [on_device(): jnp.dot(mamba_rows, mamba_mat, preferred_element_type=f32).astype(bf16)]
    unnamed x185 -> x183, local copies, waits for them, and re-layouts: 18.7 us -> 25.7 us
where the time goes in v3:
time: 911 us; the launch traced here: 901 us
  Pallas kernels  692 us (76%)
  matrix products  80.4 us (9%)
  local copies, waits for them, and re-layouts  71.2 us (8%)
  other arithmetic  55.3 us (6%)
    pallas_call x7, Pallas kernels, hosted(): pl.pallas_call(kernel, out_shape=[shape for shape, _ in outs] + [shape fo...  577 us
    pallas_call x5, Pallas kernels, together(): pl.pallas_call(kernel, out_shape=[shape for job in jobs for shape, _ in j...  109 us
    unnamed x183, local copies, waits for them, and re-layouts  25.7 us

profile of v3, /device:TPU:0, one launch (start us, length us, event | category | flops | bytes accessed | tf_op | source)
XLA Modules:
  0.0 901.1 jit_solution(6227542912450887402)
XLA Ops:
  2.6 83.4 %start.1 = (bf16[8,200,1536]{2,1,0:T(8,128)(2,1)}, bf16[8,128,1600]{2,1,0:T(8,128)(2,1)}, bf16[8,4,200]{2,1,0:T(4,128)(2,1)}, bf16[8,200,1536]{2,1,0:T(8,128)(2,1)}) custom-call(bf16[200,1600]{1,0:T(8,128)(2,1)} %refs_0_.1, bf16[200,640]{1,0:T(8,128)(2,1)} %refs_1_.1, bf16[200,6400]{1,0:T(8,128)(2,1)} %refs_2_.1, bf16[200,5504]{1,0:T(8,128)(2,1)} %refs_3_.1, ...), custom_call_target="tpu_custom_call" | custom-call | tf_op jit(solution)/shard_map/start/pallas_call | solution.py:1070
  100.3 4.9 convolution_convert_fusion.5.refs_0_
  105.2 14.9 %edges.1 = (bf16[8,280,128]{2,1,0:T(8,128)(2,1)}, bf16[4,48,512]{2,1,0:T(8,128)(2,1)}) custom-call(bf16[384,1024]{1,0:T(8,128)(2,1)} %convolution_convert_fusion.5.refs_0_, bf16[48,512]{1,0:T(8,128)(2,1)} %reshape.358.refs_1_), custom_call_target="tpu_custom_call" | custom-call | tf_op jit(solution)/shard_map/edges/pallas_call | solution.py:159
  134.9 21.5 %select.31 = (bf16[132,1024]{1,0:T(8,128)(2,1)}, bf16[4,640,128]{2,1,0:T(8,128)(2,1)}) custom-call(bf16[132,1024]{1,0:T(8,128)(2,1)} %convolution_convert_fusion.6.refs_0_, bf16[640,128]{1,0:T(8,128)(2,1)} %bitcast.184), custom_call_target="tpu_custom_call" | custom-call | tf_op jit(solution)/shard_map/select/pallas_call | solution.py:159
  156.4 4.4 compare_select_fusion
  165.2 110.6 %scan_forward.1 = (f32[1024,512]{1,0:T(8,128)}, f32[2,1,16,8,512]{4,3,2,1,0:T(8,128)}, bf16[8,1,17,8,512]{4,3,2,1,0:T(8,128)(2,1)}, bf16[8,128,1600]{2,1,0:T(8,1...) custom-call(s32[10]{0:T(128)} %pad_add_fusion.3.refs_0_, f32[1024,512]{1,0:T(8,128)} %get-tuple-element.221.refs_1_, ...), custom_call_target="tpu_custom_call" | custom-call | tf_op jit(solution)/shard_map/scan_forward/pallas_call | solution.py:1070
  283.8 5.5 copy.120
  295.9 45.8 %attention_forward.1 = (bf16[1600,128]{1,0:T(8,128)(2,1)}, f32[25,128]{1,0:T(8,128)}, f32[128,1600]{1,0:T(8,128)}) custom-call(bf16[1600,128]{1,0:T(8,128)(2,1)} %bitcast.165, bf16[5,512,64]{2,1,0:T(8,128)(2,1)} %get-tuple-element.209.refs_1_, bf16[320,512]{1,0:T(8,128)(2,1)} %bitcast.177, f32[512,128]{1,0:T(8,128)} %and_select_fusion.refs_3_.refs_4_, ...), custom_call_target="tpu_custom_call" | custom-call | tf_op jit(solution)/shard_map/attention_forward/pallas_call | solution.py:1070
  341.7 4.9 multiply_reduce_fusion.14
  349.9 40.3 %ffn_rows.1 = bf16[8,128,1600]{2,1,0:T(8,128)(2,1)} custom-call(bf16[128,1600]{1,0:T(8,128)(2,1)} %multiply_convert_fusion.8.refs_0_), custom_call_target="tpu_custom_call" | custom-call | tf_op jit(solution)/shard_map/ffn_rows/pallas_call | solution.py:159
  390.3 5.9 fusion.21
  399.3 5.3 multiply_convert_fusion
  411.5 5.4 copy.130
  420.2 58.2 %ffn_sums.1 = (bf16[8,200,384]{2,1,0:T(8,128)(2,1)}, bf16[768,1600]{1,0:T(8,128)(2,1)}, f32[128,1600]{1,0:T(8,128)}) custom-call(bf16[1024,1600]{1,0:T(8,128)(2,1)} %bitcast.149, bf16[1024,1536]{1,0:T(8,128)(2,1)} %pad_maximum_fusion.refs_1_, bf16[1024,768]{1,0:T(8,128)(2,1)} %get-tuple-element.201.refs_2_, bf16[1024,1600]{1,0:T(8,128)(2,1)} %bitcast.167, ...), custom_call_target="tpu_custom_call" | custom-call | tf_op jit(solution)/shard_map/ffn_sums/pallas_call | solution.py:1070
  492.5 52.8 %attention_backward.1 = (bf16[1600,128]{1,0:T(8,128)(2,1)}, f32[640,512]{1,0:T(8,128)}, bf16[8,128,1600]{2,1,0:T(8,128)(2,1)}, bf16[8,200,512]{2,1,0:T(8,128)(2,1)}) custom-call(bf16[1600,128]{1,0:T(8,128)(2,1)} %bitcast.166, bf16[5,512,64]{2,1,0:T(8,128)(2,1)} %get-tuple-element.209.refs_1_, bf16[320,512]{1,0:T(8,128)(2,1)} %bitcast.178, ...), custom_call_target="tpu_custom_call" | custom-call | tf_op jit(solution)/shard_map/attention_backward/pallas_call | solution.py:1070
  552.0 8.4 multiply_reduce_fusion.1
  564.6 5.4 copy.132
  570.0 124.0 %scan_backward.1 = (f32[1024,512]{1,0:T(8,128)}, f32[1024,512]{1,0:T(8,128)}, f32[1024,128]{1,0:T(8,128)}, f32[2,1,16,8,512]{4,3,2,1,0:T(8,128)}, bf16[8,200,153...) custom-call(s32[10]{0:T(128)} %pad_add_fusion.3.refs_0_, ...), custom_call_target="tpu_custom_call" | custom-call | tf_op jit(solution)/shard_map/scan_backward/pallas_call | solution.py:1070
  701.3 17.8 %select_back.1 = (bf16[132,1024]{1,0:T(8,128)(2,1)}, bf16[4,200,512]{2,1,0:T(8,128)(2,1)}, bf16[1,640,128]{2,1,0:T(8,128)(2,1)}) custom-call(bf16[132,1024]{1,0:T(8,128)(2,1)} %maximum_bitcast_fusion.refs_0_, bf16[200,512]{1,0:T(8,128)(2,1)} %convert_element_type.219.refs_1_, bf16[1,640,512]{2,1,0:T(8,128)(2,1)} %convert_bitcast_fusion.refs_2_), custom_call_target="tpu_custom_call" | custom-call | tf_op jit(solution)/shard_map/select_back/pallas_call | solution.py:159
  736.1 14.4 %edges_back.1 = (bf16[4,48,512]{2,1,0:T(8,128)(2,1)}, bf16[8,280,128]{2,1,0:T(8,128)(2,1)}) custom-call(bf16[48,512]{1,0:T(8,128)(2,1)} %reshape.377.refs_0_, bf16[8,280,128]{2,1,0:T(8,128)(2,1)} %pad_maximum_fusion.1.refs_1_), custom_call_target="tpu_custom_call" | custom-call | tf_op jit(solution)/shard_map/edges_back/pallas_call | solution.py:159
  758.2 9.4 %convolution_convert_fusion = bf16[1600,1536]{1,0:T(8,128)(2,1)} fusion(bf16[1024,1600]{1,0:T(8,128)(2,1)} %copy-done.10, bf16[1024,280]{1,0:T(8,128)(2,1)S(1)} %bitcast.169, bf16[1024,512]{1,0:T(8,128)(2,1)} %get-tuple-element.200, bf16[1024,512]{1,0:T(8,128)(2,1)S(1)} %bitcast.162, bf16[1536]{0:T(1024)(128)(2,1)S(1)} %pad.101.clone), kind=kOutput, calls=%fused_computation.4 | convolution fusion | flops 5051351040 | bytes 10865664 | tf_op jit(solution)/shard_map/ld,lk->dk/dot_general | solution.py:1718
  772.2 102.0 %finish.1 = (f32[200,5504]{1,0:T(8,128)}, f32[200,5504]{1,0:T(8,128)}, f32[128,1600]{1,0:T(8,128)}, bf16[8,200,1536]{2,1,0:T(8,128)(2,1)}, bf16[4,64,512]{2,1,0:T(8,128)(2,1)}, /*index=5*/f32[4,200]{1,0:T(4,128)}) custom-call(bf16[1024,1536]{1,0:T(8,128)(2,1)} %fusion.11.refs_0_, bf16[1600,1536]{1,0:T(8,128)(2,1)} %bitcast.155, ...), custom_call_target="tpu_custom_call" | custom-call | tf_op jit(solution)/shard_map/finish/pallas_call | solution.py:1070
  874.2 6.1 unpack_columns.1
  893.8 4.8 copy.177
  (336 shorter events, 142.8 us)
Async XLA Ops:
  90.9 6.7 copy-start.10
  100.3 20.9 %copy-start.67 = (s32[4,2]{0,1:T(2,128)S(1)}, s32[4,2]{0,1:T(2,128)}, u32[]{:S(2)}) copy-start(s32[4,2]{0,1:T(2,128)} %param.25) | copy-start | bytes 100
  131.2 25.2 %copy-start.71 = (bf16[400]{0:T(512)(128)(2,1)S(1)}, bf16[400]{0:T(512)(128)(2,1)}, u32[]{:S(2)}) copy-start(bf16[400]{0:T(512)(128)(2,1)} %param.33) | copy-start | bytes 2404
  131.2 25.3 %copy-start.46 = (bf16[100,400]{0,1:T(8,128)(2,1)S(1)}, bf16[100,400]{0,1:T(8,128)(2,1)}, u32[]{:S(2)}) copy-start(bf16[100,400]{0,1:T(8,128)(2,1)} %param.37) | copy-start | bytes 240004
  165.2 110.6 %copy-start.72 = (bf16[400]{0:T(512)(128)(2,1)S(1)}, bf16[400]{0:T(512)(128)(2,1)}, u32[]{:S(2)}) copy-start(bf16[400]{0:T(512)(128)(2,1)} %param.34) | copy-start | bytes 2404
  390.2 5.9 copy-start.19
  390.3 9.0 slice-start.4
  552.0 8.4 copy-start.24
  552.0 8.4 copy-start.76
  570.0 124.0 %copy-start.63 = (f32[512]{0:T(512)S(1)}, f32[512]{0:T(512)}, u32[]{:S(2)}) copy-start(f32[512]{0:T(512)} %copy-done.62) | copy-start | bytes 6148
  697.6 21.6 %copy-start.4 = (bf16[1024,512]{1,0:T(8,128)(2,1)S(1)}, bf16[1024,512]{1,0:T(8,128)(2,1)}, u32[]{:S(2)}) copy-start(bf16[1024,512]{1,0:T(8,128)(2,1)} %copy-done.2) | copy-start | bytes 3145732
  699.0 21.6 %copy-start.31 = (bf16[132,1024]{1,0:T(8,128)(2,1)S(1)}, bf16[132,1024]{1,0:T(8,128)(2,1)}, u32[]{:S(2)}) copy-start(bf16[132,1024]{1,0:T(8,128)(2,1)} %get-tuple-element.74) | copy-start | bytes 811012
  701.3 19.6 %copy-start.43 = (bf16[400,132]{0,1:T(8,128)(2,1)S(1)}, bf16[400,132]{0,1:T(8,128)(2,1)}, u32[]{:S(2)}) copy-start(bf16[400,132]{0,1:T(8,128)(2,1)} %param.36) | copy-start | bytes 316804
  701.3 19.6 %copy-start.61 = (f32[512]{0:T(512)S(1)}, f32[512]{0:T(512)}, u32[]{:S(2)}) copy-start(f32[512]{0:T(512)} %copy-done.60) | copy-start | bytes 6148
  734.4 17.3 %copy-start.74 = (s32[2]{0:T(128)S(1)}, s32[2]{0:T(128)}, u32[]{:S(2)}) copy-start(s32[2]{0:T(128)} %get-tuple-element.188) | copy-start | bytes 28
  735.4 17.6 %copy-start.69 = (pred[2]{0:T(512)(128)(4,1)S(1)}, pred[2]{0:T(512)(128)(4,1)}, u32[]{:S(2)}) copy-start(pred[2]{0:T(512)(128)(4,1)} %get-tuple-element.219) | copy-start | bytes 10
  758.1 9.4 %copy-start.53 = (f32[1600]{0:T(1024)S(1)}, f32[1600]{0:T(1024)}, u32[]{:S(2)}) copy-start(f32[1600]{0:T(1024)} %get-tuple-element.173) | copy-start | bytes 19204
  758.2 9.5 %copy-start.52 = (f32[1600]{0:T(1024)S(1)}, f32[1600]{0:T(1024)}, u32[]{:S(2)}) copy-start(f32[1600]{0:T(1024)} %get-tuple-element.180) | copy-start | bytes 19204
  874.2 6.1 copy-start.73
  874.2 6.1 copy-start.13
  874.2 6.1 copy-start.20
  874.2 6.1 copy-start.45
  874.2 6.4 copy-start.17
  892.2 6.3 slice-start
  (61 other events, 167.8 us)

commit v4 on v3

--- a/solution.py
+++ b/solution.py
@@ -616,8 +616,8 @@
 
 
 class Halve:
-    def __init__(self, p, source, bufs, sems):
-        self.p, self.source = p, source
+    def __init__(self, p, source, bufs, sems, here=False):
+        self.p, self.source, self.here = p, source, here
         self.own, self.got, self.away, self.total = bufs
         self.ls, self.ns, self.nr, self.fs, self.fr = sems
         self.count, self.rows = self.total.shape[:2]
@@ -625,6 +625,11 @@
     def local(self, i):
         q = self.p.c if i == 0 else self.p.far
         return pltpu.make_async_copy(self.source(q), self.own.at[i], self.ls.at[i])
+
+    def mine_of(self, i, j):
+        if self.here:
+            return self.source(self.p.c if i == 0 else self.p.far).at[j]
+        return self.own.at[i, j]
 
     def to_near(self, i):
         q = self.p.near if i == 0 else self.p.other
@@ -642,21 +647,25 @@
         )
 
     def start(self):
-        for i in (1, 0):
-            self.local(i).start()
+        if not self.here:
+            for i in (1, 0):
+                self.local(i).start()
         for i in (1, 0):
             self.to_near(i).start()
 
     def send(self):
-        self.local(1).wait()
+        if not self.here:
+            self.local(1).wait()
         self.to_near(1).wait_recv()
         for k in range(self.count):
-            own = self.own.at[1, self.index(k)]
-            add_blocks(own, [own, self.got.at[1, self.index(k)]], bf16, self.rows)
+            j = self.index(k)
+            terms = [self.mine_of(1, j), self.got.at[1, j]]
+            add_blocks(self.own.at[1, j], terms, bf16, self.rows)
             self.to_far(k).start()
 
     def mine(self):
-        self.local(0).wait()
+        if not self.here:
+            self.local(0).wait()
         self.to_near(0).wait_recv()
 
     def block(self, k):
@@ -664,7 +673,7 @@
         j = self.index(k)
         add_blocks(
             self.total.at[j],
-            [self.own.at[0, j], self.got.at[0, j], self.away.at[j]],
+            [self.mine_of(0, j), self.got.at[0, j], self.away.at[j]],
             bf16,
             self.rows,
         )
@@ -831,13 +840,16 @@
     )
 
 
-def ctx_sum_job(x):
-    rows, cols = x.shape[0] // 4, x.shape[1]
-    x = x.reshape(4, rows, cols)
+def ctx_sum_job(x, used=None):
+    rows, cols = (x.shape[0] if used is None else used) // 4, x.shape[1]
+    x = x[None]
 
     def run(p, ins, outs, scratch):
         (x_ref,), (o_ref,) = ins, outs
-        halve = Halve(p, lambda q: x_ref.at[pl.ds(q, 1)], scratch[:4], scratch[4:9])
+        def source(q):
+            return x_ref.at[:, pl.ds(pl.multiple_of(q * rows, 16), rows)]
+
+        halve = Halve(p, source, scratch[:4], scratch[4:9])
         share = Share(p, lambda d, q: o_ref.at[q], 1, scratch[10:])
         halve.start()
         yield
@@ -974,6 +986,38 @@
     return lax.fori_loop(0, length // count, some, init)
 
 
+class Product:
+    def __init__(self, left, right, size, transposed=False):
+        rows_all = left.shape[0]
+        width = right.shape[0 if transposed else 1]
+        self.size, self.rows, self.transposed = size, rows_all // size, transposed
+        self.shape = like((size, self.rows, width), bf16)
+        self.ins = [(left, VM), (right, VM)]
+        self.scratch = [pltpu.VMEM(self.shape.shape, bf16)]
+        self.held = []
+
+    def stages(self, p, left, right, out, also=None):
+        self.held.append(out)
+        contract = (((1,), (1 if self.transposed else 0,)), ((), ()))
+
+        def block(i):
+            at = pl.ds(pl.multiple_of(i * self.rows, self.rows), self.rows)
+            got = lax.dot_general(
+                left[at, :], right[...], contract, preferred_element_type=f32
+            ).astype(bf16)
+            out[i] = got
+            if also is not None:
+                also(at, got)
+
+        def partner(k):
+            block(2 * k + 1 - p.b)
+
+        def own(k):
+            block(2 * k + p.b)
+
+        return [(self.size // 2, partner), (self.size // 2, own)]
+
+
 class Scan:
     def __init__(self, streams, length, chan):
         self.width = math.gcd(streams, 8)
@@ -1204,18 +1248,21 @@
     )
 
 
-def scan_backward(order, dt, x, g, wr, rate2, starts, ends, streams, jobs, size, cid, plan):
+def scan_backward(
+    order, dt, x, g, wr, rate2, starts, ends, product, streams, jobs, size, cid, plan
+):
     chan = dt.shape[1]
     scan = Scan(streams, dt.shape[0] // streams // 2, chan)
     blocks = order.shape[0] - 2
     length, width = scan.length, scan.width
 
     def loops(p, ins, outs, scratch):
-        order_ref, dt_flat, x_flat, g_flat, wr_ref, rate_ref, start_ref, ends_ref = ins
+        order_ref, dt_flat, x_flat, g_flat, wr_ref, rate_ref, start_ref, ends_ref = ins[:8]
         sb_flat, cw_flat, wrb_ref, dec_ref = outs
         backs_ref, wb, rb, kept, decays, wparts, rparts, sums = scratch[:8]
         dt_ref, x_ref, g_ref, sb_ref, cw_ref, dt_sem, x_sem, g_sem, sb_sem, cw_sem = scratch[8:18]
-        share = Share(p, lambda d, q: backs_ref.at[pl.ds(2 * q, 2)], 1, scratch[18:])
+        share = Share(p, lambda d, q: backs_ref.at[pl.ds(2 * q, 2)], 1, scratch[18:24])
+        extra = product.stages(p, *ins[8:], scratch[24]) if product else []
 
         def load():
             copies = scan.tile_copies(dt_flat, dt_ref, dt_sem)
@@ -1265,7 +1312,16 @@
             share.forward(0)
             share.finish()
 
-        def backward(i):
+        def both(i):
+            @pl.when(lax.rem(i, 2) == 0)
+            def _():
+                again(i // 2)
+
+            @pl.when(lax.rem(i, 2) == 1)
+            def _():
+                backward(i // 2)
+
+        def again(i):
             group, block, tile = scan.piece(i)
             lanes = scan.lanes(tile)
 
@@ -1294,6 +1350,10 @@
             for n in range(NS):
                 kept[length, n] = last[n]
 
+        def backward(i):
+            group, block, tile = scan.piece(i)
+            lanes = scan.lanes(tile)
+            rates = [rate_ref[n : n + 1, lanes] for n in range(NS)]
             mine = order_ref[blocks + block]
 
             def link(j, carries):
@@ -1357,7 +1417,7 @@
 
                 steps(length, out, 0)
 
-        return [load, (scan.pieces, backs), send, arrive, (scan.pieces, backward), store]
+        return extra + [load, (scan.pieces, backs), send, arrive, (2 * scan.pieces, both), store]
 
     spread = pltpu.VMEM((length, NS, width, 128), f32)
     parts = pltpu.VMEM((length * width, NS * 128), f32)
@@ -1369,7 +1429,8 @@
         "scan_backward",
         [
             (order, SM), (dt, ANY), (x, ANY), (g, ANY), (wr, VM), (rate2, VM), (starts, VM), (ends, VM),
-        ],
+        ]
+        + (product.ins if product else []),
         [
             (like(dt.shape, f32), ANY),
             (like(dt.shape, f32), ANY),
@@ -1388,17 +1449,18 @@
         ]
         + [scan.tiled()] * 5
         + [DMA((scan.tiles,))] * 5
-        + share_sems(1),
+        + share_sems(1)
+        + (product.scratch if product else []),
         plan,
     )
 
 
-def attention_forward(q_t, k, v_t, bias_t, jobs, size, cid, plan):
+def attention_forward(q_t, k, v_t, bias_t, product, jobs, size, cid, plan):
     rows = q_t.shape[1]
     group = H // KV
 
     def loops(p, ins, outs, scratch):
-        q_ref, k_ref, v_ref, bias_ref = ins
+        q_ref, k_ref, v_ref, bias_ref = ins[:4]
         o_ref, log_ref = outs
 
         def head(h):
@@ -1416,7 +1478,7 @@
             o_ref[at, :] = jnp.dot(values, probs, preferred_element_type=f32).astype(bf16)
             log_ref[pl.ds(h, 1), :] = largest + jnp.log(total)
 
-        return [(H, head)]
+        return product.stages(p, *ins[4:], scratch[0]) + [(H, head)]
 
     return hosted(
         loops,
@@ -1424,9 +1486,9 @@
         size,
         cid,
         "attention_forward",
-        [(q_t, VM), (k, VM), (v_t, VM), (bias_t, VM)],
+        [(q_t, VM), (k, VM), (v_t, VM), (bias_t, VM)] + product.ins,
         [(like(q_t.shape, bf16), VM), (like((H, rows), f32), VM)],
-        [],
+        product.scratch,
         plan,
     )
 
@@ -1530,24 +1592,33 @@
     )
 
 
-def ffn_sums(low, back, hidden, grads, jobs, size, cid):
+def ffn_sums(low, back, hidden, grads, product, jobs, size, cid):
     rows, width = low.shape
     total, units = back.shape[1], hidden.shape[1]
     depth, quarter = width // size, total // 4
     contract = (((0,), (0,)), ((), ()))
 
     def loops(p, ins, outs, scratch):
-        low_ref, back_ref, hidden_ref, grads_ref = ins
+        low_ref, back_ref, hidden_ref, grads_ref = ins[:4]
         quarter_ref, down_ref = outs
         whole = scratch[0]
         halve = Halve(
             p,
             lambda q: whole.at[:, :, column_block(q, quarter)],
             list(scratch[1:4]) + [quarter_ref],
-            scratch[4:],
+            scratch[4:9],
+            True,
         )
-
-        def tile(i):
+        per = quarter // 128
+        extra = product.stages(p, back_ref, ins[4], scratch[9]) if product else []
+
+        def tile_of(first, second):
+            def tile(i):
+                tile_at(jnp.where(i < per, first * per + i, second * per + i - per))
+
+            return tile
+
+        def tile_at(i):
             lanes = column_block(i, 128)
             got = lax.dot_general(
                 low_ref[...], back_ref[:, lanes], contract, preferred_element_type=f32
@@ -1567,8 +1638,14 @@
                 halve.block(k)
             halve.finish()
 
-        return [
-            (total // 128, tile), halve.start, halve.send, (units // 128, down_tile), sums,
+        return extra + [
+            (2 * per, tile_of(p.other, p.near)),
+            halve.start,
+            (per, tile_of(p.far, p.far)),
+            halve.send,
+            (per, tile_of(p.c, p.c)),
+            (units // 128, down_tile),
+            sums,
         ]
 
     return hosted(
@@ -1577,72 +1654,44 @@
         size,
         cid,
         "ffn_sums",
-        [(low, VM), (back, VM), (hidden, VM), (grads, VM)],
+        [(low, VM), (back, VM), (hidden, VM), (grads, VM)] + (product.ins[1:] if product else []),
         [(like((size, depth, quarter), bf16), VM), (like((units, width), bf16), VM)],
-        [pltpu.VMEM((size, depth, total), bf16)] + halve_scratch(size, depth, quarter, False),
+        [pltpu.VMEM((size, depth, total), bf16)]
+        + halve_scratch(size, depth, quarter, False)
+        + (product.scratch if product else []),
         PLAN_FFN,
     )
 
 
-def finish(wgrad, back, mat, normed, gain, gain_rows, small, ffn_home, ffn_pack, shapes, size, cid):
-    rows_all, total = back.shape
-    width = mat.shape[0]
-    rows = rows_all // size
-    cuts, offsets = ffn_pack
-    held_rows, held_gains = [], []
-    contract = (((1,), (1,)), ((), ()))
-    n_out = len(shapes)
+def finish(wgrad, product, normed, gain, gain_rows, small, size, cid):
+    width = normed.shape[1]
+    held_gains = []
 
     def loops(p, ins, outs, scratch):
-        back_ref, mat_ref, normed_ref, gain_ref, gain_rows_ref, home_ref = ins
-        part_ref, total_ref, gains_ref, home_sem, out_sem, home_in = scratch[:6]
-        laid = scratch[6:]
-        held_rows.append(part_ref)
+        left_ref, right_ref, normed_ref, gain_ref, gain_rows_ref = ins
+        part_ref, total_ref, gains_ref = scratch
         held_gains.append(gains_ref)
 
-        def fetch():
-            return pltpu.make_async_copy(home_ref, home_in, home_sem)
-
-        def store(i):
-            return pltpu.make_async_copy(laid[i], outs[i], out_sem.at[i])
-
         def begin():
-            fetch().start()
             total_ref[...] = jnp.zeros_like(total_ref)
 
-        def block(i):
-            at = pl.ds(pl.multiple_of(i * rows, rows), rows)
-            got = lax.dot_general(
-                back_ref[at, :], mat_ref[...], contract, preferred_element_type=f32
-            ).astype(bf16)
-            part_ref[i] = got
-            product = got.astype(f32) * normed_ref[at, :].astype(f32)
-            total_ref[...] += jnp.sum(product, axis=0, keepdims=True)
+        def add_gain(at, got):
+            product_ = got.astype(f32) * normed_ref[at, :].astype(f32)
+            total_ref[...] += jnp.sum(product_, axis=0, keepdims=True)
 
         def gains():
             gains_ref[...] = gain_rows_ref[...]
-            first = (total_ref[...] / gain_ref[...]).astype(f32)
+            first = total_ref[...] / gain_ref[...]
             cols = width // size
             for f in range(size):
                 gains_ref[f, 0:1, :] = first[:, f * cols : (f + 1) * cols]
 
-        def lay_out():
-            fetch().wait()
-            unpack_pieces(home_in, laid, cuts, offsets, size)
-            for i in range(n_out):
-                store(i).start()
-
-        def stored():
-            for i in range(n_out):
-                store(i).wait()
-
-        return [begin, (size, block), gains, lay_out, stored]
-
-    part_shape = like((size, rows, width), bf16)
+        return [begin] + product.stages(p, left_ref, right_ref, part_ref, add_gain) + [gains]
+
     return hosted(
         loops,
         [
-            scatter_job(part_shape, size, held_rows),
+            scatter_job(product.shape, size, product.held),
             home_job(wgrad, size),
             ctx_sum_job(small),
             all_sum_job(gain_rows, size, held_gains),
@@ -1650,35 +1699,30 @@
         size,
         cid,
         "finish",
-        [(back, VM), (mat, VM), (normed, VM), (gain, VM), (gain_rows, VM), (ffn_home, ANY)],
-        [(like(shape, f32), ANY) for shape in shapes],
-        [
-            pltpu.VMEM(part_shape.shape, bf16),
-            pltpu.VMEM((1, width), f32),
-            pltpu.VMEM(gain_rows.shape, f32),
-            DMA,
-            DMA((n_out,)),
-            pltpu.VMEM(ffn_home.shape, bf16),
-        ]
-        + [pltpu.VMEM(shape, f32) for shape in shapes],
+        product.ins + [(normed, VM), (gain, VM), (gain_rows, VM)],
+        [],
+        product.scratch + [pltpu.VMEM((1, width), f32), pltpu.VMEM(gain_rows.shape, f32)],
         PLAN_FINISH,
     )
 
 
 PLAN_START = {1: (0, 1), 2: (0, 2), "end": (0, 2)}
 PLAN_FORWARD = {
-    1: (2, 1),
-    (1, 3): (2,),
+    1: (2,),
+    (1, 2): (2,),
+    (1, 4): (2,),
     (1, 6): (2,),
-    2: (0,),
-    (4, 0): (2, 1, 1, 1),
-    (4, 1): (0, 2),
-    (4, 3): (0, 1),
-    (4, 5): (0, 1, 2),
-    (4, 7): (0,),
+    3: (1,),
+    (4, 0): (2, 0),
+    (4, 1): (1,),
+    (4, 3): (1, 0),
+    (4, 4): (1, 2),
+    (4, 5): (0,),
+    (4, 6): (1,),
+    (4, 7): (0, 2),
 }
-PLAN_ATTEND = {0: (0,), (0, 6): (0,), (0, 14): (0,), (0, 22): (0,)}
-PLAN_FFN = {0: (0,), (0, 7): (0,), 1: (0,), (3, 1): (0,)}
+PLAN_ATTEND = {1: (0,), (2, 2): (0,), (2, 12): (0,), (2, 22): (0,)}
+PLAN_FFN = {1: (0,), (2, 2): (0,), 5: (0,), (7, 1): (0,)}
 PLAN_ATTEND_BACK = {
     0: (0, 1),
     (1, 5): (1,),
@@ -1687,30 +1731,30 @@
     "end": (0, 1, 1, 1, 0),
 }
 PLAN_FINISH = {
-    1: (1,),
+    0: (1,),
     (1, 1): (1,),
-    (1, 3): (1,),
-    (1, 5): (1,),
-    (1, 7): (1,),
-    2: (1, 0, 2),
-    3: (0, 1, 3, 2),
-    4: (0, 1, 3, 1, 0, 2),
-    "end": (1, 1, 0, 3),
+    2: (0, 1),
+    (2, 1): (1,),
+    3: (1, 1, 2, 0),
+    "end": (3, 1, 0, 2, 3, 1, 0, 1, 3, 1, 2, 0),
 }
 PLAN_BACKWARD = {
-    1: (4, 0, 3),
-    (1, 3): (3,),
-    (1, 4): (4,),
-    (1, 7): (4,),
-    3: (),
-    (4, 0): (4, 0),
-    (4, 1): (4, 1, 0, 3),
-    (4, 2): (1, 0, 2),
-    (4, 3): (1, 0, 2),
-    (4, 4): (1, 0, 3),
-    (4, 5): (1, 2),
-    (4, 6): (1, 3),
-    (4, 7): (2,),
+    3: (4, 3),
+    (3, 2): (3,),
+    (3, 4): (4,),
+    (3, 7): (0,),
+    (6, 0): (4, 3),
+    (6, 1): (1,),
+    (6, 2): (4, 0),
+    (6, 5): (0, 3, 4),
+    (6, 6): (1, 2),
+    (6, 7): (0, 2),
+    (6, 8): (1,),
+    (6, 9): (0, 2),
+    (6, 10): (1, 3),
+    (6, 12): (0, 2),
+    (6, 13): (1,),
+    (6, 15): (2,),
 }
 
 
@@ -1888,13 +1932,14 @@
     scanned = scan_rows + skip_float * signal_float
     gate_act = jax.nn.silu(gate_side)
     mamba_rows = (scanned * gate_act).astype(bf16)
-    mamba_part = jnp.dot(mamba_rows, mamba_mat, preferred_element_type=f32).astype(bf16)
+    mamba_product = Product(mamba_rows, mamba_mat, size)
     (attn_rows_t, log_totals), ((mamba_out,),) = attention_forward(
         query_t,
         key_groups,
         keyvals_t[KV * HD :],
         bias_t,
-        [scatter_job(mamba_part.reshape(size, rows, width), size)],
+        mamba_product,
+        [scatter_job(mamba_product.shape, size, mamba_product.held)],
         size,
         5,
         PLAN_ATTEND,
@@ -1912,19 +1957,21 @@
     gate_pre = jnp.dot(ffn_low, gate_mat, preferred_element_type=f32)
     up_pre = jnp.dot(ffn_low, up_mat, preferred_element_type=f32)
     hidden = (jax.nn.silu(gate_pre) * up_pre).astype(bf16)
-    down_part = jnp.dot(hidden, down_mat, preferred_element_type=f32).astype(bf16)
     hidden_back = jnp.einsum("ld,fd->lf", grads_all, down_mat, preferred_element_type=f32)
     gate_back = (hidden_back * up_pre * silu_slope(gate_pre)).astype(bf16)
     up_back = (hidden_back * jax.nn.silu(gate_pre)).astype(bf16)
-    ffn_back_part = jnp.einsum(
-        "lf,df->ld", gate_back, gate_mat, preferred_element_type=f32
-    ) + jnp.einsum("lf,df->ld", up_back, up_mat, preferred_element_type=f32)
     ffn_back_low = jnp.concatenate([gate_back, up_back], axis=1)
     ffn_back_low = jnp.pad(ffn_back_low, ((0, 0), (0, ffn_total - 2 * ff_up)))
-    ffn_jobs = [scatter_job(ffn_back_part.astype(bf16).reshape(size, rows, width), size)]
     fits = size <= 8
+    if fits:
+        ffn_product = Product(ffn_back_low, ffn_mat, size, True)
+        ffn_jobs = [scatter_job(ffn_product.shape, size, ffn_product.held)]
+    else:
+        ffn_product = None
+        ffn_part = jnp.einsum("lf,df->ld", ffn_back_low, ffn_mat, preferred_element_type=f32)
+        ffn_jobs = [scatter_job(ffn_part.astype(bf16).reshape(size, rows, width), size)]
     (ffn_quarter_sum, down_wgrad), ffn_back = ffn_sums(
-        ffn_low, ffn_back_low, hidden, grads_all, ffn_jobs * fits, size, 7
+        ffn_low, ffn_back_low, hidden, grads_all, ffn_product, ffn_jobs * fits, size, 7
     )
     if not fits:
         ffn_back = together(ffn_jobs, size, 14, "ffn_sum")
@@ -1937,8 +1984,10 @@
         branch_back, mamba_out, inv_mamba, gain_float[2]
     )
     attn_back = attn_part.astype(bf16)
-    attn_wgrad = jnp.einsum("hl,ld->hd", attn_rows_t, attn_back, preferred_element_type=f32)
-    attn_wgrad = jnp.pad(attn_wgrad.astype(bf16), ((0, 0), (0, attn_wide - width)))
+    attn_back_wide = jnp.pad(attn_back, ((0, 0), (0, attn_wide - width)))
+    attn_wgrad = jnp.einsum(
+        "hl,ld->hd", attn_rows_t, attn_back_wide, preferred_element_type=f32
+    ).astype(bf16)
     dout_t = jnp.einsum("hd,ld->hl", attn_mat, attn_back, preferred_element_type=f32).astype(bf16)
     (query_back_t, keyval_terms), ((mamba_back,), (attn_quarter,)) = (
         attention_backward(
@@ -1964,7 +2013,12 @@
     scan_back = mrows_back * gate_act
     side_back = mrows_back * scanned * silu_slope(gate_side)
     skip_grad = jnp.sum(scan_back * signal_float, axis=0)
-    down_jobs = [scatter_job(down_part.reshape(size, rows, width), size)]
+    down_product = Product(hidden, down_mat, size) if fits else None
+    if fits:
+        down_jobs = [scatter_job(down_product.shape, size, down_product.held)]
+    else:
+        down_part = jnp.dot(hidden, down_mat, preferred_element_type=f32).astype(bf16)
+        down_jobs = [scatter_job(down_part.reshape(size, rows, width), size)]
     (
         (step_back, carry_writes, read_write_back, decay_sums),
         ((ffn_home,), (attn_piece,), (mamba_share,), (down_share,), *down_out),
@@ -1977,12 +2031,13 @@
         rate2,
         start_state,
         ends_all,
+        down_product,
         size,
         [
             deliver_job(ffn_quarter_sum, size),
             scatter_job(attn_quarter, size),
-            ctx_sum_job(mamba_wgrad.astype(bf16)),
-            ctx_sum_job(down_wgrad),
+            ctx_sum_job(mamba_wgrad.astype(bf16), up_to(mamba_proj.shape[0], 64)),
+            ctx_sum_job(down_wgrad, up_to(ff_cols, 64)),
         ]
         + down_jobs * fits,
         size,
@@ -2080,17 +2135,17 @@
     )
     n_small = small.shape[0]
     small = jnp.pad(small, ((0, up_to(n_small, 64) - n_small), (0, 0))).astype(bf16)
-    (gate_share, up_share), ((input_back,), (first_home,), (small,), (gain_share,)) = finish(
+    gate_share, up_share = unpack_columns(
+        ffn_home, ffn_cuts, ffn_at, (gate_weight.shape, up_weight.shape), size
+    )
+    input_product = Product(first_back, first_mat, size, True)
+    _, ((input_back,), (first_home,), (small,), (gain_share,)) = finish(
         first_wgrad.reshape(size, depth, first_total),
-        first_back,
-        first_mat,
+        input_product,
         normed_all,
         gain_float[:1],
         gain_rows,
         small,
-        ffn_home,
-        (ffn_cuts, ffn_at),
-        (gate_weight.shape, up_weight.shape),
         size,
         13,
     )

time: 911 us -> 868 us (0.953)
  Pallas kernels: 692 us -> 673 us
  local copies, waits for them, and re-layouts: 71.2 us -> 53.6 us
  matrix products: 80.4 us -> 67.4 us
    pallas_call x7, Pallas kernels: 577 us -> 549 us  [hosted(): pl.pallas_call(kernel, out_shape=[shape for shape, _ in outs] + [shape fo...]
    convert_element_type x4 -> x0, local copies, waits for them, and re-layouts: 18.7 us -> none  [the longest x1 5.46 us: on_device(): jnp.dot(mamba_rows, mamba_mat, preferred_element_type=f32).astype(bf16)]
    dot_general x5 -> x1, matrix products: 16.3 us -> 4.36 us  [on_device(): jnp.einsum('hl,ld->hd', attn_rows_t, attn_back_wide, preferred_element_ty...]
    unnamed x183 -> x195, local copies, waits for them, and re-layouts: 25.7 us -> 23.1 us
where the time goes in v4:
time: 868 us; the launch traced here: 852 us
  Pallas kernels  673 us (78%)
  matrix products  67.4 us (8%)
  other arithmetic  55.7 us (6%)
  local copies, waits for them, and re-layouts  53.6 us (6%)
    pallas_call x7, Pallas kernels, hosted(): pl.pallas_call(kernel, out_shape=[shape for shape, _ in outs] + [shape fo...  549 us
    pallas_call x5, Pallas kernels, together(): pl.pallas_call(kernel, out_shape=[shape for job in jobs for shape, _ in j...  110 us
    unnamed x195, local copies, waits for them, and re-layouts  23.1 us

profile of v4, /device:TPU:0, one launch (start us, length us, event | category | flops | bytes accessed | tf_op | source)
XLA Modules:
  0.0 851.8 jit_solution(797651388618188670)
XLA Ops:
  2.6 83.4 %start.1 = (bf16[8,200,1536]{2,1,0:T(8,128)(2,1)}, bf16[8,128,1600]{2,1,0:T(8,128)(2,1)}, bf16[8,4,200]{2,1,0:T(4,128)(2,1)}, bf16[8,200,1536]{2,1,0:T(8,128)(2,1)}) custom-call(bf16[200,1600]{1,0:T(8,128)(2,1)} %refs_0_.1, bf16[200,640]{1,0:T(8,128)(2,1)} %refs_1_.1, bf16[200,6400]{1,0:T(8,128)(2,1)} %refs_2_.1, bf16[200,5504]{1,0:T(8,128)(2,1)} %refs_3_.1, ...), custom_call_target="tpu_custom_call" | custom-call | tf_op jit(solution)/shard_map/start/pallas_call | solution.py:1114
  96.6 3.9 fusion.7
  103.4 14.9 %edges.1 = (bf16[8,280,128]{2,1,0:T(8,128)(2,1)}, bf16[4,48,512]{2,1,0:T(8,128)(2,1)}) custom-call(bf16[384,1024]{1,0:T(8,128)(2,1)} %convolution_convert_fusion.3.refs_0_, bf16[48,512]{1,0:T(8,128)(2,1)} %reshape.340.refs_1_), custom_call_target="tpu_custom_call" | custom-call | tf_op jit(solution)/shard_map/edges/pallas_call | solution.py:159
  133.7 21.4 %select.31 = (bf16[132,1024]{1,0:T(8,128)(2,1)}, bf16[4,640,128]{2,1,0:T(8,128)(2,1)}) custom-call(bf16[132,1024]{1,0:T(8,128)(2,1)} %convolution_convert_fusion.4.refs_0_, bf16[640,128]{1,0:T(8,128)(2,1)} %bitcast.176), custom_call_target="tpu_custom_call" | custom-call | tf_op jit(solution)/shard_map/select/pallas_call | solution.py:159
  169.9 93.3 %scan_forward.1 = (f32[1024,512]{1,0:T(8,128)}, f32[2,1,16,8,512]{4,3,2,1,0:T(8,128)}, bf16[8,1,17,8,512]{4,3,2,1,0:T(8,128)(2,1)}, bf16[8,128,1600]{2,1,0:T(8,1...) custom-call(s32[10]{0:T(128)} %pad_add_fusion.3.refs_0_, f32[1024,512]{1,0:T(8,128)} %get-tuple-element.221.refs_1_, ...), custom_call_target="tpu_custom_call" | custom-call | tf_op jit(solution)/shard_map/scan_forward/pallas_call | solution.py:1114
  263.2 4.3 multiply_convert_fusion.5.refs_4_
  268.8 48.4 %attention_forward.1 = (bf16[1600,128]{1,0:T(8,128)(2,1)}, f32[25,128]{1,0:T(8,128)}, f32[128,1600]{1,0:T(8,128)}) custom-call(bf16[1600,128]{1,0:T(8,128)(2,1)} %bitcast.158, bf16[5,512,64]{2,1,0:T(8,128)(2,1)} %get-tuple-element.209.refs_1_, bf16[320,512]{1,0:T(8,128)(2,1)} %bitcast.171, f32[512,128]{1,0:T(8,128)} %and_select_fusion.refs_3_.refs_4_, ...), custom_call_target="tpu_custom_call" | custom-call | tf_op jit(solution)/shard_map/attention_forward/pallas_call | solution.py:1114
  319.2 4.9 multiply_reduce_fusion.14
  330.1 40.5 %ffn_rows.1 = bf16[8,128,1600]{2,1,0:T(8,128)(2,1)} custom-call(bf16[128,1600]{1,0:T(8,128)(2,1)} %multiply_convert_fusion.8.refs_0_), custom_call_target="tpu_custom_call" | custom-call | tf_op jit(solution)/shard_map/ffn_rows/pallas_call | solution.py:159
  370.6 5.9 fusion.14
  379.7 5.3 multiply_convert_fusion
  386.9 64.4 %ffn_sums.1 = (bf16[8,200,384]{2,1,0:T(8,128)(2,1)}, bf16[768,1600]{1,0:T(8,128)(2,1)}, f32[128,1600]{1,0:T(8,128)}) custom-call(bf16[1024,1600]{1,0:T(8,128)(2,1)} %bitcast.140, bf16[1024,1536]{1,0:T(8,128)(2,1)} %pad_maximum_fusion.refs_1_, bf16[1024,768]{1,0:T(8,128)(2,1)} %get-tuple-element.201.refs_2_.refs_8_, bf16[1024,1600]{1,0:T(8,128)(2,1)} %bitcast.160, ...), custom_call_target="tpu_custom_call" | custom-call | tf_op jit(solution)/shard_map/ffn_sums/pallas_call | solution.py:1114
  457.5 4.9 fusion.18.refs_6_
  462.3 4.4 convolution_convert_fusion.1
  466.7 46.8 %attention_backward.1 = (bf16[1600,128]{1,0:T(8,128)(2,1)}, f32[640,512]{1,0:T(8,128)}, bf16[8,128,1600]{2,1,0:T(8,128)(2,1)}, bf16[8,200,512]{2,1,0:T(8,128)(2,1)}) custom-call(bf16[1600,128]{1,0:T(8,128)(2,1)} %bitcast.159, bf16[5,512,64]{2,1,0:T(8,128)(2,1)} %get-tuple-element.209.refs_1_, bf16[320,512]{1,0:T(8,128)(2,1)} %bitcast.170, ...), custom_call_target="tpu_custom_call" | custom-call | tf_op jit(solution)/shard_map/attention_backward/pallas_call | solution.py:1114
  513.5 8.7 %multiply_reduce_fusion.1 = (bf16[512]{0:T(512)(128)(2,1)S(1)}, f32[1024,512]{1,0:T(8,128)}, bf16[1024,512]{1,0:T(8,128)(2,1)}) fusion(bf16[1024,512]{1,0:T(8,128)(2,1)} %copy-done.5, f32[1024,1024]{1,0:T(8,128)} %copy-done.27, f32[1024,512]{1,0:T(8,128)} %get-tuple-element.76, f32[512]{0:T(512)S(1)} %copy-done.72, bf16[1024,1600]{1,0:T(8,128)(2,1)} %bitcast.193, ...), kind=kOutput, calls=%fused_computation.52 | convolution fusion | flops 1686633984 | bytes 12948480 | tf_op jit(solution)/shard_map/ld,id->li/dot_general | solution.py:2012
  528.7 120.0 %scan_backward.1 = (f32[1024,512]{1,0:T(8,128)}, f32[1024,512]{1,0:T(8,128)}, f32[1024,128]{1,0:T(8,128)}, f32[2,1,16,8,512]{4,3,2,1,0:T(8,128)}, bf16[8,200,153...) custom-call(s32[10]{0:T(128)} %pad_add_fusion.3.refs_0_, ...), custom_call_target="tpu_custom_call" | custom-call | tf_op jit(solution)/shard_map/scan_backward/pallas_call | solution.py:1114
  658.4 18.6 %select_back.1 = (bf16[132,1024]{1,0:T(8,128)(2,1)}, bf16[4,200,512]{2,1,0:T(8,128)(2,1)}, bf16[1,640,128]{2,1,0:T(8,128)(2,1)}) custom-call(bf16[132,1024]{1,0:T(8,128)(2,1)} %maximum_bitcast_fusion.refs_0_, bf16[200,512]{1,0:T(8,128)(2,1)} %convert_element_type.207.refs_1_, bf16[1,640,512]{2,1,0:T(8,128)(2,1)} %convert_bitcast_fusion.refs_2_), custom_call_target="tpu_custom_call" | custom-call | tf_op jit(solution)/shard_map/select_back/pallas_call | solution.py:159
  677.1 4.3 fusion.71
  687.4 14.9 %edges_back.1 = (bf16[4,48,512]{2,1,0:T(8,128)(2,1)}, bf16[8,280,128]{2,1,0:T(8,128)(2,1)}) custom-call(bf16[48,512]{1,0:T(8,128)(2,1)} %reshape.354.refs_0_, bf16[8,280,128]{2,1,0:T(8,128)(2,1)} %pad_maximum_fusion.1.refs_1_), custom_call_target="tpu_custom_call" | custom-call | tf_op jit(solution)/shard_map/edges_back/pallas_call | solution.py:159
  716.2 9.3 %convolution_convert_fusion = bf16[1600,1536]{1,0:T(8,128)(2,1)} fusion(bf16[1024,1600]{1,0:T(8,128)(2,1)S(1)} %copy-done.12, bf16[1024,280]{1,0:T(8,128)(2,1)} %bitcast.162, bf16[1024,512]{1,0:T(8,128)(2,1)} %get-tuple-element.200, bf16[1024,512]{1,0:T(8,128)(2,1)} %bitcast.156, bf16[1536]{0:T(1024)(128)(2,1)S(1)} %pad.101.clone), kind=kOutput, calls=%fused_computation.4 | convolution fusion | flops 5051351040 | bytes 10865664 | tf_op jit(solution)/shard_map/ld,lk->dk/dot_general | solution.py:1762
  730.4 92.8 %finish.1 = (f32[128,1600]{1,0:T(8,128)}, bf16[8,200,1536]{2,1,0:T(8,128)(2,1)}, bf16[4,64,512]{2,1,0:T(8,128)(2,1)}, f32[4,200]{1,0:T(4,128)}) custom-call(bf16[1024,1536]{1,0:T(8,128)(2,1)} %fusion.11.refs_0_, bf16[1600,1536]{1,0:T(8,128)(2,1)} %bitcast.144, bf16[1024,1600]{1,0:T(8,128)(2,1)} %copy-done.11, f32[1,1600]{1,0:T(1,128)} %slice.186.refs_3_, ...), custom_call_target="tpu_custom_call" | custom-call | tf_op jit(solution)/shard_map/finish/pallas_call | solution.py:1114
  827.6 6.0 unpack_columns.2
  841.1 7.2 unpack_columns.3
  (340 shorter events, 120.8 us)
Async XLA Ops:
  91.3 5.3 copy-start.11
  103.4 17.6 %copy-start.80 = (s32[4,2]{0,1:T(2,128)S(1)}, s32[4,2]{0,1:T(2,128)}, u32[]{:S(2)}) copy-start(s32[4,2]{0,1:T(2,128)} %param.25) | copy-start | bytes 100
  157.7 5.0 copy-start.84
  157.8 5.0 copy-start.38
  157.8 5.0 copy-start.50
  169.9 93.3 %copy-start.85 = (bf16[400]{0:T(512)(128)(2,1)S(1)}, bf16[400]{0:T(512)(128)(2,1)}, u32[]{:S(2)}) copy-start(bf16[400]{0:T(512)(128)(2,1)} %param.34) | copy-start | bytes 2404
  319.2 5.3 copy-start.52
  319.2 5.3 copy-start.15
  324.4 5.6 copy-start.9
  329.1 41.5 %copy-start.76 = (f32[128]{0:T(128)}, f32[128]{0:T(128)S(1)}, u32[]{:S(2)}) copy-start(f32[128]{0:T(128)S(1)} %add_rsqrt_fusion.1) | copy-start | bytes 1540
  370.6 5.9 copy-start.24
  370.6 5.9 copy-start.28
  370.6 9.0 %slice-start = ((s8[4915200]{0:T(1024)(128)(4,1)}), s8[4194304]{0:T(1024)(128)(4,1)S(1)}, s32[]{:S(2)}) async-start(s8[4915200]{0:T(1024)(128)(4,1)} %bitcast.149), calls=%async_computation | async-start | bytes 8388608
  466.7 46.8 %copy-start.72 = (f32[512]{0:T(512)S(1)}, f32[512]{0:T(512)}, u32[]{:S(2)}) copy-start(f32[512]{0:T(512)} %copy-done.71) | copy-start | bytes 6148
  513.5 8.7 %copy-start.29 = (bf16[688,1600]{1,0:T(8,128)(2,1)S(1)}, bf16[688,1600]{1,0:T(8,128)(2,1)}, u32[]{:S(2)}) copy-start(bf16[688,1600]{1,0:T(8,128)(2,1)} %param.41) | copy-start | bytes 6604804
  656.0 21.0 %copy-start.19 = (f32[8,2,64,512]{3,2,1,0:T(8,128)S(1)}, f32[8,2,64,512]{3,2,1,0:T(8,128)}, u32[]{:S(2)}) copy-start(f32[8,2,64,512]{3,2,1,0:T(8,128)} %copy-done.18) | copy-start | bytes 6291460
  656.0 21.0 %copy-start.49 = (bf16[400,132]{0,1:T(8,128)(2,1)S(1)}, bf16[400,132]{0,1:T(8,128)(2,1)}, u32[]{:S(2)}) copy-start(bf16[400,132]{0,1:T(8,128)(2,1)} %param.36) | copy-start | bytes 316804
  685.8 19.9 %copy-start.87 = (s32[2]{0:T(128)S(1)}, s32[2]{0:T(128)}, u32[]{:S(2)}) copy-start(s32[2]{0:T(128)} %get-tuple-element.188) | copy-start | bytes 28
  686.5 20.4 %copy-start.82 = (pred[2]{0:T(512)(128)(4,1)S(1)}, pred[2]{0:T(512)(128)(4,1)}, u32[]{:S(2)}) copy-start(pred[2]{0:T(512)(128)(4,1)} %get-tuple-element.219) | copy-start | bytes 10
  716.2 10.7 %copy-start.56 = (bf16[16,400]{1,0:T(8,128)(2,1)S(1)}, bf16[16,400]{1,0:T(8,128)(2,1)}, u32[]{:S(2)}) copy-start(bf16[16,400]{1,0:T(8,128)(2,1)} %param.35) | copy-start | bytes 38404
  730.4 92.8 %copy-start.86 = (f32[128]{0:T(128)S(1)}, f32[128]{0:T(128)}, u32[]{:S(2)}) copy-start(f32[128]{0:T(128)} %get-tuple-element.214) | copy-start | bytes 1540
  730.4 92.8 %copy-start.16 = (bf16[1,128,1600]{2,1,0:T(8,128)(2,1)S(1)}, bf16[1,128,1600]{2,1,0:T(8,128)(2,1)}, u32[]{:S(2)}) copy-start(bf16[1,128,1600]{2,1,0:T(8,128)(2,1)} %copy.103) | copy-start | bytes 1228804
  827.6 6.0 copy-start.39
  841.1 7.2 copy-start.30
  (68 other events, 185.5 us)

commit v5 on v4

--- a/solution.py
+++ b/solution.py
@@ -1708,14 +1708,14 @@
 
 PLAN_START = {1: (0, 1), 2: (0, 2), "end": (0, 2)}
 PLAN_FORWARD = {
-    1: (2,),
+    1: (3, 2),
     (1, 2): (2,),
-    (1, 4): (2,),
+    (1, 4): (2, 3),
     (1, 6): (2,),
     3: (1,),
     (4, 0): (2, 0),
     (4, 1): (1,),
-    (4, 3): (1, 0),
+    (4, 3): (1, 0, 3),
     (4, 4): (1, 2),
     (4, 5): (0,),
     (4, 6): (1,),
@@ -1731,12 +1731,13 @@
     "end": (0, 1, 1, 1, 0),
 }
 PLAN_FINISH = {
-    0: (1,),
-    (1, 1): (1,),
+    0: (1, 2),
+    (1, 1): (1, 2),
+    (1, 3): (1,),
     2: (0, 1),
     (2, 1): (1,),
-    3: (1, 1, 2, 0),
-    "end": (3, 1, 0, 2, 3, 1, 0, 1, 3, 1, 2, 0),
+    3: (1, 0),
+    "end": (3, 1, 1, 0, 2, 1, 3, 1, 0, 1, 1, 3, 2, 0),
 }
 PLAN_BACKWARD = {
     3: (4, 3),
@@ -1898,18 +1899,13 @@
     selected_part = jnp.einsum(
         "ik,li->kl", select_mat, signal, preferred_element_type=f32
     ).astype(bf16)
-    (selected,), (keyvals_all,) = together(
-        [sum_job(selected_part, size), ctx_gather_job(keyval_t)], size, 3, "select"
-    )
-    keyvals_t = keyvals_all.transpose(1, 0, 2).reshape(2 * KV * HD, n_ctx * rows)
-    keyvals = keyvals_t.reshape(2 * KV, HD, n_ctx * rows).transpose(0, 2, 1)
-    key_groups, value_groups = keyvals[:KV], keyvals[KV:]
+    ((selected,),) = together([sum_job(selected_part, size)], size, 3, "select")
     step_low = selected[:RANK].T
     write_read = jnp.pad(selected[RANK:], ((0, 128 - 2 * NS), (0, 0))).T.astype(f32)
     step_pre = jnp.dot(step_low, step_mat, preferred_element_type=f32) + step_shift
     step_sizes = jax.nn.softplus(step_pre)
     order = jnp.concatenate([inverse, my_blocks]).astype(jnp.int32)
-    (scan_rows, start_state, ends_all), ((grads_all,), (ffn_mat,), (attn_mat,)) = scan_forward(
+    (scan_rows, start_state, ends_all), ((grads_all,), (ffn_mat,), (attn_mat,), (keyvals_all,)) = scan_forward(
         order,
         step_sizes,
         signal_float,
@@ -1920,11 +1916,15 @@
             gather_job(out_grad[0], size),
             move_job(ffn_packed, size),
             gather_job(attn_packed, size, True),
+            ctx_gather_job(keyval_t),
         ],
         size,
         4,
         PLAN_FORWARD,
     )
+    keyvals_t = keyvals_all.transpose(1, 0, 2).reshape(2 * KV * HD, n_ctx * rows)
+    keyvals = keyvals_t.reshape(2 * KV, HD, n_ctx * rows).transpose(0, 2, 1)
+    key_groups, value_groups = keyvals[:KV], keyvals[KV:]
     grads_all = grads_all.reshape(rows_all, width)
     ffn_mat = ffn_mat.reshape(width, ffn_total)
     gate_mat, up_mat = ffn_mat[:, :ff_up], ffn_mat[:, ff_up : 2 * ff_up]

time: 868 us -> 858 us (0.988)
    unnamed x195 -> x196, local copies, waits for them, and re-layouts: 23.1 us -> 23.3 us
where the time goes in v5:
time: 858 us; the launch traced here: 848 us
  Pallas kernels  666 us (78%)
  matrix products  68.4 us (8%)
  local copies, waits for them, and re-layouts  56.2 us (7%)
  other arithmetic  55.5 us (6%)
    pallas_call x7, Pallas kernels, hosted(): pl.pallas_call(kernel, out_shape=[shape for shape, _ in outs] + [shape fo...  543 us
    pallas_call x5, Pallas kernels, together(): pl.pallas_call(kernel, out_shape=[shape for job in jobs for shape, _ in j...  110 us
    unnamed x196, local copies, waits for them, and re-layouts  23.3 us

profile of v5, /device:TPU:0, one launch (start us, length us, event | category | flops | bytes accessed | tf_op | source)
XLA Modules:
  0.0 848.5 jit_solution(17930900105425143399)
XLA Ops:
  2.6 83.3 %start.1 = (bf16[8,200,1536]{2,1,0:T(8,128)(2,1)}, bf16[8,128,1600]{2,1,0:T(8,128)(2,1)}, bf16[8,4,200]{2,1,0:T(4,128)(2,1)}, bf16[8,200,1536]{2,1,0:T(8,128)(2,1)}) custom-call(bf16[200,1600]{1,0:T(8,128)(2,1)} %refs_0_.1, bf16[200,640]{1,0:T(8,128)(2,1)} %refs_1_.1, bf16[200,6400]{1,0:T(8,128)(2,1)} %refs_2_.1, bf16[200,5504]{1,0:T(8,128)(2,1)} %refs_3_.1, ...), custom_call_target="tpu_custom_call" | custom-call | tf_op jit(solution)/shard_map/start/pallas_call | solution.py:1114
  103.4 14.9 %edges.1 = (bf16[8,280,128]{2,1,0:T(8,128)(2,1)}, bf16[4,48,512]{2,1,0:T(8,128)(2,1)}) custom-call(bf16[384,1024]{1,0:T(8,128)(2,1)} %convolution_convert_fusion.3.refs_0_, bf16[48,512]{1,0:T(8,128)(2,1)} %reshape.340.refs_1_), custom_call_target="tpu_custom_call" | custom-call | tf_op jit(solution)/shard_map/edges/pallas_call | solution.py:159
  132.7 21.3 %select.31 = bf16[132,1024]{1,0:T(8,128)(2,1)} custom-call(bf16[132,1024]{1,0:T(8,128)(2,1)} %convolution_convert_fusion.4.refs_0_), custom_call_target="tpu_custom_call" | custom-call | tf_op jit(solution)/shard_map/select/pallas_call | solution.py:159
  154.1 4.3 compare_select_fusion
  164.6 93.3 %scan_forward.1 = (f32[1024,512]{1,0:T(8,128)}, f32[2,1,16,8,512]{4,3,2,1,0:T(8,128)}, bf16[8,1,17,8,512]{4,3,2,1,0:T(8,128)(2,1)}, bf16[8,128,1600]{2,1,0:T(8,1...) custom-call(s32[10]{0:T(128)} %pad_add_fusion.3.refs_0_, ...), custom_call_target="tpu_custom_call" | custom-call | tf_op jit(solution)/shard_map/scan_forward/pallas_call | solution.py:1114
  266.8 4.0 multiply_convert_fusion.5.refs_4_
  272.1 48.3 %attention_forward.1 = (bf16[1600,128]{1,0:T(8,128)(2,1)}, f32[25,128]{1,0:T(8,128)}, f32[128,1600]{1,0:T(8,128)}) custom-call(bf16[1600,128]{1,0:T(8,128)(2,1)} %bitcast.158, bf16[5,512,64]{2,1,0:T(8,128)(2,1)} %get-tuple-element.207.refs_1_, bf16[320,512]{1,0:T(8,128)(2,1)} %bitcast.171, f32[512,128]{1,0:T(8,128)} %and_select_fusion.refs_3_.refs_4_, ...), custom_call_target="tpu_custom_call" | custom-call | tf_op jit(solution)/shard_map/attention_forward/pallas_call | solution.py:1114
  322.4 4.9 multiply_reduce_fusion.14
  333.2 40.2 %ffn_rows.1 = bf16[8,128,1600]{2,1,0:T(8,128)(2,1)} custom-call(bf16[128,1600]{1,0:T(8,128)(2,1)} %multiply_convert_fusion.8.refs_0_), custom_call_target="tpu_custom_call" | custom-call | tf_op jit(solution)/shard_map/ffn_rows/pallas_call | solution.py:159
  373.5 5.9 fusion.14
  382.5 5.3 multiply_convert_fusion
  389.7 64.6 %ffn_sums.1 = (bf16[8,200,384]{2,1,0:T(8,128)(2,1)}, bf16[768,1600]{1,0:T(8,128)(2,1)}, f32[128,1600]{1,0:T(8,128)}) custom-call(bf16[1024,1600]{1,0:T(8,128)(2,1)} %bitcast.140, bf16[1024,1536]{1,0:T(8,128)(2,1)} %pad_maximum_fusion.refs_1_, bf16[1024,768]{1,0:T(8,128)(2,1)} %get-tuple-element.199.refs_2_.refs_8_, bf16[1024,1600]{1,0:T(8,128)(2,1)} %bitcast.160, ...), custom_call_target="tpu_custom_call" | custom-call | tf_op jit(solution)/shard_map/ffn_sums/pallas_call | solution.py:1114
  460.5 4.9 fusion.18.refs_6_
  465.4 4.3 convolution_convert_fusion.1
  469.7 46.9 %attention_backward.1 = (bf16[1600,128]{1,0:T(8,128)(2,1)}, f32[640,512]{1,0:T(8,128)}, bf16[8,128,1600]{2,1,0:T(8,128)(2,1)}, bf16[8,200,512]{2,1,0:T(8,128)(2,1)}) custom-call(bf16[1600,128]{1,0:T(8,128)(2,1)} %bitcast.159, bf16[5,512,64]{2,1,0:T(8,128)(2,1)} %get-tuple-element.207.refs_1_, bf16[320,512]{1,0:T(8,128)(2,1)} %bitcast.170, ...), custom_call_target="tpu_custom_call" | custom-call | tf_op jit(solution)/shard_map/attention_backward/pallas_call | solution.py:1114
  516.7 8.7 %multiply_reduce_fusion.1 = (bf16[512]{0:T(512)(128)(2,1)S(1)}, f32[1024,512]{1,0:T(8,128)}, bf16[1024,512]{1,0:T(8,128)(2,1)}) fusion(bf16[1024,512]{1,0:T(8,128)(2,1)} %copy-done.5, f32[1024,1024]{1,0:T(8,128)} %copy-done.28, f32[1024,512]{1,0:T(8,128)} %get-tuple-element.74, f32[512]{0:T(512)S(1)} %copy-done.72, bf16[1024,1600]{1,0:T(8,128)(2,1)} %bitcast.193, ...), kind=kOutput, calls=%fused_computation.52 | convolution fusion | flops 1686633984 | bytes 12948480 | tf_op jit(solution)/shard_map/ld,id->li/dot_general | solution.py:2012
  531.9 119.9 %scan_backward.1 = (f32[1024,512]{1,0:T(8,128)}, f32[1024,512]{1,0:T(8,128)}, f32[1024,128]{1,0:T(8,128)}, f32[2,1,16,8,512]{4,3,2,1,0:T(8,128)}, bf16[8,200,153...) custom-call(s32[10]{0:T(128)} %pad_add_fusion.3.refs_0_, ...), custom_call_target="tpu_custom_call" | custom-call | tf_op jit(solution)/shard_map/scan_backward/pallas_call | solution.py:1114
  661.5 18.8 %select_back.1 = (bf16[132,1024]{1,0:T(8,128)(2,1)}, bf16[4,200,512]{2,1,0:T(8,128)(2,1)}, bf16[1,640,128]{2,1,0:T(8,128)(2,1)}) custom-call(bf16[132,1024]{1,0:T(8,128)(2,1)} %maximum_bitcast_fusion.refs_0_, bf16[200,512]{1,0:T(8,128)(2,1)} %convert_element_type.207.refs_1_, bf16[1,640,512]{2,1,0:T(8,128)(2,1)} %convert_bitcast_fusion.refs_2_), custom_call_target="tpu_custom_call" | custom-call | tf_op jit(solution)/shard_map/select_back/pallas_call | solution.py:159
  680.4 4.3 fusion.71
  690.7 14.5 %edges_back.1 = (bf16[4,48,512]{2,1,0:T(8,128)(2,1)}, bf16[8,280,128]{2,1,0:T(8,128)(2,1)}) custom-call(bf16[48,512]{1,0:T(8,128)(2,1)} %reshape.354.refs_0_, bf16[8,280,128]{2,1,0:T(8,128)(2,1)} %pad_maximum_fusion.1.refs_1_), custom_call_target="tpu_custom_call" | custom-call | tf_op jit(solution)/shard_map/edges_back/pallas_call | solution.py:159
  719.0 9.3 %convolution_convert_fusion = bf16[1600,1536]{1,0:T(8,128)(2,1)} fusion(bf16[1024,1600]{1,0:T(8,128)(2,1)S(1)} %copy-done.13, bf16[1024,280]{1,0:T(8,128)(2,1)} %bitcast.162, bf16[1024,512]{1,0:T(8,128)(2,1)} %get-tuple-element.198, bf16[1024,512]{1,0:T(8,128)(2,1)} %bitcast.156, bf16[1536]{0:T(1024)(128)(2,1)S(1)} %pad.101.clone), kind=kOutput, calls=%fused_computation.4 | convolution fusion | flops 5051351040 | bytes 10865664 | tf_op jit(solution)/shard_map/ld,lk->dk/dot_general | solution.py:1763
  733.2 86.6 %finish.1 = (f32[128,1600]{1,0:T(8,128)}, bf16[8,200,1536]{2,1,0:T(8,128)(2,1)}, bf16[4,64,512]{2,1,0:T(8,128)(2,1)}, f32[4,200]{1,0:T(4,128)}) custom-call(bf16[1024,1536]{1,0:T(8,128)(2,1)} %fusion.11.refs_0_, bf16[1600,1536]{1,0:T(8,128)(2,1)} %bitcast.144, bf16[1024,1600]{1,0:T(8,128)(2,1)} %copy-done.12, f32[1,1600]{1,0:T(1,128)} %slice.186.refs_3_, ...), custom_call_target="tpu_custom_call" | custom-call | tf_op jit(solution)/shard_map/finish/pallas_call | solution.py:1114
  824.2 6.0 unpack_columns.2
  837.8 7.2 unpack_columns.3
  (340 shorter events, 124.1 us)
Async XLA Ops:
  102.5 17.6 %copy-start.80 = (s32[4,2]{0,1:T(2,128)S(1)}, s32[4,2]{0,1:T(2,128)}, u32[]{:S(2)}) copy-start(s32[4,2]{0,1:T(2,128)} %param.25) | copy-start | bytes 100
  102.5 20.1 %copy-start.83 = (bf16[400]{0:T(512)(128)(2,1)S(1)}, bf16[400]{0:T(512)(128)(2,1)}, u32[]{:S(2)}) copy-start(bf16[400]{0:T(512)(128)(2,1)} %param.33) | copy-start | bytes 2404
  122.6 31.4 %copy-start.69 = (f32[512]{0:T(512)}, f32[512]{0:T(512)S(1)}, u32[]{:S(2)}) copy-start(f32[512]{0:T(512)S(1)} %pad_convert_fusion.2) | copy-start | bytes 6148
  128.6 25.5 %copy-start.50 = (bf16[100,400]{0,1:T(8,128)(2,1)S(1)}, bf16[100,400]{0,1:T(8,128)(2,1)}, u32[]{:S(2)}) copy-start(bf16[100,400]{0,1:T(8,128)(2,1)} %param.37) | copy-start | bytes 240004
  154.1 6.3 copy-start.55
  154.1 6.9 copy-start.41
  322.4 5.3 copy-start.52
  322.4 5.3 copy-start.16
  327.6 5.6 copy-start.10
  332.3 41.1 %copy-start.76 = (f32[128]{0:T(128)}, f32[128]{0:T(128)S(1)}, u32[]{:S(2)}) copy-start(f32[128]{0:T(128)S(1)} %add_rsqrt_fusion.1) | copy-start | bytes 1540
  373.5 5.9 copy-start.25
  373.5 5.9 copy-start.29
  373.5 9.0 %slice-start = ((s8[4915200]{0:T(1024)(128)(4,1)}), s8[4194304]{0:T(1024)(128)(4,1)S(1)}, s32[]{:S(2)}) async-start(s8[4915200]{0:T(1024)(128)(4,1)} %bitcast.149), calls=%async_computation | async-start | bytes 8388608
  469.7 47.0 %copy-start.72 = (f32[512]{0:T(512)S(1)}, f32[512]{0:T(512)}, u32[]{:S(2)}) copy-start(f32[512]{0:T(512)} %copy-done.71) | copy-start | bytes 6148
  516.7 8.7 %copy-start.30 = (bf16[688,1600]{1,0:T(8,128)(2,1)S(1)}, bf16[688,1600]{1,0:T(8,128)(2,1)}, u32[]{:S(2)}) copy-start(bf16[688,1600]{1,0:T(8,128)(2,1)} %param.41) | copy-start | bytes 6604804
  659.1 21.2 %copy-start.20 = (f32[8,2,64,512]{3,2,1,0:T(8,128)S(1)}, f32[8,2,64,512]{3,2,1,0:T(8,128)}, u32[]{:S(2)}) copy-start(f32[8,2,64,512]{3,2,1,0:T(8,128)} %copy-done.19) | copy-start | bytes 6291460
  659.1 21.2 %copy-start.49 = (bf16[400,132]{0,1:T(8,128)(2,1)S(1)}, bf16[400,132]{0,1:T(8,128)(2,1)}, u32[]{:S(2)}) copy-start(bf16[400,132]{0,1:T(8,128)(2,1)} %param.36) | copy-start | bytes 316804
  689.1 19.4 %copy-start.87 = (s32[2]{0:T(128)S(1)}, s32[2]{0:T(128)}, u32[]{:S(2)}) copy-start(s32[2]{0:T(128)} %get-tuple-element.186) | copy-start | bytes 28
  689.8 20.0 %copy-start.82 = (pred[2]{0:T(512)(128)(4,1)S(1)}, pred[2]{0:T(512)(128)(4,1)}, u32[]{:S(2)}) copy-start(pred[2]{0:T(512)(128)(4,1)} %get-tuple-element.217) | copy-start | bytes 10
  719.0 10.7 %copy-start.56 = (bf16[16,400]{1,0:T(8,128)(2,1)S(1)}, bf16[16,400]{1,0:T(8,128)(2,1)}, u32[]{:S(2)}) copy-start(bf16[16,400]{1,0:T(8,128)(2,1)} %param.35) | copy-start | bytes 38404
  733.2 86.6 %copy-start.86 = (f32[128]{0:T(128)S(1)}, f32[128]{0:T(128)}, u32[]{:S(2)}) copy-start(f32[128]{0:T(128)} %get-tuple-element.212) | copy-start | bytes 1540
  733.2 86.6 %copy-start.17 = (bf16[1,128,1600]{2,1,0:T(8,128)(2,1)S(1)}, bf16[1,128,1600]{2,1,0:T(8,128)(2,1)}, u32[]{:S(2)}) copy-start(bf16[1,128,1600]{2,1,0:T(8,128)(2,1)} %copy.103) | copy-start | bytes 1228804
  824.2 6.0 copy-start.39
  837.8 7.2 copy-start.31
  (68 other events, 193.1 us)
